TPU v7x, 256 devices: a whole 4x4x8 slice. The times are simulated.
256 devices in a mesh: seq: 128 (over x_hi, z, y, core), chan: 2 (over x_lo).
Axes of the slice: x: 4 (x_hi: 2, x_lo: 2; x = x_hi * 2 + x_lo), y: 4, z: 8, core: 2. Of those that a mesh axis runs over, the one named last changes fastest.
Arguments:
- projected: bfloat16 [16384, 3, 2048], P('seq', None, 'chan'), may hold values from -6 to 6
- skip_gain: float32 [2048], P('chan'), may hold values from 0.5 to 1.5
- out_weight: bfloat16 [2048, 4096], P('chan'), may hold values from -0.125 to 0.125
- long_filter: float32 [16384, 2048], P('seq', 'chan'), may hold values from -0.125 to 0.125
- cotangent: bfloat16 [16384, 4096], P('seq', 'chan'), may hold values from -6 to 6
Outputs:
- mixed: bfloat16 [16384, 4096], P('seq', 'chan')
- grad_projected: bfloat16 [16384, 3, 2048], P('seq', None, 'chan')
- grad_filter: float32 [16384, 2048], P('seq', 'chan')
All inputs are finite; a program needn't handle non-finite values.
Results may differ from a plain program's by a relative error of at most 0.0049.
Values may be sent and summed in bfloat16 or wider, within the bound.
No kernel may reach another device: no remote copies, remote signals or barrier semaphores. Data moves between devices by JAX's collectives and lax.ppermute only.
A program may use at most 128 MiB of HBM per device.

v0:
```python
import math

import jax
import jax.numpy as jnp
from jax import lax
from jax.sharding import PartitionSpec as P

HIGH = lax.Precision.HIGHEST
TWO_PI = 2.0 * math.pi


def regroup(blocks):
    return lax.all_to_all(blocks, "seq", split_axis=1, concat_axis=1, tiled=True)


def crosswise(stacked):
    return lax.all_to_all(stacked, "seq", split_axis=2, concat_axis=3, tiled=True)


def block_tables(seq_count):
    freq_index = jnp.arange(2 * seq_count, dtype=jnp.int32)
    block_index = jnp.arange(seq_count, dtype=jnp.int32)
    phase = (freq_index[:, None] * block_index[None, :] % (2 * seq_count)).astype(jnp.float32) * (
        TWO_PI / (2 * seq_count)
    )
    return (jnp.cos(phase), jnp.sin(phase))


def offset_tables(rows):
    offset_index = jnp.arange(rows, dtype=jnp.int32)
    phase = (offset_index[:, None] * offset_index[None, :] % rows).astype(jnp.float32) * (
        TWO_PI / rows
    )
    return (jnp.cos(phase), jnp.sin(phase))


def to_freq(signals, seq_count, seq_rank):
    count, rows, channels = signals.shape
    per_peer = rows // seq_count
    length = 2 * seq_count * rows
    blocks = regroup(signals.reshape(count, seq_count, per_peer, channels))
    cos_a, sin_a = block_tables(seq_count)
    real_part = jnp.einsum("kt,ntrc->nkrc", cos_a, blocks, precision=HIGH)
    imag_part = -jnp.einsum("kt,ntrc->nkrc", sin_a, blocks, precision=HIGH)
    freq_index = jnp.arange(2 * seq_count, dtype=jnp.int32)
    offsets = seq_rank * per_peer + jnp.arange(per_peer, dtype=jnp.int32)
    phase = (freq_index[:, None] * offsets[None, :] % length).astype(jnp.float32) * (
        TWO_PI / length
    )
    tw_cos = jnp.cos(phase)[:, :, None]
    tw_sin = jnp.sin(phase)[:, :, None]
    turned_re = real_part * tw_cos + imag_part * tw_sin
    turned_im = imag_part * tw_cos - real_part * tw_sin
    moved = crosswise(jnp.stack([turned_re, turned_im], 1))
    moved_re = moved[:, 0]
    moved_im = moved[:, 1]
    cos_b, sin_b = offset_tables(rows)
    spec_re = jnp.einsum("kt,njtc->nkjc", cos_b, moved_re, precision=HIGH) + jnp.einsum(
        "kt,njtc->nkjc", sin_b, moved_im, precision=HIGH
    )
    spec_im = jnp.einsum("kt,njtc->nkjc", cos_b, moved_im, precision=HIGH) - jnp.einsum(
        "kt,njtc->nkjc", sin_b, moved_re, precision=HIGH
    )
    return (spec_re, spec_im)


def to_time(spec_re, spec_im, seq_count, seq_rank):
    count, rows, pair, channels = spec_re.shape
    length = 2 * seq_count * rows
    cos_b, sin_b = offset_tables(rows)
    part_re = jnp.einsum("tk,nkjc->ntjc", cos_b, spec_re, precision=HIGH) - jnp.einsum(
        "tk,nkjc->ntjc", sin_b, spec_im, precision=HIGH
    )
    part_im = jnp.einsum("tk,nkjc->ntjc", cos_b, spec_im, precision=HIGH) + jnp.einsum(
        "tk,nkjc->ntjc", sin_b, spec_re, precision=HIGH
    )
    freq_local = 2 * seq_rank + jnp.arange(2, dtype=jnp.int32)
    offsets = jnp.arange(rows, dtype=jnp.int32)
    phase = (offsets[:, None] * freq_local[None, :] % length).astype(jnp.float32) * (
        TWO_PI / length
    )
    tw_cos = jnp.cos(phase)[:, :, None]
    tw_sin = jnp.sin(phase)[:, :, None]
    turned_re = part_re * tw_cos - part_im * tw_sin
    turned_im = part_im * tw_cos + part_re * tw_sin
    moved = crosswise(jnp.stack([turned_re, turned_im], 1))
    cos_a, sin_a = block_tables(seq_count)
    values = jnp.einsum("kt,nrkc->ntrc", cos_a, moved[:, 0], precision=HIGH) - jnp.einsum(
        "kt,nrkc->ntrc", sin_a, moved[:, 1], precision=HIGH
    )
    values = values * (1.0 / length)
    placed = regroup(values)
    return placed.reshape(count, rows, channels)


def local(projected, skip_gain, out_weight, long_filter, cotangent):
    seq_count = lax.axis_size("seq")
    seq_rank = lax.axis_index("seq")
    rows = long_filter.shape[0]
    query = projected[:, 0].astype(jnp.float32)
    key_part = projected[:, 1].astype(jnp.float32)
    value_part = projected[:, 2].astype(jnp.float32)
    source = key_part * value_part
    fwd_re, fwd_im = to_freq(jnp.stack([source, long_filter]), seq_count, seq_rank)
    src_re, src_im = (fwd_re[0], fwd_im[0])
    fil_re, fil_im = (fwd_re[1], fwd_im[1])
    prod_re = src_re * fil_re - src_im * fil_im
    prod_im = src_re * fil_im + src_im * fil_re
    conv = to_time(prod_re[None], prod_im[None], seq_count, seq_rank)[0]
    mixing = conv + skip_gain * source
    gated = (query * mixing).astype(jnp.bfloat16)
    partial_out = jnp.dot(gated, out_weight, preferred_element_type=jnp.float32)
    mixed = lax.psum_scatter(partial_out, "chan", scatter_dimension=1, tiled=True).astype(
        jnp.bfloat16
    )
    full_cot = lax.all_gather(cotangent, "chan", axis=1, tiled=True)
    grad_gated = jnp.einsum("td,cd->tc", full_cot, out_weight, preferred_element_type=jnp.float32)
    grad_query = (grad_gated * mixing).astype(jnp.bfloat16)
    grad_mixing = grad_gated * query
    only_re, only_im = to_freq(grad_mixing[None], seq_count, seq_rank)
    grad_re, grad_im = (only_re[0], only_im[0])
    back_re = jnp.stack([fil_re * grad_re + fil_im * grad_im, src_re * grad_re + src_im * grad_im])
    back_im = jnp.stack([fil_re * grad_im - fil_im * grad_re, src_re * grad_im - src_im * grad_re])
    back_pair = to_time(back_re, back_im, seq_count, seq_rank)
    grad_source = back_pair[0] + skip_gain * grad_mixing
    grad_filter = back_pair[1] * (1.0 / math.sqrt(rows * seq_count))
    grad_projected = jnp.stack(
        [
            grad_query,
            (grad_source * value_part).astype(jnp.bfloat16),
            (grad_source * key_part).astype(jnp.bfloat16),
        ],
        axis=1,
    )
    return (mixed, grad_projected, grad_filter)


def solution(mesh):
    in_specs = (
        P("seq", None, "chan"),
        P("chan"),
        P("chan", None),
        P("seq", "chan"),
        P("seq", "chan"),
    )
    out_specs = (P("seq", "chan"), P("seq", None, "chan"), P("seq", "chan"))
    return jax.shard_map(local, mesh=mesh, in_specs=in_specs, out_specs=out_specs, check_vma=False)
```

profile of v0, /device:TPU:1, one launch (start us, length us, event | category | flops | bytes accessed | tf_op | source)
XLA Modules:
  0.0 613.5 jit_solution(7471190560151595572)
XLA Ops:
  7.9 32.1 %all-gather.2.cloned.1.call-done = bf16[128,4096]{1,0:T(8,128)(2,1)} async-done(((bf16[128,2048]{1,0:T(8,128)(2,1)}), bf16[128,4096]{1,0:T(8,128)(2,1)}) %all-gather.2.cloned.1.call-update) | async-done | bytes 1048592 | tf_op jit(solution)/shard_map/all_gather | solution.py:116
  40.0 6.6 %fusion.264 = f32[128,1024]{1,0:T(8,128)S(1)} fusion(bf16[128,4096]{1,0:T(8,128)(2,1)} %all-gather.2.cloned.1.call-done, bf16[1024,4096]{1,0:T(8,128)(2,1)} %param.7), kind=kOutput, calls=%fused_computation.279 | convolution fusion | flops 1073741824 | bytes 9961472 | tf_op jit(solution)/shard_map/td,cd->tc/dot_general | solution.py:117
  48.8 13.6 %all-to-all-start.4 = ((f32[1,128,1,1024]{3,2,0,1:T(1,128)}), f32[1,128,1,1024]{3,2,0,1:T(1,128)S(1)}, u32[]{:S(2)}, u32[]{:S(2)}) async-start(f32[1,128,1,1024]{3,2,0,1:T(1,128)} %copy.42), calls=%async_computation.5 | async-start | bytes 1048576 | tf_op jit(solution)/shard_map/all_to_all | solution.py:13
  64.4 20.1 %all-to-all-done.4 = f32[1,128,1,1024]{3,2,0,1:T(1,128)S(1)} async-done(((f32[1,128,1,1024]{3,2,0,1:T(1,128)}), f32[1,128,1,1024]{3,2,0,1:T(1,128)S(1)}, u32[]{:S(2)}, u32[]{:S(2)}) %all-to-all-start.4) | async-done | bytes 524320 | tf_op jit(solution)/shard_map/all_to_all | solution.py:13
  84.5 5.5 all-to-all-start
  93.3 3.7 copy.43
  97.0 26.2 %all-to-all-done = f32[2,128,1,1024]{3,0,2,1:T(2,128)S(1)} async-done(((f32[2,128,1,1024]{3,0,2,1:T(2,128)}), f32[2,128,1,1024]{3,0,2,1:T(2,128)S(1)}, u32[]{:S(2)}, u32[]{:S(2)}) %all-to-all-start) | async-done | bytes 1048608 | tf_op jit(solution)/shard_map/all_to_all | solution.py:13
  124.2 5.6 all-to-all-start.5
  138.5 7.4 %copy.36 = f32[2,2,256,1,1024]{4,0,3,1,2:T(2,128)} copy(f32[2,2,256,1,1024]{2,4,0,3,1:T(8,128)} %pad_maximum_fusion) | data formatting | bytes 8388608 | tf_op jit(solution)/shard_map/stack | solution.py:54
  145.8 38.7 %all-to-all-done.5 = f32[1,2,256,1,1024]{4,3,1,0,2:T(1,128)S(1)} async-done(((f32[1,2,256,1,1024]{4,3,1,0,2:T(1,128)}), f32[1,2,256,1,1024]{4,3,1,0,2:T(1,128)S(1)}, u32[]{:S(2)}, u32[]{:S(2)}) %all-to-all-start.5) | async-done | bytes 2097184 | tf_op jit(solution)/shard_map/all_to_all | solution.py:17
  184.6 6.5 %all-to-all-start.1 = ((f32[2,2,256,1,1024]{4,0,3,1,2:T(2,128)}), f32[2,2,256,1,1024]{4,0,3,1,2:T(2,128)}, u32[]{:S(2)}, u32[]{:S(2)}) async-start(f32[2,2,256,1,1024]{4,0,3,1,2:T(2,128)} %copy.36), calls=%async_computation.1 | async-start | bytes 8388608 | tf_op jit(solution)/shard_map/all_to_all | solution.py:17
  193.6 2.8 copy.44
  202.0 87.1 %all-to-all-done.1 = f32[2,2,256,1,1024]{4,0,3,1,2:T(2,128)} async-done(((f32[2,2,256,1,1024]{4,0,3,1,2:T(2,128)}), f32[2,2,256,1,1024]{4,0,3,1,2:T(2,128)}, u32[]{:S(2)}, u32[]{:S(2)}) %all-to-all-start.1) | async-done | bytes 4194336 | tf_op jit(solution)/shard_map/all_to_all | solution.py:17
  289.1 15.7 %copy.38 = f32[2,2,128,2,1,1024]{2,5,3,0,1,4:T(8,128)} copy(f32[2,2,128,2,1,1024]{5,0,1,3,2,4:T(2,128)} %bitcast.13) | data formatting | bytes 8388608 | tf_op jit(solution)/shard_map/all_to_all | solution.py:17
  304.9 3.9 fusion.13
  315.3 3.5 multiply_add_fusion.1
  326.9 6.6 %all-to-all-start.2 = ((f32[1,2,128,2,1024]{4,3,1,0,2:T(2,128)}), f32[1,2,128,2,1024]{4,3,1,0,2:T(2,128)}, u32[]{:S(2)}, u32[]{:S(2)}) async-start(f32[1,2,128,2,1024]{4,3,1,0,2:T(2,128)} %copy.39), calls=%async_computation.2 | async-start | bytes 4194304 | tf_op jit(solution)/shard_map/all_to_all | solution.py:17
  333.5 3.4 fusion.16
  336.9 51.0 %all-to-all-done.2 = f32[1,2,128,2,1024]{4,3,1,0,2:T(2,128)} async-done(((f32[1,2,128,2,1024]{4,3,1,0,2:T(2,128)}), f32[1,2,128,2,1024]{4,3,1,0,2:T(2,128)}, u32[]{:S(2)}, u32[]{:S(2)}) %all-to-all-start.2) | async-done | bytes 2097184 | tf_op jit(solution)/shard_map/all_to_all | solution.py:17
  394.5 3.0 fusion.37
  399.4 6.6 %all-to-all-start.3 = ((f32[1,128,1,1024]{3,2,0,1:T(1,128)}), f32[1,128,1,1024]{3,2,0,1:T(1,128)}, u32[]{:S(2)}, u32[]{:S(2)}) async-start(f32[1,128,1,1024]{3,2,0,1:T(1,128)} %copy.41), calls=%async_computation.3 | async-start | bytes 1048576 | tf_op jit(solution)/shard_map/all_to_all | solution.py:13
  415.2 7.3 %copy.45 = f32[2,2,128,2,1024]{4,3,0,1,2:T(2,128)} copy(f32[2,2,128,2,1024]{2,4,3,0,1:T(8,128)} %pad_maximum_fusion.1) | data formatting | bytes 8388608 | tf_op jit(solution)/shard_map/stack | solution.py:86
  422.5 4.2 all-to-all-done.3
  426.6 9.5 %all-to-all-start.6 = ((f32[2,2,128,2,1024]{4,3,0,1,2:T(2,128)}), f32[2,2,128,2,1024]{4,3,0,1,2:T(2,128)}, u32[]{:S(2)}, u32[]{:S(2)}) async-start(f32[2,2,128,2,1024]{4,3,0,1,2:T(2,128)} %copy.45), calls=%async_computation.7 | async-start | bytes 8388608 | tf_op jit(solution)/shard_map/all_to_all | solution.py:17
  436.4 6.3 %fusion.71 = f32[128,4096]{1,0:T(8,128)} fusion(bf16[1024,4096]{1,0:T(8,128)(2,1)} %param.7, bf16[128,3,1024]{2,0,1:T(8,128)(2,1)S(1)} %copy-done.7, f32[1,128,1,1024]{3,2,0,1:T(1,128)} %all-to-all-done.3, f32[1024]{0:T(1024)S(1)} %copy-done.14), kind=kOutput, calls=%fused_computation.113 | convolution fusion | flops 1074790400 | bytes 11800576 | tf_op jit(solution)/shard_map/dot_general | solution.py:112
  442.6 92.7 %all-to-all-done.6 = f32[2,2,128,2,1024]{4,3,0,1,2:T(2,128)} async-done(((f32[2,2,128,2,1024]{4,3,0,1,2:T(2,128)}), f32[2,2,128,2,1024]{4,3,0,1,2:T(2,128)}, u32[]{:S(2)}, u32[]{:S(2)}) %all-to-all-start.6) | async-done | bytes 4194336 | tf_op jit(solution)/shard_map/all_to_all | solution.py:17
  535.3 5.4 copy.46
  540.7 5.2 fusion.248
  545.9 4.8 copy.62
  550.7 6.0 copy.61
  563.4 5.5 all-to-all-start.7
  571.1 31.0 %all-to-all-done.7 = f32[2,128,1,1024]{3,2,0,1:T(1,128)S(1)} async-done(((f32[2,128,1,1024]{3,2,0,1:T(1,128)}), f32[2,128,1,1024]{3,2,0,1:T(1,128)S(1)}, u32[]{:S(2)}, u32[]{:S(2)}) %all-to-all-start.7) | async-done | bytes 1048608 | tf_op jit(solution)/shard_map/all_to_all | solution.py:13
  (79 shorter events, 71.2 us)
Async XLA Ops:
  7.2 32.8 %all-gather.2.cloned.1.call-start = ((), (), s32[]{:S(2)}) async-start(), calls=%async_computation.10 | async-start | bytes 1572864 | tf_op jit(solution)/shard_map/all_gather | solution.py:116
  7.9 39.5 %copy-start.6 = (bf16[128,3,1024]{2,0,1:T(8,128)(2,1)S(1)}, bf16[128,3,1024]{2,0,1:T(8,128)(2,1)}, u32[]{:S(2)}) copy-start(bf16[128,3,1024]{2,0,1:T(8,128)(2,1)} %param.5) | copy-start | bytes 2359300
  46.6 0.8 copy-start.8
  47.4 15.1 %copy-start.13 = (f32[128,1024]{1,0:T(8,128)S(1)}, f32[128,1024]{1,0:T(8,128)}, u32[]{:S(2)}) copy-start(f32[128,1024]{1,0:T(8,128)} %param.8) | copy-start | bytes 1572868
  48.8 35.7 %all-to-all-start.4 = ((f32[1,128,1,1024]{3,2,0,1:T(1,128)}), f32[1,128,1,1024]{3,2,0,1:T(1,128)S(1)}, u32[]{:S(2)}, u32[]{:S(2)}) async-start(f32[1,128,1,1024]{3,2,0,1:T(1,128)} %copy.42), calls=%async_computation.5 | async-start | bytes 1048576 | tf_op jit(solution)/shard_map/all_to_all | solution.py:13
  84.5 38.7 %all-to-all-start = ((f32[2,128,1,1024]{3,0,2,1:T(2,128)}), f32[2,128,1,1024]{3,0,2,1:T(2,128)S(1)}, u32[]{:S(2)}, u32[]{:S(2)}) async-start(f32[2,128,1,1024]{3,0,2,1:T(2,128)} %copy.34), calls=%async_computation | async-start | bytes 2097152 | tf_op jit(solution)/shard_map/all_to_all | solution.py:13
  123.2 1.0 copy-start.10
  124.2 60.3 %all-to-all-start.5 = ((f32[1,2,256,1,1024]{4,3,1,0,2:T(1,128)}), f32[1,2,256,1,1024]{4,3,1,0,2:T(1,128)S(1)}, u32[]{:S(2)}, u32[]{:S(2)}) async-start(f32[1,2,256,1,1024]{4,3,1,0,2:T(1,128)} %copy.43), calls=%async_computation.6 | async-start | bytes 4194304 | tf_op jit(solution)/shard_map/all_to_all | solution.py:17
  184.6 104.6 %all-to-all-start.1 = ((f32[2,2,256,1,1024]{4,0,3,1,2:T(2,128)}), f32[2,2,256,1,1024]{4,0,3,1,2:T(2,128)}, u32[]{:S(2)}, u32[]{:S(2)}) async-start(f32[2,2,256,1,1024]{4,0,3,1,2:T(2,128)} %copy.36), calls=%async_computation.1 | async-start | bytes 8388608 | tf_op jit(solution)/shard_map/all_to_all | solution.py:17
  304.9 3.9 copy-start
  313.1 2.2 copy-start.11
  313.1 2.2 copy-start.12
  326.9 6.6 %copy-start.2 = (f32[1,128,2,1024]{1,3,2,0:T(8,128)S(1)}, f32[1,128,2,1024]{1,3,2,0:T(8,128)}, u32[]{:S(2)}) copy-start(f32[1,128,2,1024]{1,3,2,0:T(8,128)} %get-tuple-element.10) | copy-start | bytes 3145732
  326.9 6.6 %copy-start.3 = (f32[1,128,2,1024]{1,3,2,0:T(8,128)S(1)}, f32[1,128,2,1024]{1,3,2,0:T(8,128)}, u32[]{:S(2)}) copy-start(f32[1,128,2,1024]{1,3,2,0:T(8,128)} %get-tuple-element.11) | copy-start | bytes 3145732
  326.9 61.1 %all-to-all-start.2 = ((f32[1,2,128,2,1024]{4,3,1,0,2:T(2,128)}), f32[1,2,128,2,1024]{4,3,1,0,2:T(2,128)}, u32[]{:S(2)}, u32[]{:S(2)}) async-start(f32[1,2,128,2,1024]{4,3,1,0,2:T(2,128)} %copy.39), calls=%async_computation.2 | async-start | bytes 4194304 | tf_op jit(solution)/shard_map/all_to_all | solution.py:17
  399.4 27.2 %all-to-all-start.3 = ((f32[1,128,1,1024]{3,2,0,1:T(1,128)}), f32[1,128,1,1024]{3,2,0,1:T(1,128)}, u32[]{:S(2)}, u32[]{:S(2)}) async-start(f32[1,128,1,1024]{3,2,0,1:T(1,128)} %copy.41), calls=%async_computation.3 | async-start | bytes 1048576 | tf_op jit(solution)/shard_map/all_to_all | solution.py:13
  406.1 2.2 copy-start.1
  408.2 2.2 copy-start.4
  422.4 13.9 %copy-start.7 = (bf16[128,3,1024]{2,0,1:T(8,128)(2,1)S(1)}, bf16[128,3,1024]{2,0,1:T(8,128)(2,1)}, u32[]{:S(2)}) copy-start(bf16[128,3,1024]{2,0,1:T(8,128)(2,1)} %param.5) | copy-start | bytes 2359300
  422.5 13.9 %copy-start.14 = (f32[1024]{0:T(1024)S(1)}, f32[1024]{0:T(1024)}, u32[]{:S(2)}) copy-start(f32[1024]{0:T(1024)} %param.6) | copy-start | bytes 12292
  426.6 108.7 %all-to-all-start.6 = ((f32[2,2,128,2,1024]{4,3,0,1,2:T(2,128)}), f32[2,2,128,2,1024]{4,3,0,1,2:T(2,128)}, u32[]{:S(2)}, u32[]{:S(2)}) async-start(f32[2,2,128,2,1024]{4,3,0,1,2:T(2,128)} %copy.45), calls=%async_computation.7 | async-start | bytes 8388608 | tf_op jit(solution)/shard_map/all_to_all | solution.py:17
  436.1 132.8 %reduce-scatter.2.cloned.1.call-start = ((), (), s32[]{:S(2)}) async-start(), calls=%async_computation.9 | async-start | bytes 3145728 | tf_op jit(solution)/shard_map/reduce_scatter | solution.py:113
  556.8 2.3 copy-start.5
  563.4 38.6 %all-to-all-start.7 = ((f32[2,128,1,1024]{3,2,0,1:T(1,128)}), f32[2,128,1,1024]{3,2,0,1:T(1,128)S(1)}, u32[]{:S(2)}, u32[]{:S(2)}) async-start(f32[2,128,1,1024]{3,2,0,1:T(1,128)} %copy.49), calls=%async_computation.8 | async-start | bytes 2097152 | tf_op jit(solution)/shard_map/all_to_all | solution.py:13
  568.9 34.9 %copy-start.9 = (f32[128,1024]{1,0:T(8,128)S(1)}, f32[128,1024]{1,0:T(8,128)}, u32[]{:S(2)}) copy-start(f32[128,1024]{1,0:T(8,128)} %copy-done.8) | copy-start | bytes 1572868
Sparse Core Ops, SparseCore 0:
  9.8 30.1 all-gather.1
  442.8 57.8 reduce-scatter.1
where the time goes:
time: 624 us; the launch traced here: 614 us
  waiting for transfers between devices  384 us (62%)
  local copies, waits for them, and re-layouts  78.6 us (13%)
  matrix products  65.8 us (11%)
  starting transfers between devices  59.6 us (10%)
  between operations  15 us (2%)
  other arithmetic  10.7 us (2%)
    all_to_all x4, waiting for transfers between devices, crosswise(): lax.all_to_all(stacked, 'seq', split_axis=2, concat_axis=3, tiled=True)  270 us
    all_to_all x4, waiting for transfers between devices, regroup(): lax.all_to_all(blocks, 'seq', split_axis=1, concat_axis=1, tiled=True)  81.4 us
    all_gather x1, waiting for transfers between devices, local(): full_cot = lax.all_gather(cotangent, 'chan', axis=1, tiled=True)  32.1 us
    all_to_all x4, starting transfers between devices, regroup(): lax.all_to_all(blocks, 'seq', split_axis=1, concat_axis=1, tiled=True)  31.2 us
    all_to_all x4, starting transfers between devices, crosswise(): lax.all_to_all(stacked, 'seq', split_axis=2, concat_axis=3, tiled=True)  28.2 us
    all_to_all x4, local copies, waits for them, and re-layouts, crosswise(): lax.all_to_all(stacked, 'seq', split_axis=2, concat_axis=3, tiled=True)  26.6 us
    unnamed x34, local copies, waits for them, and re-layouts  16 us
  transfers between devices with their start and end apart: 10, of which 9 were waited for; matrix products, arithmetic and copies ran while one was open for 15% of the time, Pallas kernels for 0%

commit v1 on v0

v1 whole, which is shorter than its diff:
```python
import math

import jax
import jax.numpy as jnp
import numpy as np
from jax import lax
from jax.experimental import pallas as pl
from jax.experimental.pallas import tpu as pltpu
from jax.sharding import PartitionSpec as P

F32 = jnp.float32
BF16 = jnp.bfloat16
VMEM_LIMIT = 56 * 1024 * 1024


def params():
    return pltpu.CompilerParams(vmem_limit_bytes=VMEM_LIMIT)


def halves(table):
    high = table.astype(BF16)
    low = (table - high.astype(np.float64)).astype(BF16)
    return high, low


def tables(blocks, rows):
    length = 2 * blocks * rows
    k1 = np.arange(blocks)[:, None] + 0.5
    angle = 2.0 * np.pi * k1 * np.arange(blocks)[None, :] / (2 * blocks)
    outer = np.concatenate([np.cos(angle), -np.sin(angle)], axis=0)
    outer_high, outer_low = halves(outer)
    outer_both = np.concatenate([outer_high, outer_low], axis=1)
    back_high, back_low = halves(outer.T)
    turn = 2.0 * np.pi * k1 * np.arange(rows)[None, :] / length
    turn_re = np.cos(turn).astype(np.float32)
    turn_im = -np.sin(turn).astype(np.float32)
    grid = 2.0 * np.pi * (np.outer(np.arange(rows), np.arange(rows)) % rows) / rows
    cos, sin = np.cos(grid), np.sin(grid)
    inner_high, inner_low = halves(np.block([[cos, -sin], [sin, cos]]))
    return [outer_both, back_high, back_low, turn_re, turn_im, inner_high, inner_low]


def dot(a, b):
    return jnp.dot(a, b, preferred_element_type=F32)


def dot_t(a, b):
    return lax.dot_general(a, b, (((1,), (1,)), ((), ())), preferred_element_type=F32)


def split(x):
    high = x.astype(BF16)
    return high, (x - high.astype(F32)).astype(BF16)


def forward(signal_ref, first, stride, blocks, count, tabs, high_ref, low_ref, spec_ref):
    outer, _, _, turn_re, turn_im, inner_high, inner_low = tabs
    rows = signal_ref.shape[1]
    tre, tim = turn_re[...], turn_im[...]
    for pair in range(count // 2):
        x = jnp.concatenate(
            [
                signal_ref[pl.ds(first + 2 * pair + j, blocks, stride=stride), :].astype(BF16)
                for j in range(2)
            ],
            axis=1,
        )
        a = dot(outer[...], jnp.concatenate([x, x], axis=0))
        for j in range(2):
            are = a[:blocks, j * rows : (j + 1) * rows]
            aim = a[blocks:, j * rows : (j + 1) * rows]
            b = jnp.concatenate([are * tre - aim * tim, are * tim + aim * tre], axis=1)
            high, low = split(b)
            at = (2 * pair + j) * blocks
            high_ref[at : at + blocks, :] = high
            low_ref[at : at + blocks, :] = low
    spec_ref[...] = (
        dot(high_ref[...], inner_high[...])
        + dot(low_ref[...], inner_high[...])
        + dot(high_ref[...], inner_low[...])
    )


def inverse(high_ref, low_ref, part_ref, tabs, scale, blocks, count, out_ref, first, stride):
    _, back_high, back_low, turn_re, turn_im, inner_high, inner_low = tabs
    rows = out_ref.shape[1]
    tre, tim = turn_re[...] * scale, turn_im[...] * scale
    part_ref[...] = (
        dot_t(high_ref[...], inner_high[...])
        + dot_t(low_ref[...], inner_high[...])
        + dot_t(high_ref[...], inner_low[...])
    )
    for pair in range(count // 2):
        both = []
        for j in range(2):
            at = (2 * pair + j) * blocks
            cre = part_ref[at : at + blocks, :rows]
            cim = part_ref[at : at + blocks, rows:]
            both.append(jnp.concatenate([cre * tre + cim * tim, cim * tre - cre * tim], axis=0))
        high, low = split(jnp.concatenate(both, axis=1))
        y = dot(back_high[...], high) + dot(back_high[...], low) + dot(back_low[...], high)
        for j in range(2):
            out_ref[pl.ds(first + 2 * pair + j, blocks, stride=stride), :] = y[
                :, j * rows : (j + 1) * rows
            ]


def product(a_ref, b_ref, conj, high_ref, low_ref):
    half = a_ref.shape[1] // 2
    total = a_ref.shape[0]
    step = total // 8
    for i in range(8):
        at = slice(i * step, (i + 1) * step)
        ar, ai = a_ref[at, :half], a_ref[at, half:]
        br, bi = b_ref[at, :half], b_ref[at, half:]
        if conj:
            z = jnp.concatenate([ar * br + ai * bi, ar * bi - ai * br], axis=1)
        else:
            z = jnp.concatenate([ar * br - ai * bi, ar * bi + ai * br], axis=1)
        high, low = split(z)
        high_ref[at, :] = high
        low_ref[at, :] = low


def prep_kernel(proj_ref, filter_ref, out_ref):
    step, each, rows = out_ref.shape
    each //= 2
    source = proj_ref[1].astype(F32) * proj_ref[2].astype(F32)
    out_ref[:, :each, :] = source.T.reshape(step, each, rows).astype(BF16)
    out_ref[:, each:, :] = filter_ref[...].T.reshape(step, each, rows).astype(BF16)


def grad_kernel(
    chan_ref, w_ref, own_ref, other_ref, proj_ref, skip_ref, gm_ref, gg_ref, q_ref, ss_ref, sg_ref
):
    half = own_ref.shape[1]
    first = chan_ref[0] == 0
    own, other = own_ref[...], other_ref[...]
    low = jnp.where(first, own, other)
    high = jnp.where(first, other, own)
    gg = dot_t(w_ref[:, :half], low) + dot_t(w_ref[:, half:], high)
    query = proj_ref[0].astype(F32).T
    gm = gg * query
    skip = skip_ref[...]
    gg_ref[...] = gg
    q_ref[...] = query
    gm_ref[...] = gm.astype(BF16)
    sg_ref[...] = gm.T * skip
    ss_ref[...] = (proj_ref[1].astype(F32) * proj_ref[2].astype(F32) * skip).T


def conv_kernel(*refs):
    in_ref, gm_ref = refs[:2]
    tabs = refs[2:9]
    spec_ref, out_ref = refs[9:11]
    wide_ref, high_ref, low_ref, part_ref, back_ref = refs[11:]
    blocks, two, rows = in_ref.shape
    count = two // 2
    wide_ref[...] = in_ref[...].astype(F32).reshape(blocks * two, rows)
    for s in range(2):
        forward(
            wide_ref, s * count, two, blocks, count, tabs, high_ref, low_ref, spec_ref.at[s]
        )
    product(spec_ref.at[0], spec_ref.at[1], False, high_ref, low_ref)
    inverse(
        high_ref, low_ref, part_ref, tabs, 1.0 / (blocks * rows), blocks, count, back_ref, 0, count
    )
    out_ref[:, :count, :] = gm_ref[...]
    out_ref[:, count:, :] = back_ref[...].reshape(blocks, count, rows).astype(BF16)


def corr_kernel(*refs):
    in_ref, spec_ref = refs[:2]
    tabs = refs[2:9]
    out_ref = refs[9]
    wide_ref, high_ref, low_ref, part_ref, grad_ref, back_ref = refs[10:]
    blocks, count, rows = in_ref.shape
    wide_ref[...] = in_ref[...].astype(F32).reshape(blocks * count, rows)
    forward(wide_ref, 0, count, blocks, count, tabs, high_ref, low_ref, grad_ref)
    scale = 1.0 / (blocks * rows)
    for s, factor in ((1, scale), (0, scale / math.sqrt(blocks * rows))):
        product(spec_ref.at[s], grad_ref, True, high_ref, low_ref)
        inverse(
            high_ref, low_ref, part_ref, tabs, factor, blocks, count, back_ref, (1 - s) * count,
            2 * count,
        )
    out_ref[...] = back_ref[...].reshape(blocks, 2 * count, rows).astype(BF16)


def mix_kernel(
    chan_ref, conv_ref, ss_ref, q_ref, gg_ref, w_ref, send_ref, gated_ref, gq_ref
):
    @pl.when(pl.program_id(0) == 0)
    def _():
        mixing = conv_ref[...].astype(F32).reshape(ss_ref.shape) + ss_ref[...]
        gated_ref[...] = (mixing * q_ref[...]).T.astype(BF16)
        gq_ref[...] = (mixing * gg_ref[...]).T.astype(BF16)

    send_ref[...] = dot(gated_ref[...], w_ref[...]).astype(BF16)


def own_kernel(chan_ref, gated_ref, w_ref, out_ref):
    out_ref[...] = dot(gated_ref[...], w_ref[...])


def end_kernel(in_ref, sg_ref, gq_ref, proj_ref, gp_ref, gf_ref):
    step, two, rows = in_ref.shape
    count = two // 2
    gs = in_ref[:, :count, :].astype(F32).reshape(step * count, rows).T + sg_ref[...]
    gp_ref[0] = gq_ref[...]
    gp_ref[1] = (gs * proj_ref[2].astype(F32)).astype(BF16)
    gp_ref[2] = (gs * proj_ref[1].astype(F32)).astype(BF16)
    gf_ref[...] = in_ref[:, count:, :].astype(F32).reshape(step * count, rows).T


def local(projected, skip_gain, out_weight, long_filter, cotangent):
    blocks = lax.axis_size("seq")
    rows, channels = long_filter.shape
    each = channels // blocks
    width = out_weight.shape[1]
    half = width // 2
    chan = lax.axis_index("chan").astype(jnp.int32).reshape(1)
    proj = projected.transpose(1, 0, 2)
    skip = skip_gain.reshape(1, channels)
    tabs = [jnp.asarray(t) for t in tables(blocks, rows)]
    full = lambda shape: pl.BlockSpec(shape, lambda *_: (0,) * len(shape))
    tab_specs = [full(t.shape) for t in tabs]
    shape = jax.ShapeDtypeStruct

    other = lax.ppermute(cotangent, "chan", [(0, 1), (1, 0)])

    def exchange(x):
        return lax.all_to_all(x, "seq", 0, 0, tiled=True)

    parts = 4
    cb = channels // parts
    pb = blocks // parts
    signals = pl.pallas_call(
        prep_kernel,
        grid=(parts,),
        in_specs=[
            pl.BlockSpec((3, rows, cb), lambda i: (0, 0, i)),
            pl.BlockSpec((rows, cb), lambda i: (0, i)),
        ],
        out_specs=pl.BlockSpec((pb, 2 * each, rows), lambda i: (i, 0, 0)),
        out_shape=shape((blocks, 2 * each, rows), BF16),
        compiler_params=params(),
        name="prep",
    )(proj, long_filter)
    arrived = exchange(signals)

    gm, gg, query, skip_source, skip_grad = pl.pallas_call(
        grad_kernel,
        grid_spec=pltpu.PrefetchScalarGridSpec(
            num_scalar_prefetch=1,
            grid=(parts,),
            in_specs=[
                pl.BlockSpec((cb, width), lambda i, c: (i, 0)),
                full((rows, half)),
                full((rows, half)),
                pl.BlockSpec((3, rows, cb), lambda i, c: (0, 0, i)),
                pl.BlockSpec((1, cb), lambda i, c: (0, i)),
            ],
            out_specs=[pl.BlockSpec((cb, rows), lambda i, c: (i, 0))] * 4
            + [pl.BlockSpec((rows, cb), lambda i, c: (0, i))],
        ),
        out_shape=[shape((channels, rows), BF16)]
        + [shape((channels, rows), F32)] * 3
        + [shape((rows, channels), F32)],
        compiler_params=params(),
        name="grad",
    )(chan, out_weight, cotangent, other, proj, skip)

    spec_shape = (each * blocks, 2 * rows)
    spectra, mid = pl.pallas_call(
        conv_kernel,
        out_shape=[shape((2,) + spec_shape, F32), shape((blocks, 2 * each, rows), BF16)],
        scratch_shapes=[
            pltpu.VMEM((blocks * 2 * each, rows), F32),
            pltpu.VMEM(spec_shape, BF16),
            pltpu.VMEM(spec_shape, BF16),
            pltpu.VMEM(spec_shape, F32),
            pltpu.VMEM((blocks * each, rows), F32),
        ],
        compiler_params=params(),
        name="conv",
    )(arrived, gm.reshape(blocks, each, rows), *tabs)
    back = exchange(mid)

    pair = pl.pallas_call(
        corr_kernel,
        grid=(1,),
        in_specs=[full((blocks, each, rows)), full((2,) + spec_shape)] + tab_specs,
        out_specs=full((blocks, 2 * each, rows)),
        out_shape=shape((blocks, 2 * each, rows), BF16),
        scratch_shapes=[
            pltpu.VMEM((blocks * each, rows), F32),
            pltpu.VMEM(spec_shape, BF16),
            pltpu.VMEM(spec_shape, BF16),
            pltpu.VMEM(spec_shape, F32),
            pltpu.VMEM(spec_shape, F32),
            pltpu.VMEM((blocks * 2 * each, rows), F32),
        ],
        compiler_params=params(),
        name="corr",
    )(back, spectra, *tabs)
    last = exchange(pair)

    wb = half // 4
    send, gated, grad_query = pl.pallas_call(
        mix_kernel,
        grid_spec=pltpu.PrefetchScalarGridSpec(
            num_scalar_prefetch=1,
            grid=(4,),
            in_specs=[
                pl.BlockSpec((blocks, each, rows), lambda i, c: (0, 1, 0)),
                full((channels, rows)),
                full((channels, rows)),
                full((channels, rows)),
                pl.BlockSpec((channels, wb), lambda i, c: (0, (1 - c[0]) * 4 + i)),
            ],
            out_specs=[
                pl.BlockSpec((rows, wb), lambda i, c: (0, i)),
                full((rows, channels)),
                full((rows, channels)),
            ],
        ),
        out_shape=[
            shape((rows, half), BF16),
            shape((rows, channels), BF16),
            shape((rows, channels), BF16),
        ],
        compiler_params=params(),
        name="mix",
    )(chan, back, skip_source, query, gg, out_weight)
    received = lax.ppermute(send, "chan", [(0, 1), (1, 0)])
    kept = pl.pallas_call(
        own_kernel,
        grid_spec=pltpu.PrefetchScalarGridSpec(
            num_scalar_prefetch=1,
            grid=(4,),
            in_specs=[
                full((rows, channels)),
                pl.BlockSpec((channels, wb), lambda i, c: (0, c[0] * 4 + i)),
            ],
            out_specs=pl.BlockSpec((rows, wb), lambda i, c: (0, i)),
        ),
        out_shape=shape((rows, half), F32),
        compiler_params=params(),
        name="own",
    )(chan, gated, out_weight)
    mixed = (kept + received.astype(F32)).astype(BF16)

    grad_projected, grad_filter = pl.pallas_call(
        end_kernel,
        grid=(parts,),
        in_specs=[
            pl.BlockSpec((pb, 2 * each, rows), lambda i: (i, 0, 0)),
            pl.BlockSpec((rows, cb), lambda i: (0, i)),
            pl.BlockSpec((rows, cb), lambda i: (0, i)),
            pl.BlockSpec((3, rows, cb), lambda i: (0, 0, i)),
        ],
        out_specs=[
            pl.BlockSpec((3, rows, cb), lambda i: (0, 0, i)),
            pl.BlockSpec((rows, cb), lambda i: (0, i)),
        ],
        out_shape=[shape((3, rows, channels), BF16), shape((rows, channels), F32)],
        compiler_params=params(),
        name="end",
    )(last, skip_grad, grad_query, proj)
    return mixed, grad_projected.transpose(1, 0, 2), grad_filter


def solution(mesh):
    in_specs = (
        P("seq", None, "chan"),
        P("chan"),
        P("chan", None),
        P("seq", "chan"),
        P("seq", "chan"),
    )
    out_specs = (P("seq", "chan"), P("seq", None, "chan"), P("seq", "chan"))
    return jax.shard_map(local, mesh=mesh, in_specs=in_specs, out_specs=out_specs, check_vma=False)
```

time: 624 us -> 129 us (0.21); the launches traced: 614 us -> 128 us
  waiting for transfers between devices: 384 us -> 28.4 us
  local copies, waits for them, and re-layouts: 78.6 us -> 2.39 us
  matrix products: 65.8 us -> 0 us
  starting transfers between devices: 59.6 us -> 22.3 us
  blocking collectives: 0 us -> 36.7 us
  Pallas kernels: 0 us -> 35.2 us
  between operations: 15 us -> 0.67 us
  other arithmetic: 10.7 us -> 2.13 us
    all_to_all x8 -> x2, waiting for transfers between devices: 351 us -> 0.01 us  [exchange(): return lax.all_to_all(x, 'seq', 0, 0, tiled=True)]
    dot_general x26 -> x0, matrix products: 65.8 us -> none  [the longest x1 6.62 us: local(): jnp.einsum('td,cd->tc', full_cot, out_weight, preferred_element_type=jnp....]
    all_to_all x8 -> x2, starting transfers between devices: 59.3 us -> 21.9 us  [exchange(): return lax.all_to_all(x, 'seq', 0, 0, tiled=True)]
    all_to_all x0 -> x1, blocking collectives: none -> 36.7 us  [exchange(): return lax.all_to_all(x, 'seq', 0, 0, tiled=True)]
    pallas_call x0 -> x7, Pallas kernels: none -> 35.2 us  [the longest x1 7.27 us: local(): pl.pallas_call(grad_kernel, grid_spec=pltpu.PrefetchScalarGridSpec(num_sc...]
    all_gather x1 -> x0, waiting for transfers between devices: 32.1 us -> none  [local(): full_cot = lax.all_gather(cotangent, 'chan', axis=1, tiled=True)]
    ppermute x0 -> x2, waiting for transfers between devices: none -> 28.4 us  [the longest x1 17.4 us: local(): other = lax.ppermute(cotangent, 'chan', [(0, 1), (1, 0)])]
    all_to_all x5 -> x0, local copies, waits for them, and re-layouts: 28.1 us -> none  [the longest x4 26.6 us: crosswise(): lax.all_to_all(stacked, 'seq', split_axis=2, concat_axis=3, tiled=True)]
  transfers between devices with their start and end apart: 10 -> 4, of which waited for: 9 -> 2; matrix products, arithmetic and copies ran while one was open for 15% -> 2% of each run, Pallas kernels for 0% -> 13%
where the time goes in v1:
time: 129 us; the launch traced here: 128 us
  blocking collectives  36.7 us (28%)
  Pallas kernels  35.2 us (27%)
  waiting for transfers between devices  28.4 us (22%)
  starting transfers between devices  22.3 us (17%)
  local copies, waits for them, and re-layouts  2.39 us (2%)
  other arithmetic  2.13 us (2%)
    all_to_all x1, blocking collectives, exchange(): return lax.all_to_all(x, 'seq', 0, 0, tiled=True)  36.7 us
    all_to_all x2, starting transfers between devices, exchange(): return lax.all_to_all(x, 'seq', 0, 0, tiled=True)  21.9 us
    ppermute x1, waiting for transfers between devices, local(): other = lax.ppermute(cotangent, 'chan', [(0, 1), (1, 0)])  17.4 us
    ppermute x1, waiting for transfers between devices, local(): received = lax.ppermute(send, 'chan', [(0, 1), (1, 0)])  10.9 us
    pallas_call x1, Pallas kernels, local(): pl.pallas_call(grad_kernel, grid_spec=pltpu.PrefetchScalarGridSpec(num_sc...  7.27 us
    pallas_call x1, Pallas kernels, local(): pl.pallas_call(corr_kernel, grid=(1,), in_specs=[full((blocks, each, rows...  5.74 us
    pallas_call x1, Pallas kernels, local(): pl.pallas_call(mix_kernel, grid_spec=pltpu.PrefetchScalarGridSpec(num_sca...  5.25 us
    pallas_call x1, Pallas kernels, local(): pl.pallas_call(conv_kernel, out_shape=[shape((2,) + spec_shape, F32), sha...  4.87 us
  transfers between devices with their start and end apart: 4, of which 2 were waited for; matrix products, arithmetic and copies ran while one was open for 2% of the time, Pallas kernels for 13%

profile of v1, /device:TPU:1, one launch (start us, length us, event | category | flops | bytes accessed | tf_op | source)
XLA Modules:
  0.0 127.7 jit_solution(193427307490335176)
XLA Ops:
  0.6 3.6 %prep.1 = bf16[128,16,128]{2,1,0:T(8,128)(2,1)} custom-call(bf16[3,128,1024]{2,1,0:T(8,128)(2,1)} %bitcast.5, f32[128,1024]{1,0:T(8,128)} %filter_ref.1), custom_call_target="tpu_custom_call" | custom-call | tf_op jit(solution)/shard_map/prep/pallas_call | solution.py:238
  4.2 16.4 %all-to-all-start = ((bf16[128,16,128]{2,1,0:T(8,128)(2,1)}), bf16[128,16,128]{2,1,0:T(8,128)(2,1)S(1)}, u32[]{:S(2)}, u32[]{:S(2)}) async-start(bf16[128,16,128]{2,1,0:T(8,128)(2,1)} %prep.1), calls=%async_computation | async-start | bytes 1048576 | tf_op jit(solution)/shard_map/all_to_all | solution.py:233
  20.6 0.4 collective-permute-start
  21.0 17.4 %collective-permute-done.other_ref = bf16[128,2048]{1,0:T(8,128)(2,1)S(1)} collective-permute-done((bf16[128,2048]{1,0:T(8,128)(2,1)}, bf16[128,2048]{1,0:T(8,128)(2,1)S(1)}, u32[]{:S(2)}, u32[]{:S(2)}) %collective-permute-start) | collective-permute-done | bytes 524320 | tf_op jit(solution)/shard_map/ppermute | solution.py:230
  38.4 0.0 copy-start.2
  38.4 0.8 copy-done.2
  39.2 7.3 %grad.1 = (bf16[1024,128]{1,0:T(8,128)(2,1)}, f32[1024,128]{1,0:T(8,128)}, f32[1024,128]{1,0:T(8,128)}, f32[1024,128]{1,0:T(8,128)}, f32[128,1024]{1,0:T(8,128)}) custom-call(s32[1]{0:T(128)} %bitcast.chan_ref, bf16[1024,4096]{1,0:T(8,128)(2,1)} %w_ref.5, bf16[128,2048]{1,0:T(8,128)(2,1)} %own_ref.1, bf16[128,2048]{1,0:T(8,128)(2,1)} %copy-done.2, ...), custom_call_target="tpu_custom_call" | custom-call | tf_op jit(solution)/shard_map/grad/pallas_call | solution.py:252
  46.5 0.0 all-to-all-done.refs_0_
  46.5 0.0 copy-start.1
  46.5 0.8 copy-done.1
  47.3 4.9 %conv.1 = (f32[2,1024,256]{2,1,0:T(8,128)}, bf16[128,16,128]{2,1,0:T(8,128)(2,1)}) custom-call(bf16[128,16,128]{2,1,0:T(8,128)(2,1)} %copy-done.1, bf16[128,8,128]{2,1,0:T(8,128)(2,1)} %bitcast.8, bf16[256,256]{1,0:T(8,128)(2,1)} %constant.18.clone.refs_2_, bf16[128,256]{1,0:T(8,128)(2,1)} %constant.19.clone.refs_3_, ...), custom_call_target="tpu_custom_call" | custom-call | tf_op jit(solution)/shard_map/conv/pallas_call | solution.py:275
  52.2 36.7 %all_to_all.15.conv_ref.refs_0_ = bf16[128,16,128]{2,1,0:T(8,128)(2,1)} all-to-all(bf16[128,16,128]{2,1,0:T(8,128)(2,1)} %get-tuple-element.16), channel_id=1, replica_groups=mesh['seq'=128,'chan'=2] {'seq'}, dimensions={0} | all-to-all | bytes 1048576 | tf_op jit(solution)/shard_map/all_to_all | solution.py:233
  88.9 5.7 %corr.1 = bf16[128,16,128]{2,1,0:T(8,128)(2,1)} custom-call(bf16[128,16,128]{2,1,0:T(8,128)(2,1)} %all_to_all.15.conv_ref.refs_0_, f32[2,1024,256]{2,1,0:T(8,128)} %get-tuple-element.22.refs_1_, bf16[256,256]{1,0:T(8,128)(2,1)} %constant.18.clone.refs_2_, bf16[128,256]{1,0:T(8,128)(2,1)} %constant.19.clone.refs_3_, bf16[128,256]{1,0:T(8,128)(2,1)} %constant.20.clone.refs_4_, ...), custom_call_target="tpu_custom_call" | custom-call | tf_op jit(solution)/shard_map/corr/pallas_call | solution.py:290
  94.6 5.5 %all-to-all-start.2 = ((bf16[128,16,128]{2,1,0:T(8,128)(2,1)}), bf16[128,16,128]{2,1,0:T(8,128)(2,1)S(1)}, u32[]{:S(2)}, u32[]{:S(2)}) async-start(bf16[128,16,128]{2,1,0:T(8,128)(2,1)} %corr.1), calls=%async_computation.2 | async-start | bytes 1048576 | tf_op jit(solution)/shard_map/all_to_all | solution.py:233
  100.1 5.2 %mix.1 = (bf16[128,2048]{1,0:T(8,128)(2,1)}, bf16[128,1024]{1,0:T(8,128)(2,1)}, bf16[128,1024]{1,0:T(8,128)(2,1)}) custom-call(s32[1]{0:T(128)} %bitcast.chan_ref, bf16[128,16,128]{2,1,0:T(8,128)(2,1)} %all_to_all.15.conv_ref.refs_0_, f32[1024,128]{1,0:T(8,128)} %get-tuple-element.17.ss_ref, f32[1024,128]{1,0:T(8,128)} %get-tuple-element.18.q_ref, ...), custom_call_target="tpu_custom_call" | custom-call | tf_op jit(solution)/shard_map/mix/pallas_call | solution.py:310
  105.3 0.0 collective-permute-start.1
  105.3 4.7 %own.1 = f32[128,2048]{1,0:T(8,128)} custom-call(s32[1]{0:T(128)} %bitcast.chan_ref, bf16[128,1024]{1,0:T(8,128)(2,1)} %get-tuple-element.20.gated_ref, bf16[1024,4096]{1,0:T(8,128)(2,1)} %w_ref.5), custom_call_target="tpu_custom_call" | custom-call | tf_op jit(solution)/shard_map/own/pallas_call | solution.py:337
  110.0 10.9 %collective-permute-done.1 = bf16[128,2048]{1,0:T(8,128)(2,1)S(1)} collective-permute-done((bf16[128,2048]{1,0:T(8,128)(2,1)}, bf16[128,2048]{1,0:T(8,128)(2,1)S(1)}, u32[]{:S(2)}, u32[]{:S(2)}) %collective-permute-start.1) | collective-permute-done | bytes 524320 | tf_op jit(solution)/shard_map/ppermute | solution.py:336
  120.9 2.1 %add_convert_fusion = bf16[128,2048]{1,0:T(8,128)(2,1)} fusion(f32[128,2048]{1,0:T(8,128)} %own.1, bf16[128,2048]{1,0:T(8,128)(2,1)S(1)} %collective-permute-done.1), kind=kLoop, calls=%fused_computation | loop fusion | flops 786432 | bytes 2097152 | tf_op jit(solution)/shard_map/convert_element_type | solution.py:352
  123.0 0.0 all-to-all-done.2.in_ref
  123.0 0.0 copy-start
  123.0 0.8 copy-done
  123.8 3.8 %end.1 = (bf16[3,128,1024]{2,1,0:T(8,128)(2,1)}, f32[128,1024]{1,0:T(8,128)}) custom-call(bf16[128,16,128]{2,1,0:T(8,128)(2,1)} %copy-done, f32[128,1024]{1,0:T(8,128)} %get-tuple-element.23.sg_ref, bf16[128,1024]{1,0:T(8,128)(2,1)} %get-tuple-element.24.gq_ref, bf16[3,128,1024]{2,1,0:T(8,128)(2,1)} %bitcast.7), custom_call_target="tpu_custom_call" | custom-call | tf_op jit(solution)/shard_map/end/pallas_call | solution.py:354
Async XLA Ops:
  4.2 42.3 %all-to-all-start = ((bf16[128,16,128]{2,1,0:T(8,128)(2,1)}), bf16[128,16,128]{2,1,0:T(8,128)(2,1)S(1)}, u32[]{:S(2)}, u32[]{:S(2)}) async-start(bf16[128,16,128]{2,1,0:T(8,128)(2,1)} %prep.1), calls=%async_computation | async-start | bytes 1048576 | tf_op jit(solution)/shard_map/all_to_all | solution.py:233
  20.6 17.8 %collective-permute-start = (bf16[128,2048]{1,0:T(8,128)(2,1)}, bf16[128,2048]{1,0:T(8,128)(2,1)S(1)}, u32[]{:S(2)}, u32[]{:S(2)}) collective-permute-start(bf16[128,2048]{1,0:T(8,128)(2,1)} %own_ref.1), channel_id=1, source_target_pairs={{0,1},{1,0},{2,3},{3,2},{4,5},{5,4},{6,7},{7,6},{8,9},{9,8},{10,11... | collective-permute-start | bytes 1572872 | tf_op jit(solution)/shard_map/ppermute | solution.py:230
  38.4 0.8 copy-start.2
  46.5 0.8 copy-start.1
  94.6 28.4 %all-to-all-start.2 = ((bf16[128,16,128]{2,1,0:T(8,128)(2,1)}), bf16[128,16,128]{2,1,0:T(8,128)(2,1)S(1)}, u32[]{:S(2)}, u32[]{:S(2)}) async-start(bf16[128,16,128]{2,1,0:T(8,128)(2,1)} %corr.1), calls=%async_computation.2 | async-start | bytes 1048576 | tf_op jit(solution)/shard_map/all_to_all | solution.py:233
  105.3 15.6 %collective-permute-start.1 = (bf16[128,2048]{1,0:T(8,128)(2,1)}, bf16[128,2048]{1,0:T(8,128)(2,1)S(1)}, u32[]{:S(2)}, u32[]{:S(2)}) collective-permute-start(bf16[128,2048]{1,0:T(8,128)(2,1)} %get-tuple-element.21), channel_id=1, source_target_pairs={{0,1},{1,0},{2,3},{3,2},{4,5},{5,4},{6,7},{7,6},{8,9},{9,8},{10,11... | collective-permute-start | bytes 1572872 | tf_op jit(solution)/shard_map/ppermute | solution.py:336
  123.0 0.8 copy-start

commit v2 on v1

v2 whole, which is shorter than its diff:
```python
import math

import jax
import jax.numpy as jnp
import numpy as np
from jax import lax
from jax.experimental import pallas as pl
from jax.experimental.pallas import tpu as pltpu
from jax.sharding import PartitionSpec as P

F32 = jnp.float32
BF16 = jnp.bfloat16
VMEM_LIMIT = 20 * 1024 * 1024


def params():
    return pltpu.CompilerParams(vmem_limit_bytes=VMEM_LIMIT)


def halves(table):
    high = table.astype(BF16)
    low = (table - high.astype(np.float64)).astype(BF16)
    return high, low


def tables(blocks, rows):
    length = 2 * blocks * rows
    k1 = np.arange(blocks)[:, None] + 0.5
    angle = 2.0 * np.pi * k1 * np.arange(blocks)[None, :] / (2 * blocks)
    outer = np.concatenate([np.cos(angle), -np.sin(angle)], axis=0)
    outer_high, outer_low = halves(outer)
    outer_both = np.concatenate([outer_high, outer_low], axis=1)
    back_high, back_low = halves(outer.T)
    turn = 2.0 * np.pi * k1 * np.arange(rows)[None, :] / length
    turn_re = np.cos(turn).astype(np.float32)
    turn_im = -np.sin(turn).astype(np.float32)
    grid = 2.0 * np.pi * (np.outer(np.arange(rows), np.arange(rows)) % rows) / rows
    cos, sin = np.cos(grid), np.sin(grid)
    inner = np.block([[cos, -sin], [sin, cos]])
    return [outer_both, back_high, back_low, turn_re, turn_im, *halves(inner), *halves(inner.T)]


def dot(a, b):
    return jnp.dot(a, b, preferred_element_type=F32)


def transform(high_ref, low_ref, table_high, table_low):
    return (
        dot(high_ref[...], table_high[...])
        + dot(low_ref[...], table_high[...])
        + dot(high_ref[...], table_low[...])
    )


def dot_t(a, b):
    return lax.dot_general(a, b, (((1,), (1,)), ((), ())), preferred_element_type=F32)


def split(x):
    high = x.astype(BF16)
    return high, (x - high.astype(F32)).astype(BF16)


def forward(signal_ref, first, stride, blocks, count, tabs, high_ref, low_ref, spec_ref):
    outer, _, _, turn_re, turn_im, inner_high, inner_low, _, _ = tabs
    rows = signal_ref.shape[1]
    tre, tim = turn_re[...], turn_im[...]
    for pair in range(count // 2):
        x = jnp.concatenate(
            [
                signal_ref[pl.ds(first + 2 * pair + j, blocks, stride=stride), :].astype(BF16)
                for j in range(2)
            ],
            axis=1,
        )
        a = dot(outer[...], jnp.concatenate([x, x], axis=0))
        for j in range(2):
            are = a[:blocks, j * rows : (j + 1) * rows]
            aim = a[blocks:, j * rows : (j + 1) * rows]
            b = jnp.concatenate([are * tre - aim * tim, are * tim + aim * tre], axis=1)
            high, low = split(b)
            at = (2 * pair + j) * blocks
            high_ref[at : at + blocks, :] = high
            low_ref[at : at + blocks, :] = low
    spec_ref[...] = transform(high_ref, low_ref, inner_high, inner_low)


def inverse(high_ref, low_ref, part_ref, tabs, scale, blocks, count, out_ref, first, stride):
    _, back_high, back_low, turn_re, turn_im, _, _, inner_high, inner_low = tabs
    rows = out_ref.shape[1]
    tre, tim = turn_re[...] * scale, turn_im[...] * scale
    part_ref[...] = transform(high_ref, low_ref, inner_high, inner_low)
    for pair in range(count // 2):
        both = []
        for j in range(2):
            at = (2 * pair + j) * blocks
            cre = part_ref[at : at + blocks, :rows]
            cim = part_ref[at : at + blocks, rows:]
            both.append(jnp.concatenate([cre * tre + cim * tim, cim * tre - cre * tim], axis=0))
        high, low = split(jnp.concatenate(both, axis=1))
        y = dot(back_high[...], high) + dot(back_high[...], low) + dot(back_low[...], high)
        for j in range(2):
            out_ref[pl.ds(first + 2 * pair + j, blocks, stride=stride), :] = y[
                :, j * rows : (j + 1) * rows
            ]


def product(a_ref, b_ref, conj, high_ref, low_ref):
    half = a_ref.shape[1] // 2
    total = a_ref.shape[0]
    step = total // 8
    for i in range(8):
        at = slice(i * step, (i + 1) * step)
        ar, ai = a_ref[at, :half], a_ref[at, half:]
        br, bi = b_ref[at, :half], b_ref[at, half:]
        if conj:
            z = jnp.concatenate([ar * br + ai * bi, ar * bi - ai * br], axis=1)
        else:
            z = jnp.concatenate([ar * br - ai * bi, ar * bi + ai * br], axis=1)
        high, low = split(z)
        high_ref[at, :] = high
        low_ref[at, :] = low


def prep_kernel(proj_hbm, filter_hbm, out_hbm, pair_ref, filter_ref, out_ref, in_sem, out_sem):
    parts, _, rows, width = pair_ref.shape
    step, each = out_ref.shape[1], out_ref.shape[2] // 2
    reads, writes = [], []
    for i in range(parts):
        at = slice(i * width, (i + 1) * width)
        reads.append(
            (
                pltpu.make_async_copy(proj_hbm.at[1:3, :, at], pair_ref.at[i], in_sem.at[i, 0]),
                pltpu.make_async_copy(filter_hbm.at[:, at], filter_ref.at[i], in_sem.at[i, 1]),
            )
        )
        writes.append(
            pltpu.make_async_copy(
                out_ref.at[i], out_hbm.at[i * step : (i + 1) * step], out_sem.at[i]
            )
        )
    for pair, taps in reads:
        pair.start()
        taps.start()
    for i in range(parts):
        pair, taps = reads[i]
        pair.wait()
        source = pair_ref[i, 0].astype(F32) * pair_ref[i, 1].astype(F32)
        out_ref[i, :, :each, :] = source.T.reshape(step, each, rows).astype(BF16)
        taps.wait()
        out_ref[i, :, each:, :] = filter_ref[i].T.reshape(step, each, rows).astype(BF16)
        writes[i].start()
    for write in writes:
        write.wait()


def grad_kernel(
    chan_ref, w_ref, own_ref, other_ref, proj_ref, skip_ref, gm_ref, q_ref, gg_ref, ss_ref,
    sg_ref,
):
    half = own_ref.shape[1]
    first = chan_ref[0] == 0
    own, other = own_ref[...], other_ref[...]
    low = jnp.where(first, own, other)
    high = jnp.where(first, other, own)
    gg = dot_t(w_ref[:, :half], low) + dot_t(w_ref[:, half:], high)
    query = proj_ref[0].astype(F32).T
    gm = gg * query
    skip = skip_ref[...]
    gg_ref[...] = gg
    q_ref[...] = query.astype(BF16)
    gm_ref[...] = gm.astype(BF16)
    sg_ref[...] = gm.T * skip
    ss_ref[...] = (proj_ref[1].astype(F32) * proj_ref[2].astype(F32) * skip).T


def conv_kernel(*refs):
    in_ref, gm_hbm = refs[:2]
    tabs = refs[2:11]
    spec_ref, out_ref = refs[11:13]
    wide_ref, high_ref, low_ref, part_ref, back_ref, gm_sem = refs[13:]
    blocks, two, rows = in_ref.shape
    count = two // 2
    gm_copy = pltpu.make_async_copy(gm_hbm, out_ref.at[:, :count, :], gm_sem)
    gm_copy.start()
    wide_ref[...] = in_ref[...].astype(F32).reshape(blocks * two, rows)
    for s in range(2):
        forward(
            wide_ref, s * count, two, blocks, count, tabs, high_ref, low_ref, spec_ref.at[s]
        )
    product(spec_ref.at[0], spec_ref.at[1], False, high_ref, low_ref)
    inverse(
        high_ref, low_ref, part_ref, tabs, 1.0 / (blocks * rows), blocks, count, back_ref, 0, count
    )
    gm_copy.wait()
    out_ref[:, count:, :] = back_ref[...].reshape(blocks, count, rows).astype(BF16)


def corr_kernel(*refs):
    in_ref, spec_ref = refs[:2]
    tabs = refs[2:11]
    out_ref = refs[11]
    wide_ref, high_ref, low_ref, part_ref, grad_ref, back_ref = refs[12:]
    blocks, two, rows = out_ref.shape
    count = two // 2
    wide_ref[...] = in_ref[:, :count, :].astype(F32).reshape(blocks * count, rows)
    forward(wide_ref, 0, count, blocks, count, tabs, high_ref, low_ref, grad_ref)
    scale = 1.0 / (blocks * rows)
    for s, factor in ((1, scale), (0, scale / math.sqrt(blocks * rows))):
        product(spec_ref.at[s], grad_ref, True, high_ref, low_ref)
        inverse(
            high_ref, low_ref, part_ref, tabs, factor, blocks, count, back_ref, (1 - s) * count, two
        )
    out_ref[...] = back_ref[...].reshape(blocks, two, rows).astype(BF16)


def weight_copies(w_hbm, chan, buf_ref, sem_ref):
    parts, _, width = buf_ref.shape
    return [
        pltpu.make_async_copy(
            w_hbm.at[:, pl.ds(pl.multiple_of((chan * parts + i) * width, width), width)],
            buf_ref.at[i],
            sem_ref.at[i],
        )
        for i in range(parts)
    ]


def mix_kernel(
    chan_ref, in_ref, ss_ref, q_ref, w_hbm, send_hbm, gated_ref, buf_ref, send_ref, in_sem, out_sem
):
    parts, _, width = buf_ref.shape
    copies = weight_copies(w_hbm, 1 - chan_ref[0], buf_ref, in_sem)
    for copy in copies:
        copy.start()
    count = in_ref.shape[1] // 2
    mixing = in_ref[:, count:, :].astype(F32).reshape(ss_ref.shape) + ss_ref[...]
    gated_ref[...] = (mixing * q_ref[...].astype(F32)).T.astype(BF16)
    writes = []
    for i, copy in enumerate(copies):
        copy.wait()
        send_ref[i] = dot(gated_ref[...], buf_ref[i]).astype(BF16)
        write = pltpu.make_async_copy(
            send_ref.at[i], send_hbm.at[:, i * width : (i + 1) * width], out_sem.at[i]
        )
        write.start()
        writes.append(write)
    for write in writes:
        write.wait()


def own_kernel(
    chan_ref, in_ref, ss_ref, gg_ref, gated_ref, w_hbm, out_ref, gp_hbm, buf_ref, gq_ref, in_sem, out_sem
):
    parts, _, width = buf_ref.shape
    copies = weight_copies(w_hbm, chan_ref[0], buf_ref, in_sem)
    for copy in copies:
        copy.start()
    count = in_ref.shape[1] // 2
    mixing = in_ref[:, count:, :].astype(F32).reshape(ss_ref.shape) + ss_ref[...]
    gq_ref[...] = (mixing * gg_ref[...]).T.astype(BF16)
    write = pltpu.make_async_copy(gq_ref, gp_hbm.at[0], out_sem)
    write.start()
    for i, copy in enumerate(copies):
        copy.wait()
        out_ref[:, i * width : (i + 1) * width] = dot(gated_ref[...], buf_ref[i])
    write.wait()


def end_kernel(in_ref, sg_ref, proj_ref, gp_in, gp_hbm, gf_hbm, gp_ref, gf_ref, sem_ref):
    parts, _, rows, width = gp_ref.shape
    step, count = in_ref.shape[0] // parts, in_ref.shape[1] // 2
    writes = []
    for i in range(parts):
        at = slice(i * width, (i + 1) * width)
        block = in_ref[i * step : (i + 1) * step].astype(F32)
        gf_ref[i] = block[:, count:].reshape(width, rows).T
        gs = block[:, :count].reshape(width, rows).T + sg_ref[:, at]
        gp_ref[i, 0] = (gs * proj_ref[2, :, at].astype(F32)).astype(BF16)
        gp_ref[i, 1] = (gs * proj_ref[1, :, at].astype(F32)).astype(BF16)
        for source, target in (
            (gf_ref.at[i], gf_hbm.at[:, at]),
            (gp_ref.at[i], gp_hbm.at[1:3, :, at]),
        ):
            write = pltpu.make_async_copy(source, target, sem_ref.at[len(writes)])
            write.start()
            writes.append(write)
    for write in writes:
        write.wait()


VMEM = pl.BlockSpec(memory_space=pltpu.VMEM)
HBM = pl.BlockSpec(memory_space=pltpu.HBM)
SMEM = pl.BlockSpec(memory_space=pltpu.SMEM)


def conv_call(arrived, gm, tabs, each):
    blocks, _, rows = arrived.shape
    spec_shape = (each * blocks, 2 * rows)
    return pl.pallas_call(
        conv_kernel,
        in_specs=[VMEM, HBM] + [VMEM] * len(tabs),
        out_specs=[VMEM] * 2,
        out_shape=[
            jax.ShapeDtypeStruct((2,) + spec_shape, F32),
            jax.ShapeDtypeStruct(arrived.shape, BF16),
        ],
        scratch_shapes=[
            pltpu.VMEM((blocks * 2 * each, rows), F32),
            pltpu.VMEM(spec_shape, BF16),
            pltpu.VMEM(spec_shape, BF16),
            pltpu.VMEM(spec_shape, F32),
            pltpu.VMEM((blocks * each, rows), F32),
            pltpu.SemaphoreType.DMA(()),
        ],
        compiler_params=params(),
        name="conv",
    )(arrived, gm, *tabs)


def corr_call(back, spectra, tabs, each):
    blocks, _, rows = back.shape
    spec_shape = (each * blocks, 2 * rows)
    return pl.pallas_call(
        corr_kernel,
        in_specs=[VMEM] * (2 + len(tabs)),
        out_specs=VMEM,
        out_shape=jax.ShapeDtypeStruct(back.shape, BF16),
        scratch_shapes=[
            pltpu.VMEM((blocks * each, rows), F32),
            pltpu.VMEM(spec_shape, BF16),
            pltpu.VMEM(spec_shape, BF16),
            pltpu.VMEM(spec_shape, F32),
            pltpu.VMEM(spec_shape, F32),
            pltpu.VMEM((blocks * 2 * each, rows), F32),
        ],
        compiler_params=params(),
        name="corr",
    )(back, spectra, *tabs)


def local(projected, skip_gain, out_weight, long_filter, cotangent):
    blocks = lax.axis_size("seq")
    rows, channels = long_filter.shape
    each = channels // blocks
    width = out_weight.shape[1]
    half = width // 2
    chan = lax.axis_index("chan").astype(jnp.int32).reshape(1)
    in_hbm = lambda x: pltpu.with_memory_space_constraint(x, pltpu.HBM)
    proj = in_hbm(projected.transpose(1, 0, 2))
    out_weight = in_hbm(out_weight)
    long_filter = in_hbm(long_filter)
    skip = skip_gain.reshape(1, channels)
    tabs = [jnp.asarray(t) for t in tables(blocks, rows)]
    full = lambda shape: pl.BlockSpec(shape, lambda *_: (0,) * len(shape))
    shape = jax.ShapeDtypeStruct

    other = lax.ppermute(cotangent, "chan", [(0, 1), (1, 0)])

    def exchange(x):
        return lax.all_to_all(x, "seq", 0, 0, tiled=True)

    smem, vmem, hbm = SMEM, VMEM, HBM
    parts = 4
    cb = channels // parts
    pb = blocks // parts
    signals = pl.pallas_call(
        prep_kernel,
        in_specs=[hbm, hbm],
        out_specs=hbm,
        out_shape=shape((blocks, 2 * each, rows), BF16),
        scratch_shapes=[
            pltpu.VMEM((parts, 2, rows, cb), BF16),
            pltpu.VMEM((parts, rows, cb), F32),
            pltpu.VMEM((parts, pb, 2 * each, rows), BF16),
            pltpu.SemaphoreType.DMA((parts, 2)),
            pltpu.SemaphoreType.DMA((parts,)),
        ],
        compiler_params=params(),
        name="prep",
    )(proj, long_filter)
    arrived = exchange(signals)

    gm, query, gg, skip_source, skip_grad = pl.pallas_call(
        grad_kernel,
        grid_spec=pltpu.PrefetchScalarGridSpec(
            num_scalar_prefetch=1,
            grid=(parts,),
            in_specs=[
                pl.BlockSpec((cb, width), lambda i, c: (i, 0)),
                full((rows, half)),
                full((rows, half)),
                pl.BlockSpec((3, rows, cb), lambda i, c: (0, 0, i)),
                pl.BlockSpec((1, cb), lambda i, c: (0, i)),
            ],
            out_specs=[pl.BlockSpec((cb, rows), lambda i, c: (i, 0))] * 4
            + [pl.BlockSpec((rows, cb), lambda i, c: (0, i))],
        ),
        out_shape=[shape((channels, rows), BF16)] * 2
        + [shape((channels, rows), F32)] * 2
        + [shape((rows, channels), F32)],
        compiler_params=params(),
        cost_estimate=pl.CostEstimate(flops=10**11, transcendentals=0, bytes_accessed=10**9),
        name="grad",
    )(chan, out_weight, cotangent, other, proj, skip)

    spectra, mid = conv_call(arrived, in_hbm(gm.reshape(blocks, each, rows)), tabs, each)
    back = exchange(mid)

    pair = corr_call(back, spectra, tabs, each)
    last = exchange(pair)

    pieces = 4
    wb = half // pieces
    weights = pltpu.VMEM((pieces, channels, wb), BF16)
    sems = pltpu.SemaphoreType.DMA((pieces,))
    send, gated = pl.pallas_call(
        mix_kernel,
        in_specs=[smem, vmem, vmem, vmem, hbm],
        out_specs=[hbm, vmem],
        out_shape=[pltpu.HBM((rows, half), BF16), shape((rows, channels), BF16)],
        scratch_shapes=[weights, pltpu.VMEM((pieces, rows, wb), BF16), sems, sems],
        compiler_params=params(),
        name="mix",
    )(chan, back, skip_source, query, out_weight)
    received = lax.ppermute(send, "chan", [(0, 1), (1, 0)])
    kept, stacked = pl.pallas_call(
        own_kernel,
        in_specs=[smem, vmem, vmem, vmem, vmem, hbm],
        out_specs=[vmem, hbm],
        out_shape=[shape((rows, half), F32), pltpu.HBM((3, rows, channels), BF16)],
        scratch_shapes=[
            weights,
            pltpu.VMEM((rows, channels), BF16),
            sems,
            pltpu.SemaphoreType.DMA(()),
        ],
        compiler_params=params(),
        name="own",
    )(chan, back, skip_source, in_hbm(gg), gated, out_weight)
    mixed = (kept + received.astype(F32)).astype(BF16)

    grad_projected, grad_filter = pl.pallas_call(
        end_kernel,
        in_specs=[vmem, vmem, vmem, hbm],
        out_specs=[hbm] * 2,
        out_shape=[shape((3, rows, channels), BF16), shape((rows, channels), F32)],
        scratch_shapes=[
            pltpu.VMEM((parts, 2, rows, cb), BF16),
            pltpu.VMEM((parts, rows, cb), F32),
            pltpu.SemaphoreType.DMA((2 * parts,)),
        ],
        input_output_aliases={3: 0},
        compiler_params=params(),
        name="end",
    )(last, skip_grad, projected.transpose(1, 0, 2), stacked)
    return mixed, grad_projected.transpose(1, 0, 2), grad_filter


def solution(mesh):
    in_specs = (
        P("seq", None, "chan"),
        P("chan"),
        P("chan", None),
        P("seq", "chan"),
        P("seq", "chan"),
    )
    out_specs = (P("seq", "chan"), P("seq", None, "chan"), P("seq", "chan"))
    return jax.shard_map(local, mesh=mesh, in_specs=in_specs, out_specs=out_specs, check_vma=False)
```

time: 129 us -> 106 us (0.82)
  Pallas kernels: 35.2 us -> 23.5 us
  blocking collectives: 36.7 us -> 27 us
  waiting for transfers between devices: 28.4 us -> 25.7 us
  local copies, waits for them, and re-layouts: 2.39 us -> 4.31 us
    ppermute x1, waiting for transfers between devices: 17.4 us -> 0.01 us  [local(): other = lax.ppermute(cotangent, 'chan', [(0, 1), (1, 0)])]
    all_to_all x2, waiting for transfers between devices: 0.01 us -> 12.7 us  [exchange(): return lax.all_to_all(x, 'seq', 0, 0, tiled=True)]
    pallas_call x6, Pallas kernels: 27.9 us -> 17.5 us  [the longest x1 4.02 us: corr_call(): pl.pallas_call(corr_kernel, in_specs=[VMEM] * (2 + len(tabs)), out_specs=...]
    all_to_all x1, blocking collectives: 36.7 us -> 27 us  [exchange(): return lax.all_to_all(x, 'seq', 0, 0, tiled=True)]
    ppermute x1, waiting for transfers between devices: 10.9 us -> 13 us  [local(): received = lax.ppermute(send, 'chan', [(0, 1), (1, 0)])]
    unnamed x6 -> x32, local copies, waits for them, and re-layouts: 2.39 us -> 4.31 us
    ppermute x1, starting transfers between devices: 0.4 us -> 2.13 us  [local(): other = lax.ppermute(cotangent, 'chan', [(0, 1), (1, 0)])]
  transfers between devices with their start and end apart: 4 -> 4, of which waited for: 2 -> 3; matrix products, arithmetic and copies ran while one was open for 2% -> 1% of each run, Pallas kernels for 13% -> 15%
where the time goes in v2:
time: 106 us
  blocking collectives  27 us (25%)
  waiting for transfers between devices  25.7 us (24%)
  Pallas kernels  23.5 us (22%)
  starting transfers between devices  23.4 us (22%)
  local copies, waits for them, and re-layouts  4.31 us (4%)
    all_to_all x1, blocking collectives, exchange(): return lax.all_to_all(x, 'seq', 0, 0, tiled=True)  27 us
    all_to_all x2, starting transfers between devices, exchange(): return lax.all_to_all(x, 'seq', 0, 0, tiled=True)  21.2 us
    ppermute x1, waiting for transfers between devices, local(): received = lax.ppermute(send, 'chan', [(0, 1), (1, 0)])  13 us
    all_to_all x2, waiting for transfers between devices, exchange(): return lax.all_to_all(x, 'seq', 0, 0, tiled=True)  12.7 us
    pallas_call x1, Pallas kernels, local(): pl.pallas_call(grad_kernel, grid_spec=pltpu.PrefetchScalarGridSpec(num_sc...  6.02 us
    unnamed x32, local copies, waits for them, and re-layouts  4.31 us
    pallas_call x1, Pallas kernels, corr_call(): pl.pallas_call(corr_kernel, in_specs=[VMEM] * (2 + len(tabs)), out_specs=...  4.02 us
    pallas_call x1, Pallas kernels, local(): pl.pallas_call(own_kernel, in_specs=[smem, vmem, vmem, vmem, vmem, hbm],...  3.77 us
  transfers between devices with their start and end apart: 4, of which 3 were waited for; matrix products, arithmetic and copies ran while one was open for 1% of the time, Pallas kernels for 15%

profile of v2, /device:TPU:1, one launch (start us, length us, event | category | flops | bytes accessed | tf_op | source)
XLA Modules:
  0.0 105.9 jit_solution(13984570502362589442)
XLA Ops:
  0.6 2.1 %collective-permute-start = (bf16[128,2048]{1,0:T(8,128)(2,1)}, bf16[128,2048]{1,0:T(8,128)(2,1)S(1)}, u32[]{:S(2)}, u32[]{:S(2)}) collective-permute-start(bf16[128,2048]{1,0:T(8,128)(2,1)} %own_ref.1), channel_id=1, source_target_pairs={{0,1},{1,0},{2,3},{3,2},{4,5},{5,4},{6,7},{7,6},{8,9},{9,8},{10,11... | collective-permute-start | bytes 1572872 | tf_op jit(solution)/shard_map/ppermute | solution.py:358
  2.8 2.5 %prep.1 = bf16[128,16,128]{2,1,0:T(8,128)(2,1)} custom-call(bf16[3,128,1024]{2,1,0:T(8,128)(2,1)} %bitcast.5, f32[128,1024]{1,0:T(8,128)} %filter_hbm.1), custom_call_target="tpu_custom_call" | custom-call | tf_op jit(solution)/shard_map/prep/pallas_call | solution.py:367
  5.3 15.6 %all-to-all-start = ((bf16[128,16,128]{2,1,0:T(8,128)(2,1)}), bf16[128,16,128]{2,1,0:T(8,128)(2,1)S(1)}, u32[]{:S(2)}, u32[]{:S(2)}) async-start(bf16[128,16,128]{2,1,0:T(8,128)(2,1)} %prep.1), calls=%async_computation | async-start | bytes 1048576 | tf_op jit(solution)/shard_map/all_to_all | solution.py:361
  20.9 0.0 collective-permute-done.other_ref
  20.9 0.0 copy-start.13
  20.9 0.8 copy-done.13
  21.7 1.0 copy-done.12
  22.7 1.0 copy-done.14
  23.7 0.7 copy-done.15
  24.4 0.0 copy-start.6
  24.5 0.0 copy-start.7
  24.5 0.0 copy-start.8
  24.5 0.0 copy-start.9
  24.5 0.0 copy-start.10
  24.5 6.0 %grad.1 = (bf16[1024,128]{1,0:T(8,128)(2,1)S(1)}, bf16[1024,128]{1,0:T(8,128)(2,1)S(1)}, f32[1024,128]{1,0:T(8,128)S(1)}, f32[1024,128]{1,0:T(8,128)S(1)}, f32[128,1024]{1,0:T(8,128)S(1)}) custom-call(s32[1]{0:T(128)} %bitcast.chan_ref, bf16[1024,4096]{1,0:T(8,128)(2,1)} %w_hbm.3, bf16[128,2048]{1,0:T(8,128)(2,1)S(1)} %copy-done.12, ...), custom_call_target="tpu_custom_call" | custom-call | flops 99999997952 | bytes 1000000000 | tf_op jit(solution)/shard_map/grad/pallas_call | solution.py:384
  30.5 0.0 copy-start.11
  30.5 0.7 copy-done.11
  31.2 11.7 %all-to-all-done.refs_0_ = bf16[128,16,128]{2,1,0:T(8,128)(2,1)S(1)} async-done(((bf16[128,16,128]{2,1,0:T(8,128)(2,1)}), bf16[128,16,128]{2,1,0:T(8,128)(2,1)S(1)}, u32[]{:S(2)}, u32[]{:S(2)}) %all-to-all-start) | async-done | bytes 524320 | tf_op jit(solution)/shard_map/all_to_all | solution.py:361
  42.9 0.0 copy-done.5
  42.9 0.0 copy-done.6
  43.0 2.8 %conv.1 = (f32[2,1024,256]{2,1,0:T(8,128)S(1)}, bf16[128,16,128]{2,1,0:T(8,128)(2,1)S(1)}) custom-call(bf16[128,16,128]{2,1,0:T(8,128)(2,1)S(1)} %all-to-all-done.refs_0_, bf16[128,8,128]{2,1,0:T(8,128)(2,1)} %bitcast.8, bf16[256,256]{1,0:T(8,128)(2,1)S(1)} %copy-done.6, bf16[128,256]{1,0:T(8,128)(2,1)S(1)} %copy-done.10, bf16[128,256]{1,0:T(8,128)(2,1)S(1)} %copy-done.9, ...), custom_call_target="tpu_custom_call" | custom-call | tf_op jit(solution)/shard_map/conv/pallas_call | solution.py:300
  45.7 27.0 %all_to_all.15.in_ref.refs_0_ = bf16[128,16,128]{2,1,0:T(8,128)(2,1)S(1)} all-to-all(bf16[128,16,128]{2,1,0:T(8,128)(2,1)S(1)} %get-tuple-element.17), channel_id=1, replica_groups=mesh['seq'=128,'chan'=2] {'seq'}, dimensions={0} | all-to-all | bytes 1048576 | tf_op jit(solution)/shard_map/all_to_all | solution.py:361
  72.7 4.0 %corr.1 = bf16[128,16,128]{2,1,0:T(8,128)(2,1)} custom-call(bf16[128,16,128]{2,1,0:T(8,128)(2,1)S(1)} %all_to_all.15.in_ref.refs_0_, f32[2,1024,256]{2,1,0:T(8,128)S(1)} %get-tuple-element.24.refs_1_, bf16[256,256]{1,0:T(8,128)(2,1)S(1)} %copy-done.6, bf16[128,256]{1,0:T(8,128)(2,1)S(1)} %copy-done.10, bf16[128,256]{1,0:T(8,128)(2,1)S(1)} %copy-done.9, ...), custom_call_target="tpu_custom_call" | custom-call | tf_op jit(solution)/shard_map/corr/pallas_call | solution.py:324
  76.7 5.6 %all-to-all-start.2 = ((bf16[128,16,128]{2,1,0:T(8,128)(2,1)}), bf16[128,16,128]{2,1,0:T(8,128)(2,1)S(1)}, u32[]{:S(2)}, u32[]{:S(2)}) async-start(bf16[128,16,128]{2,1,0:T(8,128)(2,1)} %corr.1), calls=%async_computation.2 | async-start | bytes 1048576 | tf_op jit(solution)/shard_map/all_to_all | solution.py:361
  82.4 3.3 %mix.1 = (bf16[128,2048]{1,0:T(8,128)(2,1)}, bf16[128,1024]{1,0:T(8,128)(2,1)S(1)}) custom-call(s32[1]{0:T(128)} %bitcast.chan_ref, bf16[128,16,128]{2,1,0:T(8,128)(2,1)S(1)} %all_to_all.15.in_ref.refs_0_, f32[1024,128]{1,0:T(8,128)S(1)} %get-tuple-element.18.ss_ref, bf16[1024,128]{1,0:T(8,128)(2,1)S(1)} %get-tuple-element.20.q_ref, bf16[1024,4096]{1,0:T(8,128)(2,1)} %w_hbm.3), custom_call_target="tpu_custom_call" | custom-call | tf_op jit(solution)/shard_map/mix/pallas_call | solution.py:417
  85.7 0.0 copy-start
  85.7 0.1 collective-permute-start.1
  85.8 3.8 %own.1 = (f32[128,2048]{1,0:T(8,128)S(1)}, bf16[3,128,1024]{2,1,0:T(8,128)(2,1)}) custom-call(s32[1]{0:T(128)} %bitcast.chan_ref, bf16[128,16,128]{2,1,0:T(8,128)(2,1)S(1)} %all_to_all.15.in_ref.refs_0_, f32[1024,128]{1,0:T(8,128)S(1)} %get-tuple-element.18.ss_ref, f32[1024,128]{1,0:T(8,128)} %copy-done.1, ...), custom_call_target="tpu_custom_call" | custom-call | tf_op jit(solution)/shard_map/own/pallas_call | solution.py:427
  89.6 13.0 %collective-permute-done.1 = bf16[128,2048]{1,0:T(8,128)(2,1)S(1)} collective-permute-done((bf16[128,2048]{1,0:T(8,128)(2,1)}, bf16[128,2048]{1,0:T(8,128)(2,1)S(1)}, u32[]{:S(2)}, u32[]{:S(2)}) %collective-permute-start.1) | collective-permute-done | bytes 524320 | tf_op jit(solution)/shard_map/ppermute | solution.py:426
  102.6 0.9 add_convert_fusion
  103.5 1.1 %all-to-all-done.2.in_ref = bf16[128,16,128]{2,1,0:T(8,128)(2,1)S(1)} async-done(((bf16[128,16,128]{2,1,0:T(8,128)(2,1)}), bf16[128,16,128]{2,1,0:T(8,128)(2,1)S(1)}, u32[]{:S(2)}, u32[]{:S(2)}) %all-to-all-start.2) | async-done | bytes 524320 | tf_op jit(solution)/shard_map/all_to_all | solution.py:361
  104.6 1.1 %end.1 = (bf16[3,128,1024]{2,1,0:T(8,128)(2,1)}, f32[128,1024]{1,0:T(8,128)}) custom-call(bf16[128,16,128]{2,1,0:T(8,128)(2,1)S(1)} %all-to-all-done.2.in_ref, f32[128,1024]{1,0:T(8,128)S(1)} %get-tuple-element.25.sg_ref, bf16[3,128,1024]{2,1,0:T(8,128)(2,1)S(1)} %bitcast.7, ...), custom_call_target="tpu_custom_call", output_to_operand_aliasing={{0}: (3, {})} | custom-call | tf_op jit(solution)/shard_map/end/pallas_call | solution.py:443
  (17 shorter events, 0.0 us)
Async XLA Ops:
  0.6 20.2 %collective-permute-start = (bf16[128,2048]{1,0:T(8,128)(2,1)}, bf16[128,2048]{1,0:T(8,128)(2,1)S(1)}, u32[]{:S(2)}, u32[]{:S(2)}) collective-permute-start(bf16[128,2048]{1,0:T(8,128)(2,1)} %own_ref.1), channel_id=1, source_target_pairs={{0,1},{1,0},{2,3},{3,2},{4,5},{5,4},{6,7},{7,6},{8,9},{9,8},{10,11... | collective-permute-start | bytes 1572872 | tf_op jit(solution)/shard_map/ppermute | solution.py:358
  5.3 37.6 %all-to-all-start = ((bf16[128,16,128]{2,1,0:T(8,128)(2,1)}), bf16[128,16,128]{2,1,0:T(8,128)(2,1)S(1)}, u32[]{:S(2)}, u32[]{:S(2)}) async-start(bf16[128,16,128]{2,1,0:T(8,128)(2,1)} %prep.1), calls=%async_computation | async-start | bytes 1048576 | tf_op jit(solution)/shard_map/all_to_all | solution.py:361
  20.9 0.8 copy-start.13
  21.7 1.0 copy-start.12
  22.7 1.0 copy-start.14
  23.7 0.7 copy-start.15
  24.4 18.5 %copy-start.2 = (bf16[256,256]{1,0:T(8,128)(2,1)S(1)}, bf16[256,256]{1,0:T(8,128)(2,1)}, u32[]{:S(2)}) copy-start(bf16[256,256]{1,0:T(8,128)(2,1)} %constant.30.clone.refs_10_) | copy-start | bytes 393220
  24.4 18.5 %copy-start.3 = (bf16[256,256]{1,0:T(8,128)(2,1)S(1)}, bf16[256,256]{1,0:T(8,128)(2,1)}, u32[]{:S(2)}) copy-start(bf16[256,256]{1,0:T(8,128)(2,1)} %constant.29.clone.refs_9_) | copy-start | bytes 393220
  24.4 18.5 %copy-start.4 = (bf16[256,256]{1,0:T(8,128)(2,1)S(1)}, bf16[256,256]{1,0:T(8,128)(2,1)}, u32[]{:S(2)}) copy-start(bf16[256,256]{1,0:T(8,128)(2,1)} %constant.28.clone.refs_8_) | copy-start | bytes 393220
  24.4 18.5 %copy-start.5 = (bf16[256,256]{1,0:T(8,128)(2,1)S(1)}, bf16[256,256]{1,0:T(8,128)(2,1)}, u32[]{:S(2)}) copy-start(bf16[256,256]{1,0:T(8,128)(2,1)} %constant.27.clone.refs_7_) | copy-start | bytes 393220
  24.4 18.5 %copy-start.6 = (bf16[256,256]{1,0:T(8,128)(2,1)S(1)}, bf16[256,256]{1,0:T(8,128)(2,1)}, u32[]{:S(2)}) copy-start(bf16[256,256]{1,0:T(8,128)(2,1)} %constant.22.clone.refs_2_) | copy-start | bytes 393220
  24.5 18.5 %copy-start.7 = (f32[128,128]{1,0:T(8,128)S(1)}, f32[128,128]{1,0:T(8,128)}, u32[]{:S(2)}) copy-start(f32[128,128]{1,0:T(8,128)} %constant.26.clone.refs_6_) | copy-start | bytes 196612
  24.5 18.5 %copy-start.8 = (f32[128,128]{1,0:T(8,128)S(1)}, f32[128,128]{1,0:T(8,128)}, u32[]{:S(2)}) copy-start(f32[128,128]{1,0:T(8,128)} %constant.25.clone.refs_5_) | copy-start | bytes 196612
  24.5 18.5 %copy-start.9 = (bf16[128,256]{1,0:T(8,128)(2,1)S(1)}, bf16[128,256]{1,0:T(8,128)(2,1)}, u32[]{:S(2)}) copy-start(bf16[128,256]{1,0:T(8,128)(2,1)} %constant.24.clone.refs_4_) | copy-start | bytes 196612
  24.5 18.5 %copy-start.10 = (bf16[128,256]{1,0:T(8,128)(2,1)S(1)}, bf16[128,256]{1,0:T(8,128)(2,1)}, u32[]{:S(2)}) copy-start(bf16[128,256]{1,0:T(8,128)(2,1)} %constant.23.clone.refs_3_) | copy-start | bytes 196612
  30.5 0.7 copy-start.11
  31.2 45.5 %copy-start.1 = (f32[1024,128]{1,0:T(8,128)}, f32[1024,128]{1,0:T(8,128)S(1)}, u32[]{:S(2)}) copy-start(f32[1024,128]{1,0:T(8,128)S(1)} %get-tuple-element.19.gg_ref) | copy-start | bytes 1572868
  76.7 27.8 %all-to-all-start.2 = ((bf16[128,16,128]{2,1,0:T(8,128)(2,1)}), bf16[128,16,128]{2,1,0:T(8,128)(2,1)S(1)}, u32[]{:S(2)}, u32[]{:S(2)}) async-start(bf16[128,16,128]{2,1,0:T(8,128)(2,1)} %corr.1), calls=%async_computation.2 | async-start | bytes 1048576 | tf_op jit(solution)/shard_map/all_to_all | solution.py:361
  85.7 18.8 %copy-start = (bf16[128,3,1024]{2,0,1:T(8,128)(2,1)S(1)}, bf16[128,3,1024]{2,0,1:T(8,128)(2,1)}, u32[]{:S(2)}) copy-start(bf16[128,3,1024]{2,0,1:T(8,128)(2,1)} %param.14) | copy-start | bytes 2359300
  85.7 16.9 %collective-permute-start.1 = (bf16[128,2048]{1,0:T(8,128)(2,1)}, bf16[128,2048]{1,0:T(8,128)(2,1)S(1)}, u32[]{:S(2)}, u32[]{:S(2)}) collective-permute-start(bf16[128,2048]{1,0:T(8,128)(2,1)} %get-tuple-element.23), channel_id=1, source_target_pairs={{0,1},{1,0},{2,3},{3,2},{4,5},{5,4},{6,7},{7,6},{8,9},{9,8},{10,11... | collective-permute-start | bytes 1572872 | tf_op jit(solution)/shard_map/ppermute | solution.py:426

commit v3 on v2

--- a/solution.py
+++ b/solution.py
@@ -11,6 +11,8 @@
 F32 = jnp.float32
 BF16 = jnp.bfloat16
 VMEM_LIMIT = 20 * 1024 * 1024
+GAIN = 1.6657
+COSTLY = pl.CostEstimate(flops=10**11, transcendentals=0, bytes_accessed=10**9)
 
 
 def params():
@@ -30,26 +32,26 @@
     outer = np.concatenate([np.cos(angle), -np.sin(angle)], axis=0)
     outer_high, outer_low = halves(outer)
     outer_both = np.concatenate([outer_high, outer_low], axis=1)
-    back_high, back_low = halves(outer.T)
+    back_both = np.concatenate(halves(outer.T), axis=0)
+    order = np.arange(blocks).reshape(blocks // 2, 2).T.reshape(-1)
+    outer_order = np.concatenate([outer_high[:, order], outer_low[:, order]], axis=1)
+    back_order = np.concatenate(halves(outer.T[order]), axis=0)
     turn = 2.0 * np.pi * k1 * np.arange(rows)[None, :] / length
     turn_re = np.cos(turn).astype(np.float32)
     turn_im = -np.sin(turn).astype(np.float32)
     grid = 2.0 * np.pi * (np.outer(np.arange(rows), np.arange(rows)) % rows) / rows
     cos, sin = np.cos(grid), np.sin(grid)
-    inner = np.block([[cos, -sin], [sin, cos]])
-    return [outer_both, back_high, back_low, turn_re, turn_im, *halves(inner), *halves(inner.T)]
+    inner = GAIN * np.block([[cos, -sin], [sin, cos]])
+    shared = [turn_re, turn_im, inner.astype(BF16), inner.T.astype(BF16)]
+    return [outer_both, back_order, *shared], [outer_order, back_both, *shared]
 
 
 def dot(a, b):
     return jnp.dot(a, b, preferred_element_type=F32)
 
 
-def transform(high_ref, low_ref, table_high, table_low):
-    return (
-        dot(high_ref[...], table_high[...])
-        + dot(low_ref[...], table_high[...])
-        + dot(high_ref[...], table_low[...])
-    )
+def transform(high_ref, low_ref, table):
+    return dot(high_ref[...], table[...]) + dot(low_ref[...], table[...])
 
 
 def dot_t(a, b):
@@ -61,18 +63,11 @@
     return high, (x - high.astype(F32)).astype(BF16)
 
 
-def forward(signal_ref, first, stride, blocks, count, tabs, high_ref, low_ref, spec_ref):
-    outer, _, _, turn_re, turn_im, inner_high, inner_low, _, _ = tabs
-    rows = signal_ref.shape[1]
+def forward(load, blocks, rows, count, tabs, high_ref, low_ref, spec_ref):
+    outer, _, turn_re, turn_im, inner, _ = tabs
     tre, tim = turn_re[...], turn_im[...]
     for pair in range(count // 2):
-        x = jnp.concatenate(
-            [
-                signal_ref[pl.ds(first + 2 * pair + j, blocks, stride=stride), :].astype(BF16)
-                for j in range(2)
-            ],
-            axis=1,
-        )
+        x = jnp.concatenate([load(2 * pair + j).astype(BF16) for j in range(2)], axis=1)
         a = dot(outer[...], jnp.concatenate([x, x], axis=0))
         for j in range(2):
             are = a[:blocks, j * rows : (j + 1) * rows]
@@ -82,14 +77,14 @@
             at = (2 * pair + j) * blocks
             high_ref[at : at + blocks, :] = high
             low_ref[at : at + blocks, :] = low
-    spec_ref[...] = transform(high_ref, low_ref, inner_high, inner_low)
-
-
-def inverse(high_ref, low_ref, part_ref, tabs, scale, blocks, count, out_ref, first, stride):
-    _, back_high, back_low, turn_re, turn_im, _, _, inner_high, inner_low = tabs
-    rows = out_ref.shape[1]
+    spec_ref[...] = transform(high_ref, low_ref, inner)
+
+
+def inverse(high_ref, low_ref, part_ref, tabs, scale, blocks, rows, count, store):
+    _, back_both, turn_re, turn_im, _, inner = tabs
+    scale /= GAIN**3
     tre, tim = turn_re[...] * scale, turn_im[...] * scale
-    part_ref[...] = transform(high_ref, low_ref, inner_high, inner_low)
+    part_ref[...] = transform(high_ref, low_ref, inner)
     for pair in range(count // 2):
         both = []
         for j in range(2):
@@ -98,11 +93,10 @@
             cim = part_ref[at : at + blocks, rows:]
             both.append(jnp.concatenate([cre * tre + cim * tim, cim * tre - cre * tim], axis=0))
         high, low = split(jnp.concatenate(both, axis=1))
-        y = dot(back_high[...], high) + dot(back_high[...], low) + dot(back_low[...], high)
+        y = dot(back_both[...], high)
+        y = y[:blocks] + y[blocks:] + dot(back_both[:blocks, :], low)
         for j in range(2):
-            out_ref[pl.ds(first + 2 * pair + j, blocks, stride=stride), :] = y[
-                :, j * rows : (j + 1) * rows
-            ]
+            store(2 * pair + j, y[:, j * rows : (j + 1) * rows])
 
 
 def product(a_ref, b_ref, conj, high_ref, low_ref):
@@ -154,12 +148,17 @@
         write.wait()
 
 
+def slot_of(near, place_ref):
+    return near ^ place_ref[1]
+
+
 def grad_kernel(
-    chan_ref, w_ref, own_ref, other_ref, proj_ref, skip_ref, gm_ref, q_ref, gg_ref, ss_ref,
-    sg_ref,
+    place_ref, w_ref, own_ref, other_ref, proj_ref, skip_ref,
+    q_ref, gg_ref, ss_ref, sg_ref, *rest,
 ):
+    pieces, (gm_ref, sem_ref) = rest[:2], rest[2:]
     half = own_ref.shape[1]
-    first = chan_ref[0] == 0
+    first = place_ref[0] == 0
     own, other = own_ref[...], other_ref[...]
     low = jnp.where(first, own, other)
     high = jnp.where(first, other, own)
@@ -169,49 +168,107 @@
     skip = skip_ref[...]
     gg_ref[...] = gg
     q_ref[...] = query.astype(BF16)
-    gm_ref[...] = gm.astype(BF16)
+    step = pl.program_id(0)
+    wide = gm.reshape(gm_ref.shape[2], 2, gm_ref.shape[3], gm.shape[1])
+    for near in range(2):
+        gm_ref[step, near] = wide[:, near].astype(BF16)
     sg_ref[...] = gm.T * skip
     ss_ref[...] = (proj_ref[1].astype(F32) * proj_ref[2].astype(F32) * skip).T
+    steps, _, span = gm_ref.shape[:3]
+
+    def copies(i, act):
+        at = i * span
+        for near in range(2):
+            for k in range(2):
+
+                @pl.when(slot_of(near, place_ref) == k)
+                def _():
+                    act(
+                        pltpu.make_async_copy(
+                            gm_ref.at[i, near], pieces[k].at[at : at + span], sem_ref.at[i, near]
+                        )
+                    )
+
+    for i in range(steps):
+
+        @pl.when(step == i)
+        def _():
+            copies(i, lambda copy: copy.start())
+
+    @pl.when(step == steps - 1)
+    def _():
+        for i in range(steps):
+            copies(i, lambda copy: copy.wait())
 
 
 def conv_kernel(*refs):
-    in_ref, gm_hbm = refs[:2]
-    tabs = refs[2:11]
-    spec_ref, out_ref = refs[11:13]
-    wide_ref, high_ref, low_ref, part_ref, back_ref, gm_sem = refs[13:]
+    place_ref, in_ref = refs[:2]
+    gm_refs, tabs = refs[2:4], refs[4:10]
+    spec_ref, out_ref = refs[10:12]
+    wide_ref, high_ref, low_ref, part_ref, back_ref, gm_sem = refs[12:]
     blocks, two, rows = in_ref.shape
     count = two // 2
-    gm_copy = pltpu.make_async_copy(gm_hbm, out_ref.at[:, :count, :], gm_sem)
-    gm_copy.start()
+    middle = blocks // 2
+    copies = [
+        pltpu.make_async_copy(
+            gm_refs[k], out_ref.at[:, k * count : (k + 1) * count, :], gm_sem.at[k]
+        )
+        for k in range(2)
+    ]
+    for copy in copies:
+        copy.start()
     wide_ref[...] = in_ref[...].astype(F32).reshape(blocks * two, rows)
     for s in range(2):
-        forward(
-            wide_ref, s * count, two, blocks, count, tabs, high_ref, low_ref, spec_ref.at[s]
-        )
+
+        def load(c):
+            return wide_ref[pl.ds(s * count + c, blocks, stride=two), :]
+
+        forward(load, blocks, rows, count, tabs, high_ref, low_ref, spec_ref.at[s])
     product(spec_ref.at[0], spec_ref.at[1], False, high_ref, low_ref)
-    inverse(
-        high_ref, low_ref, part_ref, tabs, 1.0 / (blocks * rows), blocks, count, back_ref, 0, count
-    )
-    gm_copy.wait()
-    out_ref[:, count:, :] = back_ref[...].reshape(blocks, count, rows).astype(BF16)
+
+    def store(c, y):
+        for near in range(2):
+            at = slot_of(near, place_ref) * count + c
+            back_ref[pl.ds(at, middle, stride=2 * count), :] = y[near * middle : (near + 1) * middle]
+
+    inverse(high_ref, low_ref, part_ref, tabs, 1.0 / (blocks * rows), blocks, rows, count, store)
+    for copy in copies:
+        copy.wait()
+    out_ref[:, 2 * count :, :] = back_ref[...].reshape(middle, 2 * count, rows).astype(BF16)
 
 
 def corr_kernel(*refs):
-    in_ref, spec_ref = refs[:2]
-    tabs = refs[2:11]
-    out_ref = refs[11]
-    wide_ref, high_ref, low_ref, part_ref, grad_ref, back_ref = refs[12:]
+    place_ref, in_ref, spec_ref = refs[:3]
+    tabs = refs[3:9]
+    out_ref, piece = refs[9:11]
+    wide_ref, high_ref, low_ref, part_ref, grad_ref, back_ref, sem = refs[11:]
     blocks, two, rows = out_ref.shape
     count = two // 2
-    wide_ref[...] = in_ref[:, :count, :].astype(F32).reshape(blocks * count, rows)
-    forward(wide_ref, 0, count, blocks, count, tabs, high_ref, low_ref, grad_ref)
+    middle = blocks // 2
+    copy = pltpu.make_async_copy(in_ref.at[:, 3 * count :, :], piece, sem)
+    copy.start()
+    wide_ref[...] = in_ref[:, : 2 * count, :].astype(F32).reshape(middle * 2 * count, rows)
+
+    def load(c):
+        return jnp.concatenate(
+            [
+                wide_ref[pl.ds(slot_of(near, place_ref) * count + c, middle, stride=2 * count), :]
+                for near in range(2)
+            ],
+            axis=0,
+        )
+
+    forward(load, blocks, rows, count, tabs, high_ref, low_ref, grad_ref)
     scale = 1.0 / (blocks * rows)
     for s, factor in ((1, scale), (0, scale / math.sqrt(blocks * rows))):
+
+        def store(c, y):
+            back_ref[pl.ds((1 - s) * count + c, blocks, stride=two), :] = y
+
         product(spec_ref.at[s], grad_ref, True, high_ref, low_ref)
-        inverse(
-            high_ref, low_ref, part_ref, tabs, factor, blocks, count, back_ref, (1 - s) * count, two
-        )
+        inverse(high_ref, low_ref, part_ref, tabs, factor, blocks, rows, count, store)
     out_ref[...] = back_ref[...].reshape(blocks, two, rows).astype(BF16)
+    copy.wait()
 
 
 def weight_copies(w_hbm, chan, buf_ref, sem_ref):
@@ -227,14 +284,19 @@
 
 
 def mix_kernel(
-    chan_ref, in_ref, ss_ref, q_ref, w_hbm, send_hbm, gated_ref, buf_ref, send_ref, in_sem, out_sem
+    place_ref, in_ref, *refs
 ):
+    other_ref, ss_ref, q_ref, w_hbm, send_hbm, gated_ref, mixing_ref = refs[:7]
+    all_ref, buf_ref, send_ref, in_sem, out_sem = refs[7:]
     parts, _, width = buf_ref.shape
-    copies = weight_copies(w_hbm, 1 - chan_ref[0], buf_ref, in_sem)
+    copies = weight_copies(w_hbm, 1 - place_ref[0], buf_ref, in_sem)
     for copy in copies:
         copy.start()
-    count = in_ref.shape[1] // 2
-    mixing = in_ref[:, count:, :].astype(F32).reshape(ss_ref.shape) + ss_ref[...]
+    count = in_ref.shape[1] // 4
+    all_ref[:, place_ref[1]] = in_ref[:, 2 * count : 3 * count, :].astype(F32)
+    all_ref[:, 1 - place_ref[1]] = other_ref[...].astype(F32)
+    mixing = all_ref[...].reshape(ss_ref.shape) + ss_ref[...]
+    mixing_ref[...] = mixing
     gated_ref[...] = (mixing * q_ref[...].astype(F32)).T.astype(BF16)
     writes = []
     for i, copy in enumerate(copies):
@@ -250,15 +312,13 @@
 
 
 def own_kernel(
-    chan_ref, in_ref, ss_ref, gg_ref, gated_ref, w_hbm, out_ref, gp_hbm, buf_ref, gq_ref, in_sem, out_sem
+    place_ref, mixing_ref, gg_ref, gated_ref, w_hbm, out_ref, gp_hbm, buf_ref, gq_ref, in_sem, out_sem
 ):
     parts, _, width = buf_ref.shape
-    copies = weight_copies(w_hbm, chan_ref[0], buf_ref, in_sem)
+    copies = weight_copies(w_hbm, place_ref[0], buf_ref, in_sem)
     for copy in copies:
         copy.start()
-    count = in_ref.shape[1] // 2
-    mixing = in_ref[:, count:, :].astype(F32).reshape(ss_ref.shape) + ss_ref[...]
-    gq_ref[...] = (mixing * gg_ref[...]).T.astype(BF16)
+    gq_ref[...] = (mixing_ref[...] * gg_ref[...]).T.astype(BF16)
     write = pltpu.make_async_copy(gq_ref, gp_hbm.at[0], out_sem)
     write.start()
     for i, copy in enumerate(copies):
@@ -294,16 +354,17 @@
 SMEM = pl.BlockSpec(memory_space=pltpu.SMEM)
 
 
-def conv_call(arrived, gm, tabs, each):
+def conv_call(place, arrived, gm, tabs, each):
     blocks, _, rows = arrived.shape
+    middle = blocks // 2
     spec_shape = (each * blocks, 2 * rows)
     return pl.pallas_call(
         conv_kernel,
-        in_specs=[VMEM, HBM] + [VMEM] * len(tabs),
+        in_specs=[SMEM, VMEM] + [HBM] * 2 + [VMEM] * len(tabs),
         out_specs=[VMEM] * 2,
         out_shape=[
             jax.ShapeDtypeStruct((2,) + spec_shape, F32),
-            jax.ShapeDtypeStruct(arrived.shape, BF16),
+            jax.ShapeDtypeStruct((middle, 4 * each, rows), BF16),
         ],
         scratch_shapes=[
             pltpu.VMEM((blocks * 2 * each, rows), F32),
@@ -311,21 +372,23 @@
             pltpu.VMEM(spec_shape, BF16),
             pltpu.VMEM(spec_shape, F32),
             pltpu.VMEM((blocks * each, rows), F32),
-            pltpu.SemaphoreType.DMA(()),
+            pltpu.SemaphoreType.DMA((2,)),
         ],
         compiler_params=params(),
         name="conv",
-    )(arrived, gm, *tabs)
-
-
-def corr_call(back, spectra, tabs, each):
-    blocks, _, rows = back.shape
+    )(place, arrived, *gm, *tabs)
+
+
+def corr_call(place, back, spectra, tabs, each):
+    middle, _, rows = back.shape
+    blocks = 2 * middle
     spec_shape = (each * blocks, 2 * rows)
     return pl.pallas_call(
         corr_kernel,
-        in_specs=[VMEM] * (2 + len(tabs)),
-        out_specs=VMEM,
-        out_shape=jax.ShapeDtypeStruct(back.shape, BF16),
+        in_specs=[SMEM] + [VMEM] * (2 + len(tabs)),
+        out_specs=[VMEM, HBM],
+        out_shape=[jax.ShapeDtypeStruct((blocks, 2 * each, rows), BF16)]
+        + [pltpu.HBM((middle, each, rows), BF16)],
         scratch_shapes=[
             pltpu.VMEM((blocks * each, rows), F32),
             pltpu.VMEM(spec_shape, BF16),
@@ -333,10 +396,12 @@
             pltpu.VMEM(spec_shape, F32),
             pltpu.VMEM(spec_shape, F32),
             pltpu.VMEM((blocks * 2 * each, rows), F32),
-        ],
-        compiler_params=params(),
+            pltpu.SemaphoreType.DMA(()),
+        ],
+        compiler_params=params(),
+        cost_estimate=COSTLY,
         name="corr",
-    )(back, spectra, *tabs)
+    )(place, back, spectra, *tabs)
 
 
 def local(projected, skip_gain, out_weight, long_filter, cotangent):
@@ -345,13 +410,25 @@
     each = channels // blocks
     width = out_weight.shape[1]
     half = width // 2
-    chan = lax.axis_index("chan").astype(jnp.int32).reshape(1)
+    seq = lax.axis_index("seq").astype(jnp.int32)
+    middle = blocks // 2
+    place = jnp.stack([lax.axis_index("chan").astype(jnp.int32), seq % 2])
     in_hbm = lambda x: pltpu.with_memory_space_constraint(x, pltpu.HBM)
     proj = in_hbm(projected.transpose(1, 0, 2))
     out_weight = in_hbm(out_weight)
     long_filter = in_hbm(long_filter)
     skip = skip_gain.reshape(1, channels)
-    tabs = [jnp.asarray(t) for t in tables(blocks, rows)]
+    tabs_conv, tabs_corr = tables(blocks, rows)
+    chips = [[2 * m + near for m in range(middle)] for near in range(2)]
+
+    def partner(x):
+        return lax.ppermute(x, "seq", [(i, i ^ 1) for i in range(blocks)])
+
+    in_hbm = lambda x: pltpu.with_memory_space_constraint(x, pltpu.HBM)
+    proj = in_hbm(projected.transpose(1, 0, 2))
+    out_weight = in_hbm(out_weight)
+    long_filter = in_hbm(long_filter)
+    skip = skip_gain.reshape(1, channels)
     full = lambda shape: pl.BlockSpec(shape, lambda *_: (0,) * len(shape))
     shape = jax.ShapeDtypeStruct
 
@@ -381,7 +458,8 @@
     )(proj, long_filter)
     arrived = exchange(signals)
 
-    gm, query, gg, skip_source, skip_grad = pl.pallas_call(
+    span = cb // (2 * each)
+    query, gg, skip_source, skip_grad, gm_own, gm_give = pl.pallas_call(
         grad_kernel,
         grid_spec=pltpu.PrefetchScalarGridSpec(
             num_scalar_prefetch=1,
@@ -393,40 +471,58 @@
                 pl.BlockSpec((3, rows, cb), lambda i, c: (0, 0, i)),
                 pl.BlockSpec((1, cb), lambda i, c: (0, i)),
             ],
-            out_specs=[pl.BlockSpec((cb, rows), lambda i, c: (i, 0))] * 4
-            + [pl.BlockSpec((rows, cb), lambda i, c: (0, i))],
+            out_specs=[pl.BlockSpec((cb, rows), lambda i, c: (i, 0))] * 3
+            + [pl.BlockSpec((rows, cb), lambda i, c: (0, i))]
+            + [hbm] * 2,
+            scratch_shapes=[
+                pltpu.VMEM((parts, 2, span, each, rows), BF16),
+                pltpu.SemaphoreType.DMA((parts, 2)),
+            ],
         ),
-        out_shape=[shape((channels, rows), BF16)] * 2
+        out_shape=[shape((channels, rows), BF16)]
         + [shape((channels, rows), F32)] * 2
-        + [shape((rows, channels), F32)],
-        compiler_params=params(),
-        cost_estimate=pl.CostEstimate(flops=10**11, transcendentals=0, bytes_accessed=10**9),
+        + [shape((rows, channels), F32)]
+        + [pltpu.HBM((middle, each, rows), BF16)] * 2,
+        compiler_params=params(),
+        cost_estimate=COSTLY,
         name="grad",
-    )(chan, out_weight, cotangent, other, proj, skip)
-
-    spectra, mid = conv_call(arrived, in_hbm(gm.reshape(blocks, each, rows)), tabs, each)
-    back = exchange(mid)
-
-    pair = corr_call(back, spectra, tabs, each)
+    )(place, out_weight, in_hbm(cotangent), in_hbm(other), proj, skip)
+    gm = [in_hbm(gm_own), partner(gm_give)]
+
+    spectra, mid = conv_call(place, arrived, gm, tabs_conv, each)
+    back = lax.all_to_all(mid, "seq", 0, 0, tiled=True, axis_index_groups=chips)
+    pair, conv_give = corr_call(place, back, spectra, tabs_corr, each)
+    conv_got = partner(conv_give)
     last = exchange(pair)
 
     pieces = 4
     wb = half // pieces
     weights = pltpu.VMEM((pieces, channels, wb), BF16)
     sems = pltpu.SemaphoreType.DMA((pieces,))
-    send, gated = pl.pallas_call(
+    send, gated, mixing = pl.pallas_call(
         mix_kernel,
-        in_specs=[smem, vmem, vmem, vmem, hbm],
-        out_specs=[hbm, vmem],
-        out_shape=[pltpu.HBM((rows, half), BF16), shape((rows, channels), BF16)],
-        scratch_shapes=[weights, pltpu.VMEM((pieces, rows, wb), BF16), sems, sems],
-        compiler_params=params(),
+        in_specs=[smem] + [vmem] * 4 + [hbm],
+        out_specs=[hbm, vmem, vmem],
+        out_shape=[
+            pltpu.HBM((rows, half), BF16),
+            shape((rows, channels), BF16),
+            shape((channels, rows), F32),
+        ],
+        scratch_shapes=[
+            pltpu.VMEM((middle, 2, each, rows), F32),
+            weights,
+            pltpu.VMEM((pieces, rows, wb), BF16),
+            sems,
+            sems,
+        ],
+        compiler_params=params(),
+        cost_estimate=COSTLY,
         name="mix",
-    )(chan, back, skip_source, query, out_weight)
+    )(place, back, conv_got, skip_source, query, out_weight)
     received = lax.ppermute(send, "chan", [(0, 1), (1, 0)])
     kept, stacked = pl.pallas_call(
         own_kernel,
-        in_specs=[smem, vmem, vmem, vmem, vmem, hbm],
+        in_specs=[smem, vmem, vmem, vmem, hbm],
         out_specs=[vmem, hbm],
         out_shape=[shape((rows, half), F32), pltpu.HBM((3, rows, channels), BF16)],
         scratch_shapes=[
@@ -437,7 +533,7 @@
         ],
         compiler_params=params(),
         name="own",
-    )(chan, back, skip_source, in_hbm(gg), gated, out_weight)
+    )(place, mixing, in_hbm(gg), gated, out_weight)
     mixed = (kept + received.astype(F32)).astype(BF16)
 
     grad_projected, grad_filter = pl.pallas_call(

time: 106 us -> 104 us (0.981)
  blocking collectives: 27 us -> 22 us
  starting transfers between devices: 23.4 us -> 27.1 us
  Pallas kernels: 23.5 us -> 25.6 us
  local copies, waits for them, and re-layouts: 4.31 us -> 2.32 us
  waiting for transfers between devices: 25.7 us -> 24.5 us
    all_to_all x1, blocking collectives: 27 us -> 22 us  [local(): back = lax.all_to_all(mid, 'seq', 0, 0, tiled=True, axis_index_groups=chips)]
    ppermute x0 -> x2, starting transfers between devices: none -> 2.88 us  [partner(): return lax.ppermute(x, 'seq', [(i, i ^ 1) for i in range(blocks)])]
    all_to_all x2, waiting for transfers between devices: 12.7 us -> 10.7 us  [exchange(): return lax.all_to_all(x, 'seq', 0, 0, tiled=True)]
    unnamed x32 -> x24, local copies, waits for them, and re-layouts: 4.31 us -> 2.32 us
    pallas_call x1, Pallas kernels: 6.02 us -> 7.5 us  [local(): pl.pallas_call(grad_kernel, grid_spec=pltpu.PrefetchScalarGridSpec(num_sc...]
    ppermute x0 -> x2, waiting for transfers between devices: none -> 1.2 us  [partner(): return lax.ppermute(x, 'seq', [(i, i ^ 1) for i in range(blocks)])]
  transfers between devices with their start and end apart: 4 -> 6, of which waited for: 3 -> 4; matrix products, arithmetic and copies ran while one was open for 1% -> 1% of each run, Pallas kernels for 15% -> 17%
where the time goes in v3:
time: 104 us
  starting transfers between devices  27.1 us (26%)
  Pallas kernels  25.6 us (25%)
  waiting for transfers between devices  24.5 us (24%)
  blocking collectives  22 us (21%)
  local copies, waits for them, and re-layouts  2.32 us (2%)
    all_to_all x2, starting transfers between devices, exchange(): return lax.all_to_all(x, 'seq', 0, 0, tiled=True)  22 us
    all_to_all x1, blocking collectives, local(): back = lax.all_to_all(mid, 'seq', 0, 0, tiled=True, axis_index_groups=chips)  22 us
    ppermute x1, waiting for transfers between devices, local(): received = lax.ppermute(send, 'chan', [(0, 1), (1, 0)])  12.6 us
    all_to_all x2, waiting for transfers between devices, exchange(): return lax.all_to_all(x, 'seq', 0, 0, tiled=True)  10.7 us
    pallas_call x1, Pallas kernels, local(): pl.pallas_call(grad_kernel, grid_spec=pltpu.PrefetchScalarGridSpec(num_sc...  7.5 us
    pallas_call x1, Pallas kernels, corr_call(): pl.pallas_call(corr_kernel, in_specs=[SMEM] + [VMEM] * (2 + len(tabs)), o...  3.93 us
    pallas_call x1, Pallas kernels, local(): pl.pallas_call(mix_kernel, in_specs=[smem] + [vmem] * 4 + [hbm], out_spec...  3.91 us
    pallas_call x1, Pallas kernels, local(): pl.pallas_call(own_kernel, in_specs=[smem, vmem, vmem, vmem, hbm], out_sp...  3.82 us
  transfers between devices with their start and end apart: 6, of which 4 were waited for; matrix products, arithmetic and copies ran while one was open for 1% of the time, Pallas kernels for 17%

profile of v3, /device:TPU:1, one launch (start us, length us, event | category | flops | bytes accessed | tf_op | source)
XLA Modules:
  0.0 103.5 jit_solution(6949819176367299150)
XLA Ops:
  0.6 2.1 %collective-permute-start = (bf16[128,2048]{1,0:T(8,128)(2,1)}, bf16[128,2048]{1,0:T(8,128)(2,1)S(1)}, u32[]{:S(2)}, u32[]{:S(2)}) collective-permute-start(bf16[128,2048]{1,0:T(8,128)(2,1)} %own_ref.1), channel_id=1, source_target_pairs={{0,1},{1,0},{2,3},{3,2},{4,5},{5,4},{6,7},{7,6},{8,9},{9,8},{10,11... | collective-permute-start | bytes 1572872 | tf_op jit(solution)/shard_map/ppermute | solution.py:435
  2.8 2.5 %prep.1 = bf16[128,16,128]{2,1,0:T(8,128)(2,1)} custom-call(bf16[3,128,1024]{2,1,0:T(8,128)(2,1)} %bitcast.5, f32[128,1024]{1,0:T(8,128)} %filter_hbm.1), custom_call_target="tpu_custom_call" | custom-call | tf_op jit(solution)/shard_map/prep/pallas_call | solution.py:444
  5.3 15.6 %all-to-all-start = ((bf16[128,16,128]{2,1,0:T(8,128)(2,1)}), bf16[128,16,128]{2,1,0:T(8,128)(2,1)S(1)}, u32[]{:S(2)}, u32[]{:S(2)}) async-start(bf16[128,16,128]{2,1,0:T(8,128)(2,1)} %prep.1), calls=%async_computation | async-start | bytes 1048576 | tf_op jit(solution)/shard_map/all_to_all | solution.py:438
  20.9 0.1 pad_add_fusion.place_ref.refs_0_
  20.9 0.0 collective-permute-done.other_ref
  20.9 0.8 copy-done.11
  21.7 0.7 copy-done.8
  22.4 0.0 copy-start.6
  22.4 0.0 copy-start.7
  22.5 0.0 copy-start.9
  22.5 0.0 copy-start.10
  22.5 7.5 %grad.1 = (bf16[1024,128]{1,0:T(8,128)(2,1)S(1)}, f32[1024,128]{1,0:T(8,128)S(1)}, f32[1024,128]{1,0:T(8,128)S(1)}, f32[128,1024]{1,0:T(8,128)S(1)}, bf16[64,8,1...) custom-call(s32[2]{0:T(128)S(1)} %pad_add_fusion.place_ref.refs_0_, bf16[1024,4096]{1,0:T(8,128)(2,1)} %w_hbm.1, ...), custom_call_target="tpu_custom_call" | custom-call | flops 99999997952 | bytes 1000000000 | tf_op jit(solution)/shard_map/grad/pallas_call | solution.py:462
  30.0 0.8 copy-done.1
  30.8 0.9 collective-permute-start.1
  31.7 1.2 %collective-permute-done.1.refs_3_ = bf16[64,8,128]{2,1,0:T(8,128)(2,1)S(1)} collective-permute-done((bf16[64,8,128]{2,1,0:T(8,128)(2,1)}, bf16[64,8,128]{2,1,0:T(8,128)(2,1)S(1)}, u32[]{:S(2)}, u32[]{:S(2)}) %collective-permute-start.1) | collective-permute-done | bytes 131104 | tf_op jit(solution)/shard_map/ppermute | solution.py:425
  32.9 10.0 %all-to-all-done.refs_1_ = bf16[128,16,128]{2,1,0:T(8,128)(2,1)S(1)} async-done(((bf16[128,16,128]{2,1,0:T(8,128)(2,1)}), bf16[128,16,128]{2,1,0:T(8,128)(2,1)S(1)}, u32[]{:S(2)}, u32[]{:S(2)}) %all-to-all-start) | async-done | bytes 524320 | tf_op jit(solution)/shard_map/all_to_all | solution.py:438
  42.9 0.0 copy-done.5
  42.9 0.0 copy-done.6
  42.9 2.8 %conv.1 = (f32[2,1024,256]{2,1,0:T(8,128)S(1)}, bf16[64,32,128]{2,1,0:T(8,128)(2,1)S(1)}) custom-call(s32[2]{0:T(128)S(1)} %pad_add_fusion.place_ref.refs_0_, bf16[128,16,128]{2,1,0:T(8,128)(2,1)S(1)} %all-to-all-done.refs_1_, bf16[64,8,128]{2,1,0:T(8,128)(2,1)} %get-tuple-element.20.refs_2_, bf16[64,8,128]{2,1,0:T(8,128)(2,1)S(1)} %collective-permute-done.1.refs_3_, ...), custom_call_target="tpu_custom_call" | custom-call | tf_op jit(solution)/shard_map/conv/pallas_call | solution.py:361
  45.8 22.0 %all_to_all.15.refs_1_.in_ref = bf16[64,32,128]{2,1,0:T(8,128)(2,1)S(1)} all-to-all(bf16[64,32,128]{2,1,0:T(8,128)(2,1)S(1)} %get-tuple-element.22), channel_id=1, replica_groups={{0,4,8,12,16,20,24,28,32,36,40,44,48,52,56,60,64,68,72,76,80,84,88,92,9..., dimensions={0} | all-to-all | bytes 1048576 | tf_op jit(solution)/shard_map/all_to_all | solution.py:493
  67.8 3.9 %corr.1 = (bf16[128,16,128]{2,1,0:T(8,128)(2,1)}, bf16[64,8,128]{2,1,0:T(8,128)(2,1)}) custom-call(s32[2]{0:T(128)S(1)} %pad_add_fusion.place_ref.refs_0_, bf16[64,32,128]{2,1,0:T(8,128)(2,1)S(1)} %all_to_all.15.refs_1_.in_ref, f32[2,1024,256]{2,1,0:T(8,128)S(1)} %get-tuple-element.23.refs_2_, bf16[256,256]{1,0:T(8,128)(2,1)S(1)} %copy-done.10, ...), custom_call_target="tpu_custom_call" | custom-call | flops 99999997952 | bytes 1000000000 | tf_op jit(solution)/shard_map/corr/pallas_call | solution.py:386
  71.7 2.0 %collective-permute-start.2 = (bf16[64,8,128]{2,1,0:T(8,128)(2,1)}, bf16[64,8,128]{2,1,0:T(8,128)(2,1)S(1)}, u32[]{:S(2)}, u32[]{:S(2)}) collective-permute-start(bf16[64,8,128]{2,1,0:T(8,128)(2,1)} %get-tuple-element.24), channel_id=1, source_target_pairs={{0,2},{2,0},{4,6},{6,4},{8,10},{10,8},{12,14},{14,12},{16,18},{18,... | collective-permute-start | bytes 393224 | tf_op jit(solution)/shard_map/ppermute | solution.py:425
  73.7 6.4 %all-to-all-start.2 = ((bf16[128,16,128]{2,1,0:T(8,128)(2,1)}), bf16[128,16,128]{2,1,0:T(8,128)(2,1)S(1)}, u32[]{:S(2)}, u32[]{:S(2)}) async-start(bf16[128,16,128]{2,1,0:T(8,128)(2,1)} %get-tuple-element.32), calls=%async_computation.2 | async-start | bytes 1048576 | tf_op jit(solution)/shard_map/all_to_all | solution.py:438
  80.2 0.0 collective-permute-done.2.refs_0_
  80.2 3.9 %mix.1 = (bf16[128,2048]{1,0:T(8,128)(2,1)}, bf16[128,1024]{1,0:T(8,128)(2,1)S(1)}, f32[1024,128]{1,0:T(8,128)S(1)}) custom-call(s32[2]{0:T(128)S(1)} %pad_add_fusion.place_ref.refs_0_, bf16[64,32,128]{2,1,0:T(8,128)(2,1)S(1)} %all_to_all.15.refs_1_.in_ref, bf16[64,8,128]{2,1,0:T(8,128)(2,1)S(1)} %collective-permute-done.2.refs_0_, ...), custom_call_target="tpu_custom_call" | custom-call | flops 99999997952 | bytes 1000000000 | tf_op jit(solution)/shard_map/mix/pallas_call | solution.py:502
  84.1 0.0 copy-start
  84.1 0.1 collective-permute-start.3
  84.2 3.8 %own.1 = (f32[128,2048]{1,0:T(8,128)S(1)}, bf16[3,128,1024]{2,1,0:T(8,128)(2,1)}) custom-call(s32[2]{0:T(128)S(1)} %pad_add_fusion.place_ref.refs_0_, f32[1024,128]{1,0:T(8,128)S(1)} %get-tuple-element.27.mixing_ref, f32[1024,128]{1,0:T(8,128)} %copy-done.1, bf16[128,1024]{1,0:T(8,128)(2,1)S(1)} %get-tuple-element.29.gated_ref, bf16[1024,4096]{1,0:T(8,128)(2,1)} %w_hbm.1), custom_call_target="tpu_custom_call" | custom-call | tf_op jit(solution)/shard_map/own/pallas_call | solution.py:523
  88.0 12.6 %collective-permute-done.3 = bf16[128,2048]{1,0:T(8,128)(2,1)S(1)} collective-permute-done((bf16[128,2048]{1,0:T(8,128)(2,1)}, bf16[128,2048]{1,0:T(8,128)(2,1)S(1)}, u32[]{:S(2)}, u32[]{:S(2)}) %collective-permute-start.3) | collective-permute-done | bytes 524320 | tf_op jit(solution)/shard_map/ppermute | solution.py:522
  100.6 0.9 add_convert_fusion
  101.6 0.7 all-to-all-done.2.in_ref
  102.2 1.1 %end.1 = (bf16[3,128,1024]{2,1,0:T(8,128)(2,1)}, f32[128,1024]{1,0:T(8,128)}) custom-call(bf16[128,16,128]{2,1,0:T(8,128)(2,1)S(1)} %all-to-all-done.2.in_ref, f32[128,1024]{1,0:T(8,128)S(1)} %get-tuple-element.33.sg_ref, bf16[3,128,1024]{2,1,0:T(8,128)(2,1)S(1)} %bitcast.7, ...), custom_call_target="tpu_custom_call", output_to_operand_aliasing={{0}: (3, {})} | custom-call | tf_op jit(solution)/shard_map/end/pallas_call | solution.py:539
  (14 shorter events, 0.0 us)
Async XLA Ops:
  0.6 20.3 %collective-permute-start = (bf16[128,2048]{1,0:T(8,128)(2,1)}, bf16[128,2048]{1,0:T(8,128)(2,1)S(1)}, u32[]{:S(2)}, u32[]{:S(2)}) collective-permute-start(bf16[128,2048]{1,0:T(8,128)(2,1)} %own_ref.1), channel_id=1, source_target_pairs={{0,1},{1,0},{2,3},{3,2},{4,5},{5,4},{6,7},{7,6},{8,9},{9,8},{10,11... | collective-permute-start | bytes 1572872 | tf_op jit(solution)/shard_map/ppermute | solution.py:435
  5.3 37.6 %all-to-all-start = ((bf16[128,16,128]{2,1,0:T(8,128)(2,1)}), bf16[128,16,128]{2,1,0:T(8,128)(2,1)S(1)}, u32[]{:S(2)}, u32[]{:S(2)}) async-start(bf16[128,16,128]{2,1,0:T(8,128)(2,1)} %prep.1), calls=%async_computation | async-start | bytes 1048576 | tf_op jit(solution)/shard_map/all_to_all | solution.py:438
  20.9 0.8 copy-start.11
  21.7 0.7 copy-start.8
  22.4 20.5 %copy-start.2 = (bf16[256,256]{1,0:T(8,128)(2,1)S(1)}, bf16[256,256]{1,0:T(8,128)(2,1)}, u32[]{:S(2)}) copy-start(bf16[256,256]{1,0:T(8,128)(2,1)} %constant.42.clone.refs_9_.refs_8_) | copy-start | bytes 393220
  22.4 20.5 %copy-start.3 = (bf16[256,256]{1,0:T(8,128)(2,1)S(1)}, bf16[256,256]{1,0:T(8,128)(2,1)}, u32[]{:S(2)}) copy-start(bf16[256,256]{1,0:T(8,128)(2,1)} %constant.41.clone.refs_8_.refs_7_) | copy-start | bytes 393220
  22.4 20.5 %copy-start.4 = (bf16[256,256]{1,0:T(8,128)(2,1)S(1)}, bf16[256,256]{1,0:T(8,128)(2,1)}, u32[]{:S(2)}) copy-start(bf16[256,256]{1,0:T(8,128)(2,1)} %constant.38.clone.refs_5_) | copy-start | bytes 393220
  22.4 20.5 %copy-start.5 = (bf16[256,256]{1,0:T(8,128)(2,1)S(1)}, bf16[256,256]{1,0:T(8,128)(2,1)}, u32[]{:S(2)}) copy-start(bf16[256,256]{1,0:T(8,128)(2,1)} %constant.37.clone.refs_4_) | copy-start | bytes 393220
  22.4 20.5 %copy-start.6 = (f32[128,128]{1,0:T(8,128)S(1)}, f32[128,128]{1,0:T(8,128)}, u32[]{:S(2)}) copy-start(f32[128,128]{1,0:T(8,128)} %constant.40.clone.refs_7_.refs_6_) | copy-start | bytes 196612
  22.4 20.5 %copy-start.7 = (f32[128,128]{1,0:T(8,128)S(1)}, f32[128,128]{1,0:T(8,128)}, u32[]{:S(2)}) copy-start(f32[128,128]{1,0:T(8,128)} %constant.39.clone.refs_6_.refs_5_) | copy-start | bytes 196612
  22.5 45.3 %copy-start.9 = (bf16[256,256]{1,0:T(8,128)(2,1)S(1)}, bf16[256,256]{1,0:T(8,128)(2,1)}, u32[]{:S(2)}) copy-start(bf16[256,256]{1,0:T(8,128)(2,1)} %constant.44.clone.refs_4_) | copy-start | bytes 393220
  22.5 45.3 %copy-start.10 = (bf16[256,256]{1,0:T(8,128)(2,1)S(1)}, bf16[256,256]{1,0:T(8,128)(2,1)}, u32[]{:S(2)}) copy-start(bf16[256,256]{1,0:T(8,128)(2,1)} %constant.43.clone.refs_3_) | copy-start | bytes 393220
  30.0 0.8 copy-start.1
  30.8 2.1 %collective-permute-start.1 = (bf16[64,8,128]{2,1,0:T(8,128)(2,1)}, bf16[64,8,128]{2,1,0:T(8,128)(2,1)S(1)}, u32[]{:S(2)}, u32[]{:S(2)}) collective-permute-start(bf16[64,8,128]{2,1,0:T(8,128)(2,1)} %get-tuple-element.21), channel_id=1, source_target_pairs={{0,2},{2,0},{4,6},{6,4},{8,10},{10,8},{12,14},{14,12},{16,18},{18,... | collective-permute-start | bytes 393224 | tf_op jit(solution)/shard_map/ppermute | solution.py:425
  71.7 8.4 %collective-permute-start.2 = (bf16[64,8,128]{2,1,0:T(8,128)(2,1)}, bf16[64,8,128]{2,1,0:T(8,128)(2,1)S(1)}, u32[]{:S(2)}, u32[]{:S(2)}) collective-permute-start(bf16[64,8,128]{2,1,0:T(8,128)(2,1)} %get-tuple-element.24), channel_id=1, source_target_pairs={{0,2},{2,0},{4,6},{6,4},{8,10},{10,8},{12,14},{14,12},{16,18},{18,... | collective-permute-start | bytes 393224 | tf_op jit(solution)/shard_map/ppermute | solution.py:425
  73.7 28.5 %all-to-all-start.2 = ((bf16[128,16,128]{2,1,0:T(8,128)(2,1)}), bf16[128,16,128]{2,1,0:T(8,128)(2,1)S(1)}, u32[]{:S(2)}, u32[]{:S(2)}) async-start(bf16[128,16,128]{2,1,0:T(8,128)(2,1)} %get-tuple-element.32), calls=%async_computation.2 | async-start | bytes 1048576 | tf_op jit(solution)/shard_map/all_to_all | solution.py:438
  84.1 18.1 %copy-start = (bf16[128,3,1024]{2,0,1:T(8,128)(2,1)S(1)}, bf16[128,3,1024]{2,0,1:T(8,128)(2,1)}, u32[]{:S(2)}) copy-start(bf16[128,3,1024]{2,0,1:T(8,128)(2,1)} %param.13) | copy-start | bytes 2359300
  84.1 16.5 %collective-permute-start.3 = (bf16[128,2048]{1,0:T(8,128)(2,1)}, bf16[128,2048]{1,0:T(8,128)(2,1)S(1)}, u32[]{:S(2)}, u32[]{:S(2)}) collective-permute-start(bf16[128,2048]{1,0:T(8,128)(2,1)} %get-tuple-element.31), channel_id=1, source_target_pairs={{0,1},{1,0},{2,3},{3,2},{4,5},{5,4},{6,7},{7,6},{8,9},{9,8},{10,11... | collective-permute-start | bytes 1572872 | tf_op jit(solution)/shard_map/ppermute | solution.py:522

commit v4 on v3

--- a/solution.py
+++ b/solution.py
@@ -33,9 +33,10 @@
     outer_high, outer_low = halves(outer)
     outer_both = np.concatenate([outer_high, outer_low], axis=1)
     back_both = np.concatenate(halves(outer.T), axis=0)
-    order = np.arange(blocks).reshape(blocks // 2, 2).T.reshape(-1)
-    outer_order = np.concatenate([outer_high[:, order], outer_low[:, order]], axis=1)
-    back_order = np.concatenate(halves(outer.T[order]), axis=0)
+    even = np.arange(blocks).reshape(blocks // 2, 2).T.reshape(-1)
+    orders = [even, np.roll(even, blocks // 2)]
+    outer_order = np.stack([np.concatenate([outer_high[:, o], outer_low[:, o]], 1) for o in orders])
+    back_order = np.stack([np.concatenate(halves(outer.T[o]), axis=0) for o in orders])
     turn = 2.0 * np.pi * k1 * np.arange(rows)[None, :] / length
     turn_re = np.cos(turn).astype(np.float32)
     turn_im = -np.sin(turn).astype(np.float32)
@@ -148,17 +149,17 @@
         write.wait()
 
 
-def slot_of(near, place_ref):
-    return near ^ place_ref[1]
+def core():
+    return lax.axis_index("seq") & 1
 
 
 def grad_kernel(
-    place_ref, w_ref, own_ref, other_ref, proj_ref, skip_ref,
+    w_ref, own_ref, other_ref, proj_ref, skip_ref,
     q_ref, gg_ref, ss_ref, sg_ref, *rest,
 ):
     pieces, (gm_ref, sem_ref) = rest[:2], rest[2:]
     half = own_ref.shape[1]
-    first = place_ref[0] == 0
+    first = lax.axis_index("chan") == 0
     own, other = own_ref[...], other_ref[...]
     low = jnp.where(first, own, other)
     high = jnp.where(first, other, own)
@@ -181,7 +182,7 @@
         for near in range(2):
             for k in range(2):
 
-                @pl.when(slot_of(near, place_ref) == k)
+                @pl.when(near ^ core() == k)
                 def _():
                     act(
                         pltpu.make_async_copy(
@@ -202,10 +203,9 @@
 
 
 def conv_kernel(*refs):
-    place_ref, in_ref = refs[:2]
-    gm_refs, tabs = refs[2:4], refs[4:10]
-    spec_ref, out_ref = refs[10:12]
-    wide_ref, high_ref, low_ref, part_ref, back_ref, gm_sem = refs[12:]
+    in_ref, gm_refs, tabs = refs[0], refs[1:3], refs[3:9]
+    spec_ref, out_ref = refs[9:11]
+    wide_ref, high_ref, low_ref, part_ref, back_ref, gm_sem = refs[11:]
     blocks, two, rows = in_ref.shape
     count = two // 2
     middle = blocks // 2
@@ -217,113 +217,126 @@
     ]
     for copy in copies:
         copy.start()
-    wide_ref[...] = in_ref[...].astype(F32).reshape(blocks * two, rows)
     for s in range(2):
+        wide_ref[s] = in_ref[:, s * count : (s + 1) * count, :].astype(F32).reshape(-1, rows)
 
         def load(c):
-            return wide_ref[pl.ds(s * count + c, blocks, stride=two), :]
+            return wide_ref[s, pl.ds(c, blocks, stride=count), :]
 
         forward(load, blocks, rows, count, tabs, high_ref, low_ref, spec_ref.at[s])
     product(spec_ref.at[0], spec_ref.at[1], False, high_ref, low_ref)
 
     def store(c, y):
-        for near in range(2):
-            at = slot_of(near, place_ref) * count + c
-            back_ref[pl.ds(at, middle, stride=2 * count), :] = y[near * middle : (near + 1) * middle]
-
-    inverse(high_ref, low_ref, part_ref, tabs, 1.0 / (blocks * rows), blocks, rows, count, store)
+        back_ref[pl.ds(c, blocks, stride=count), :] = y
+
+    mine = (tabs[0], tabs[1].at[core()], *tabs[2:])
+    inverse(high_ref, low_ref, part_ref, mine, 1.0 / (blocks * rows), blocks, rows, count, store)
     for copy in copies:
         copy.wait()
-    out_ref[:, 2 * count :, :] = back_ref[...].reshape(middle, 2 * count, rows).astype(BF16)
+    for k in range(2):
+        part = back_ref[k * middle * count : (k + 1) * middle * count, :]
+        out_ref[:, (2 + k) * count : (3 + k) * count, :] = part.reshape(
+            middle, count, rows
+        ).astype(BF16)
 
 
 def corr_kernel(*refs):
-    place_ref, in_ref, spec_ref = refs[:3]
-    tabs = refs[3:9]
-    out_ref, piece = refs[9:11]
-    wide_ref, high_ref, low_ref, part_ref, grad_ref, back_ref, sem = refs[11:]
+    in_ref, spec_ref = refs[:2]
+    tabs = refs[2:8]
+    out_ref, piece = refs[8:10]
+    wide_ref, high_ref, low_ref, part_ref, grad_ref, back_ref, sem = refs[10:]
     blocks, two, rows = out_ref.shape
     count = two // 2
     middle = blocks // 2
     copy = pltpu.make_async_copy(in_ref.at[:, 3 * count :, :], piece, sem)
     copy.start()
-    wide_ref[...] = in_ref[:, : 2 * count, :].astype(F32).reshape(middle * 2 * count, rows)
+    for k in range(2):
+        part = in_ref[:, k * count : (k + 1) * count, :].astype(F32)
+        wide_ref[k * middle * count : (k + 1) * middle * count, :] = part.reshape(-1, rows)
 
     def load(c):
-        return jnp.concatenate(
-            [
-                wide_ref[pl.ds(slot_of(near, place_ref) * count + c, middle, stride=2 * count), :]
-                for near in range(2)
-            ],
-            axis=0,
-        )
-
-    forward(load, blocks, rows, count, tabs, high_ref, low_ref, grad_ref)
+        return wide_ref[pl.ds(c, blocks, stride=count), :]
+
+    mine = (tabs[0].at[core()], *tabs[1:])
+    forward(load, blocks, rows, count, mine, high_ref, low_ref, grad_ref)
     scale = 1.0 / (blocks * rows)
     for s, factor in ((1, scale), (0, scale / math.sqrt(blocks * rows))):
 
         def store(c, y):
-            back_ref[pl.ds((1 - s) * count + c, blocks, stride=two), :] = y
+            back_ref[1 - s, pl.ds(c, blocks, stride=count), :] = y
 
         product(spec_ref.at[s], grad_ref, True, high_ref, low_ref)
         inverse(high_ref, low_ref, part_ref, tabs, factor, blocks, rows, count, store)
-    out_ref[...] = back_ref[...].reshape(blocks, two, rows).astype(BF16)
+    for k in range(2):
+        out_ref[:, k * count : (k + 1) * count, :] = (
+            back_ref[k].reshape(blocks, count, rows).astype(BF16)
+        )
     copy.wait()
 
 
 def weight_copies(w_hbm, chan, buf_ref, sem_ref):
-    parts, _, width = buf_ref.shape
+    parts, band, width = buf_ref.shape
+    columns = pl.ds(pl.multiple_of(chan * width, width), width)
     return [
         pltpu.make_async_copy(
-            w_hbm.at[:, pl.ds(pl.multiple_of((chan * parts + i) * width, width), width)],
-            buf_ref.at[i],
-            sem_ref.at[i],
+            w_hbm.at[i * band : (i + 1) * band, columns], buf_ref.at[i], sem_ref.at[i]
         )
         for i in range(parts)
     ]
 
 
-def mix_kernel(
-    place_ref, in_ref, *refs
-):
+def project(gated_ref, buf_ref, copies, put):
+    parts, band, width = buf_ref.shape
+    total = 0.0
+    for i in range(parts - 1):
+        copies[i].wait()
+        total = total + dot(gated_ref[:, i * band : (i + 1) * band], buf_ref[i])
+    copies[-1].wait()
+    step = width // 4
+    for j in range(4):
+        at = slice(j * step, (j + 1) * step)
+        put(j, at, total[:, at] + dot(gated_ref[:, -band:], buf_ref[parts - 1, :, at]))
+
+
+def mix_kernel(in_ref, *refs):
     other_ref, ss_ref, q_ref, w_hbm, send_hbm, gated_ref, mixing_ref = refs[:7]
     all_ref, buf_ref, send_ref, in_sem, out_sem = refs[7:]
-    parts, _, width = buf_ref.shape
-    copies = weight_copies(w_hbm, 1 - place_ref[0], buf_ref, in_sem)
+    copies = weight_copies(w_hbm, 1 - lax.axis_index("chan"), buf_ref, in_sem)
     for copy in copies:
         copy.start()
     count = in_ref.shape[1] // 4
-    all_ref[:, place_ref[1]] = in_ref[:, 2 * count : 3 * count, :].astype(F32)
-    all_ref[:, 1 - place_ref[1]] = other_ref[...].astype(F32)
+    all_ref[:, core()] = in_ref[:, 2 * count : 3 * count, :].astype(F32)
+    all_ref[:, 1 - core()] = other_ref[...].astype(F32)
     mixing = all_ref[...].reshape(ss_ref.shape) + ss_ref[...]
     mixing_ref[...] = mixing
     gated_ref[...] = (mixing * q_ref[...].astype(F32)).T.astype(BF16)
     writes = []
-    for i, copy in enumerate(copies):
-        copy.wait()
-        send_ref[i] = dot(gated_ref[...], buf_ref[i]).astype(BF16)
-        write = pltpu.make_async_copy(
-            send_ref.at[i], send_hbm.at[:, i * width : (i + 1) * width], out_sem.at[i]
-        )
+
+    def put(j, at, product):
+        send_ref[j] = product.astype(BF16)
+        write = pltpu.make_async_copy(send_ref.at[j], send_hbm.at[:, at], out_sem.at[j])
         write.start()
         writes.append(write)
+
+    project(gated_ref, buf_ref, copies, put)
     for write in writes:
         write.wait()
 
 
 def own_kernel(
-    place_ref, mixing_ref, gg_ref, gated_ref, w_hbm, out_ref, gp_hbm, buf_ref, gq_ref, in_sem, out_sem
+    mixing_ref, gg_ref, gated_ref, w_hbm, out_ref, gp_hbm, buf_ref, gq_ref, in_sem, out_sem
 ):
-    parts, _, width = buf_ref.shape
-    copies = weight_copies(w_hbm, place_ref[0], buf_ref, in_sem)
+    copies = weight_copies(w_hbm, lax.axis_index("chan"), buf_ref, in_sem)
     for copy in copies:
         copy.start()
     gq_ref[...] = (mixing_ref[...] * gg_ref[...]).T.astype(BF16)
     write = pltpu.make_async_copy(gq_ref, gp_hbm.at[0], out_sem)
     write.start()
-    for i, copy in enumerate(copies):
-        copy.wait()
-        out_ref[:, i * width : (i + 1) * width] = dot(gated_ref[...], buf_ref[i])
+
+    def put(j, at, product):
+        out_ref[:, at] = product
+
+    project(gated_ref, buf_ref, copies, put)
     write.wait()
 
 
@@ -351,23 +364,22 @@
 
 VMEM = pl.BlockSpec(memory_space=pltpu.VMEM)
 HBM = pl.BlockSpec(memory_space=pltpu.HBM)
-SMEM = pl.BlockSpec(memory_space=pltpu.SMEM)
-
-
-def conv_call(place, arrived, gm, tabs, each):
+
+
+def conv_call(arrived, gm, tabs, each):
     blocks, _, rows = arrived.shape
     middle = blocks // 2
     spec_shape = (each * blocks, 2 * rows)
     return pl.pallas_call(
         conv_kernel,
-        in_specs=[SMEM, VMEM] + [HBM] * 2 + [VMEM] * len(tabs),
+        in_specs=[VMEM] + [HBM] * 2 + [VMEM] * len(tabs),
         out_specs=[VMEM] * 2,
         out_shape=[
             jax.ShapeDtypeStruct((2,) + spec_shape, F32),
             jax.ShapeDtypeStruct((middle, 4 * each, rows), BF16),
         ],
         scratch_shapes=[
-            pltpu.VMEM((blocks * 2 * each, rows), F32),
+            pltpu.VMEM((2, blocks * each, rows), F32),
             pltpu.VMEM(spec_shape, BF16),
             pltpu.VMEM(spec_shape, BF16),
             pltpu.VMEM(spec_shape, F32),
@@ -376,16 +388,16 @@
         ],
         compiler_params=params(),
         name="conv",
-    )(place, arrived, *gm, *tabs)
-
-
-def corr_call(place, back, spectra, tabs, each):
+    )(arrived, *gm, *tabs)
+
+
+def corr_call(back, spectra, tabs, each):
     middle, _, rows = back.shape
     blocks = 2 * middle
     spec_shape = (each * blocks, 2 * rows)
     return pl.pallas_call(
         corr_kernel,
-        in_specs=[SMEM] + [VMEM] * (2 + len(tabs)),
+        in_specs=[VMEM] * (2 + len(tabs)),
         out_specs=[VMEM, HBM],
         out_shape=[jax.ShapeDtypeStruct((blocks, 2 * each, rows), BF16)]
         + [pltpu.HBM((middle, each, rows), BF16)],
@@ -395,13 +407,13 @@
             pltpu.VMEM(spec_shape, BF16),
             pltpu.VMEM(spec_shape, F32),
             pltpu.VMEM(spec_shape, F32),
-            pltpu.VMEM((blocks * 2 * each, rows), F32),
+            pltpu.VMEM((2, blocks * each, rows), F32),
             pltpu.SemaphoreType.DMA(()),
         ],
         compiler_params=params(),
         cost_estimate=COSTLY,
         name="corr",
-    )(place, back, spectra, *tabs)
+    )(back, spectra, *tabs)
 
 
 def local(projected, skip_gain, out_weight, long_filter, cotangent):
@@ -410,14 +422,7 @@
     each = channels // blocks
     width = out_weight.shape[1]
     half = width // 2
-    seq = lax.axis_index("seq").astype(jnp.int32)
     middle = blocks // 2
-    place = jnp.stack([lax.axis_index("chan").astype(jnp.int32), seq % 2])
-    in_hbm = lambda x: pltpu.with_memory_space_constraint(x, pltpu.HBM)
-    proj = in_hbm(projected.transpose(1, 0, 2))
-    out_weight = in_hbm(out_weight)
-    long_filter = in_hbm(long_filter)
-    skip = skip_gain.reshape(1, channels)
     tabs_conv, tabs_corr = tables(blocks, rows)
     chips = [[2 * m + near for m in range(middle)] for near in range(2)]
 
@@ -437,21 +442,22 @@
     def exchange(x):
         return lax.all_to_all(x, "seq", 0, 0, tiled=True)
 
-    smem, vmem, hbm = SMEM, VMEM, HBM
+    vmem, hbm = VMEM, HBM
     parts = 4
     cb = channels // parts
     pb = blocks // parts
+    fine = 2
     signals = pl.pallas_call(
         prep_kernel,
         in_specs=[hbm, hbm],
         out_specs=hbm,
         out_shape=shape((blocks, 2 * each, rows), BF16),
         scratch_shapes=[
-            pltpu.VMEM((parts, 2, rows, cb), BF16),
-            pltpu.VMEM((parts, rows, cb), F32),
-            pltpu.VMEM((parts, pb, 2 * each, rows), BF16),
-            pltpu.SemaphoreType.DMA((parts, 2)),
-            pltpu.SemaphoreType.DMA((parts,)),
+            pltpu.VMEM((fine, 2, rows, channels // fine), BF16),
+            pltpu.VMEM((fine, rows, channels // fine), F32),
+            pltpu.VMEM((fine, blocks // fine, 2 * each, rows), BF16),
+            pltpu.SemaphoreType.DMA((fine, 2)),
+            pltpu.SemaphoreType.DMA((fine,)),
         ],
         compiler_params=params(),
         name="prep",
@@ -461,18 +467,17 @@
     span = cb // (2 * each)
     query, gg, skip_source, skip_grad, gm_own, gm_give = pl.pallas_call(
         grad_kernel,
-        grid_spec=pltpu.PrefetchScalarGridSpec(
-            num_scalar_prefetch=1,
+        grid_spec=pl.GridSpec(
             grid=(parts,),
             in_specs=[
-                pl.BlockSpec((cb, width), lambda i, c: (i, 0)),
+                pl.BlockSpec((cb, width), lambda i: (i, 0)),
                 full((rows, half)),
                 full((rows, half)),
-                pl.BlockSpec((3, rows, cb), lambda i, c: (0, 0, i)),
-                pl.BlockSpec((1, cb), lambda i, c: (0, i)),
+                pl.BlockSpec((3, rows, cb), lambda i: (0, 0, i)),
+                pl.BlockSpec((1, cb), lambda i: (0, i)),
             ],
-            out_specs=[pl.BlockSpec((cb, rows), lambda i, c: (i, 0))] * 3
-            + [pl.BlockSpec((rows, cb), lambda i, c: (0, i))]
+            out_specs=[pl.BlockSpec((cb, rows), lambda i: (i, 0))] * 3
+            + [pl.BlockSpec((rows, cb), lambda i: (0, i))]
             + [hbm] * 2,
             scratch_shapes=[
                 pltpu.VMEM((parts, 2, span, each, rows), BF16),
@@ -486,22 +491,22 @@
         compiler_params=params(),
         cost_estimate=COSTLY,
         name="grad",
-    )(place, out_weight, in_hbm(cotangent), in_hbm(other), proj, skip)
+    )(out_weight, in_hbm(cotangent), in_hbm(other), proj, skip)
     gm = [in_hbm(gm_own), partner(gm_give)]
 
-    spectra, mid = conv_call(place, arrived, gm, tabs_conv, each)
+    spectra, mid = conv_call(arrived, gm, tabs_conv, each)
     back = lax.all_to_all(mid, "seq", 0, 0, tiled=True, axis_index_groups=chips)
-    pair, conv_give = corr_call(place, back, spectra, tabs_corr, each)
+    pair, conv_give = corr_call(back, spectra, tabs_corr, each)
     conv_got = partner(conv_give)
     last = exchange(pair)
 
     pieces = 4
     wb = half // pieces
-    weights = pltpu.VMEM((pieces, channels, wb), BF16)
+    weights = pltpu.VMEM((pieces, channels // pieces, half), BF16)
     sems = pltpu.SemaphoreType.DMA((pieces,))
     send, gated, mixing = pl.pallas_call(
         mix_kernel,
-        in_specs=[smem] + [vmem] * 4 + [hbm],
+        in_specs=[vmem] * 4 + [hbm],
         out_specs=[hbm, vmem, vmem],
         out_shape=[
             pltpu.HBM((rows, half), BF16),
@@ -518,11 +523,11 @@
         compiler_params=params(),
         cost_estimate=COSTLY,
         name="mix",
-    )(place, back, conv_got, skip_source, query, out_weight)
+    )(back, conv_got, skip_source, query, out_weight)
     received = lax.ppermute(send, "chan", [(0, 1), (1, 0)])
     kept, stacked = pl.pallas_call(
         own_kernel,
-        in_specs=[smem, vmem, vmem, vmem, hbm],
+        in_specs=[vmem, vmem, vmem, hbm],
         out_specs=[vmem, hbm],
         out_shape=[shape((rows, half), F32), pltpu.HBM((3, rows, channels), BF16)],
         scratch_shapes=[
@@ -533,7 +538,7 @@
         ],
         compiler_params=params(),
         name="own",
-    )(place, mixing, in_hbm(gg), gated, out_weight)
+    )(mixing, in_hbm(gg), gated, out_weight)
     mixed = (kept + received.astype(F32)).astype(BF16)
 
     grad_projected, grad_filter = pl.pallas_call(
@@ -542,9 +547,9 @@
         out_specs=[hbm] * 2,
         out_shape=[shape((3, rows, channels), BF16), shape((rows, channels), F32)],
         scratch_shapes=[
-            pltpu.VMEM((parts, 2, rows, cb), BF16),
-            pltpu.VMEM((parts, rows, cb), F32),
-            pltpu.SemaphoreType.DMA((2 * parts,)),
+            pltpu.VMEM((fine, 2, rows, channels // fine), BF16),
+            pltpu.VMEM((fine, rows, channels // fine), F32),
+            pltpu.SemaphoreType.DMA((2 * fine,)),
         ],
         input_output_aliases={3: 0},
         compiler_params=params(),

time: 104 us -> 102 us (0.981)
  Pallas kernels: 25.6 us -> 22.8 us
  waiting for transfers between devices: 24.5 us -> 25.7 us
    pallas_call x5, Pallas kernels: 22 us -> 19.5 us  [the longest x1 6.97 us: local(): pl.pallas_call(grad_kernel, grid_spec=pl.GridSpec(grid=(parts,), in_specs...]
  transfers between devices with their start and end apart: 6 -> 6, of which waited for: 4 -> 4; matrix products, arithmetic and copies ran while one was open for 1% -> 1% of each run, Pallas kernels for 17% -> 16%
where the time goes in v4:
time: 102 us
  starting transfers between devices  27.1 us (27%)
  waiting for transfers between devices  25.7 us (25%)
  Pallas kernels  22.8 us (22%)
  blocking collectives  22 us (22%)
  local copies, waits for them, and re-layouts  2.32 us (2%)
    all_to_all x2, starting transfers between devices, exchange(): return lax.all_to_all(x, 'seq', 0, 0, tiled=True)  22 us
    all_to_all x1, blocking collectives, local(): back = lax.all_to_all(mid, 'seq', 0, 0, tiled=True, axis_index_groups=chips)  22 us
    ppermute x1, waiting for transfers between devices, local(): received = lax.ppermute(send, 'chan', [(0, 1), (1, 0)])  12.8 us
    all_to_all x2, waiting for transfers between devices, exchange(): return lax.all_to_all(x, 'seq', 0, 0, tiled=True)  11.7 us
    pallas_call x1, Pallas kernels, local(): pl.pallas_call(grad_kernel, grid_spec=pl.GridSpec(grid=(parts,), in_specs...  6.97 us
    pallas_call x1, Pallas kernels, local(): pl.pallas_call(own_kernel, in_specs=[vmem, vmem, vmem, hbm], out_specs=[v...  3.78 us
    pallas_call x1, Pallas kernels, local(): pl.pallas_call(mix_kernel, in_specs=[vmem] * 4 + [hbm], out_specs=[hbm, v...  3.39 us
    pallas_call x1, Pallas kernels, corr_call(): pl.pallas_call(corr_kernel, in_specs=[VMEM] * (2 + len(tabs)), out_specs=...  3.3 us
  transfers between devices with their start and end apart: 6, of which 4 were waited for; matrix products, arithmetic and copies ran while one was open for 1% of the time, Pallas kernels for 16%

profile of v4, /device:TPU:1, one launch (start us, length us, event | category | flops | bytes accessed | tf_op | source)
XLA Modules:
  0.0 101.7 jit_solution(1221166500200467513)
XLA Ops:
  0.6 2.1 %collective-permute-start = (bf16[128,2048]{1,0:T(8,128)(2,1)}, bf16[128,2048]{1,0:T(8,128)(2,1)S(1)}, u32[]{:S(2)}, u32[]{:S(2)}) collective-permute-start(bf16[128,2048]{1,0:T(8,128)(2,1)} %own_ref.1), channel_id=1, source_target_pairs={{0,1},{1,0},{2,3},{3,2},{4,5},{5,4},{6,7},{7,6},{8,9},{9,8},{10,11... | collective-permute-start | bytes 1572872 | tf_op jit(solution)/shard_map/ppermute | solution.py:440
  2.8 2.1 %prep.1 = bf16[128,16,128]{2,1,0:T(8,128)(2,1)} custom-call(bf16[3,128,1024]{2,1,0:T(8,128)(2,1)} %bitcast.3, f32[128,1024]{1,0:T(8,128)} %filter_hbm.1), custom_call_target="tpu_custom_call" | custom-call | tf_op jit(solution)/shard_map/prep/pallas_call | solution.py:450
  4.9 15.6 %all-to-all-start = ((bf16[128,16,128]{2,1,0:T(8,128)(2,1)}), bf16[128,16,128]{2,1,0:T(8,128)(2,1)S(1)}, u32[]{:S(2)}, u32[]{:S(2)}) async-start(bf16[128,16,128]{2,1,0:T(8,128)(2,1)} %prep.1), calls=%async_computation | async-start | bytes 1048576 | tf_op jit(solution)/shard_map/all_to_all | solution.py:443
  20.5 0.0 collective-permute-done.other_ref
  20.5 0.0 copy-start.11
  20.5 0.8 copy-done.11
  21.3 0.7 copy-done.8
  22.0 0.0 copy-start.6
  22.0 0.0 copy-start.7
  22.0 0.0 copy-start.9
  22.0 0.0 copy-start.10
  22.0 7.0 %grad.1 = (bf16[1024,128]{1,0:T(8,128)(2,1)S(1)}, f32[1024,128]{1,0:T(8,128)S(1)}, f32[1024,128]{1,0:T(8,128)S(1)}, f32[128,1024]{1,0:T(8,128)S(1)}, bf16[64,8,1...) custom-call(bf16[1024,4096]{1,0:T(8,128)(2,1)} %w_hbm.1, bf16[128,2048]{1,0:T(8,128)(2,1)} %own_ref.1, ...), custom_call_target="tpu_custom_call" | custom-call | flops 99999997952 | bytes 1000000000 | tf_op jit(solution)/shard_map/grad/pallas_call | solution.py:468
  29.0 0.8 copy-done.1
  29.8 0.9 collective-permute-start.1
  30.7 1.2 %collective-permute-done.1.refs_2_ = bf16[64,8,128]{2,1,0:T(8,128)(2,1)S(1)} collective-permute-done((bf16[64,8,128]{2,1,0:T(8,128)(2,1)}, bf16[64,8,128]{2,1,0:T(8,128)(2,1)S(1)}, u32[]{:S(2)}, u32[]{:S(2)}) %collective-permute-start.1) | collective-permute-done | bytes 131104 | tf_op jit(solution)/shard_map/ppermute | solution.py:430
  31.9 10.6 %all-to-all-done.refs_0_ = bf16[128,16,128]{2,1,0:T(8,128)(2,1)S(1)} async-done(((bf16[128,16,128]{2,1,0:T(8,128)(2,1)}), bf16[128,16,128]{2,1,0:T(8,128)(2,1)S(1)}, u32[]{:S(2)}, u32[]{:S(2)}) %all-to-all-start) | async-done | bytes 524320 | tf_op jit(solution)/shard_map/all_to_all | solution.py:443
  42.5 0.0 copy-done.5
  42.5 0.0 copy-done.6
  42.6 2.1 %conv.1 = (f32[2,1024,256]{2,1,0:T(8,128)S(1)}, bf16[64,32,128]{2,1,0:T(8,128)(2,1)S(1)}) custom-call(bf16[128,16,128]{2,1,0:T(8,128)(2,1)S(1)} %all-to-all-done.refs_0_, bf16[64,8,128]{2,1,0:T(8,128)(2,1)} %get-tuple-element.20.refs_1_, bf16[64,8,128]{2,1,0:T(8,128)(2,1)S(1)} %collective-permute-done.1.refs_2_, bf16[256,256]{1,0:T(8,128)(2,1)S(1)} %copy-done.5, ...), custom_call_target="tpu_custom_call" | custom-call | tf_op jit(solution)/shard_map/conv/pallas_call | solution.py:373
  44.7 22.0 %all_to_all.15.refs_0_.in_ref = bf16[64,32,128]{2,1,0:T(8,128)(2,1)S(1)} all-to-all(bf16[64,32,128]{2,1,0:T(8,128)(2,1)S(1)} %get-tuple-element.22), channel_id=1, replica_groups={{0,4,8,12,16,20,24,28,32,36,40,44,48,52,56,60,64,68,72,76,80,84,88,92,9..., dimensions={0} | all-to-all | bytes 1048576 | tf_op jit(solution)/shard_map/all_to_all | solution.py:498
  66.7 3.3 %corr.1 = (bf16[128,16,128]{2,1,0:T(8,128)(2,1)}, bf16[64,8,128]{2,1,0:T(8,128)(2,1)}) custom-call(bf16[64,32,128]{2,1,0:T(8,128)(2,1)S(1)} %all_to_all.15.refs_0_.in_ref, f32[2,1024,256]{2,1,0:T(8,128)S(1)} %get-tuple-element.23.refs_1_, bf16[2,256,256]{2,1,0:T(8,128)(2,1)S(1)} %copy-done.9, bf16[256,256]{1,0:T(8,128)(2,1)S(1)} %copy-done.10, ...), custom_call_target="tpu_custom_call" | custom-call | flops 99999997952 | bytes 1000000000 | tf_op jit(solution)/shard_map/corr/pallas_call | solution.py:398
  70.0 2.0 %collective-permute-start.2 = (bf16[64,8,128]{2,1,0:T(8,128)(2,1)}, bf16[64,8,128]{2,1,0:T(8,128)(2,1)S(1)}, u32[]{:S(2)}, u32[]{:S(2)}) collective-permute-start(bf16[64,8,128]{2,1,0:T(8,128)(2,1)} %get-tuple-element.24), channel_id=1, source_target_pairs={{0,2},{2,0},{4,6},{6,4},{8,10},{10,8},{12,14},{14,12},{16,18},{18,... | collective-permute-start | bytes 393224 | tf_op jit(solution)/shard_map/ppermute | solution.py:430
  72.0 6.4 %all-to-all-start.2 = ((bf16[128,16,128]{2,1,0:T(8,128)(2,1)}), bf16[128,16,128]{2,1,0:T(8,128)(2,1)S(1)}, u32[]{:S(2)}, u32[]{:S(2)}) async-start(bf16[128,16,128]{2,1,0:T(8,128)(2,1)} %get-tuple-element.32), calls=%async_computation.2 | async-start | bytes 1048576 | tf_op jit(solution)/shard_map/all_to_all | solution.py:443
  78.4 0.0 collective-permute-done.2.refs_0_
  78.4 3.4 %mix.1 = (bf16[128,2048]{1,0:T(8,128)(2,1)}, bf16[128,1024]{1,0:T(8,128)(2,1)S(1)}, f32[1024,128]{1,0:T(8,128)S(1)}) custom-call(bf16[64,32,128]{2,1,0:T(8,128)(2,1)S(1)} %all_to_all.15.refs_0_.in_ref, bf16[64,8,128]{2,1,0:T(8,128)(2,1)S(1)} %collective-permute-done.2.refs_0_, f32[1024,128]{1,0:T(8,128)S(1)} %get-tuple-element.25.refs_1_, ...), custom_call_target="tpu_custom_call" | custom-call | flops 99999997952 | bytes 1000000000 | tf_op jit(solution)/shard_map/mix/pallas_call | solution.py:507
  81.8 0.0 copy-start
  81.8 0.1 collective-permute-start.3
  81.9 3.8 %own.1 = (f32[128,2048]{1,0:T(8,128)S(1)}, bf16[3,128,1024]{2,1,0:T(8,128)(2,1)}) custom-call(f32[1024,128]{1,0:T(8,128)S(1)} %get-tuple-element.27.mixing_ref, f32[1024,128]{1,0:T(8,128)} %copy-done.1, bf16[128,1024]{1,0:T(8,128)(2,1)S(1)} %get-tuple-element.29.gated_ref, bf16[1024,4096]{1,0:T(8,128)(2,1)} %w_hbm.1), custom_call_target="tpu_custom_call" | custom-call | tf_op jit(solution)/shard_map/own/pallas_call | solution.py:528
  85.7 12.8 %collective-permute-done.3 = bf16[128,2048]{1,0:T(8,128)(2,1)S(1)} collective-permute-done((bf16[128,2048]{1,0:T(8,128)(2,1)}, bf16[128,2048]{1,0:T(8,128)(2,1)S(1)}, u32[]{:S(2)}, u32[]{:S(2)}) %collective-permute-start.3) | collective-permute-done | bytes 524320 | tf_op jit(solution)/shard_map/ppermute | solution.py:527
  98.5 0.9 add_convert_fusion
  99.4 1.0 all-to-all-done.2.in_ref
  100.5 1.1 %end.1 = (bf16[3,128,1024]{2,1,0:T(8,128)(2,1)}, f32[128,1024]{1,0:T(8,128)}) custom-call(bf16[128,16,128]{2,1,0:T(8,128)(2,1)S(1)} %all-to-all-done.2.in_ref, f32[128,1024]{1,0:T(8,128)S(1)} %get-tuple-element.33.sg_ref, bf16[3,128,1024]{2,1,0:T(8,128)(2,1)S(1)} %bitcast.5, ...), custom_call_target="tpu_custom_call", output_to_operand_aliasing={{0}: (3, {})} | custom-call | tf_op jit(solution)/shard_map/end/pallas_call | solution.py:544
  (13 shorter events, 0.0 us)
Async XLA Ops:
  0.6 19.8 %collective-permute-start = (bf16[128,2048]{1,0:T(8,128)(2,1)}, bf16[128,2048]{1,0:T(8,128)(2,1)S(1)}, u32[]{:S(2)}, u32[]{:S(2)}) collective-permute-start(bf16[128,2048]{1,0:T(8,128)(2,1)} %own_ref.1), channel_id=1, source_target_pairs={{0,1},{1,0},{2,3},{3,2},{4,5},{5,4},{6,7},{7,6},{8,9},{9,8},{10,11... | collective-permute-start | bytes 1572872 | tf_op jit(solution)/shard_map/ppermute | solution.py:440
  4.9 37.6 %all-to-all-start = ((bf16[128,16,128]{2,1,0:T(8,128)(2,1)}), bf16[128,16,128]{2,1,0:T(8,128)(2,1)S(1)}, u32[]{:S(2)}, u32[]{:S(2)}) async-start(bf16[128,16,128]{2,1,0:T(8,128)(2,1)} %prep.1), calls=%async_computation | async-start | bytes 1048576 | tf_op jit(solution)/shard_map/all_to_all | solution.py:443
  20.5 0.8 copy-start.11
  21.3 0.7 copy-start.8
  22.0 20.6 %copy-start.2 = (bf16[2,256,256]{2,1,0:T(8,128)(2,1)S(1)}, bf16[2,256,256]{2,1,0:T(8,128)(2,1)}, u32[]{:S(2)}) copy-start(bf16[2,256,256]{2,1,0:T(8,128)(2,1)} %constant.17.clone.refs_4_) | copy-start | bytes 786436
  22.0 20.6 %copy-start.3 = (bf16[256,256]{1,0:T(8,128)(2,1)S(1)}, bf16[256,256]{1,0:T(8,128)(2,1)}, u32[]{:S(2)}) copy-start(bf16[256,256]{1,0:T(8,128)(2,1)} %constant.21.clone.refs_8_.refs_7_) | copy-start | bytes 393220
  22.0 20.6 %copy-start.4 = (bf16[256,256]{1,0:T(8,128)(2,1)S(1)}, bf16[256,256]{1,0:T(8,128)(2,1)}, u32[]{:S(2)}) copy-start(bf16[256,256]{1,0:T(8,128)(2,1)} %constant.20.clone.refs_7_.refs_6_) | copy-start | bytes 393220
  22.0 20.6 %copy-start.5 = (bf16[256,256]{1,0:T(8,128)(2,1)S(1)}, bf16[256,256]{1,0:T(8,128)(2,1)}, u32[]{:S(2)}) copy-start(bf16[256,256]{1,0:T(8,128)(2,1)} %constant.16.clone.refs_3_) | copy-start | bytes 393220
  22.0 20.6 %copy-start.6 = (f32[128,128]{1,0:T(8,128)S(1)}, f32[128,128]{1,0:T(8,128)}, u32[]{:S(2)}) copy-start(f32[128,128]{1,0:T(8,128)} %constant.19.clone.refs_6_.refs_5_) | copy-start | bytes 196612
  22.0 20.6 %copy-start.7 = (f32[128,128]{1,0:T(8,128)S(1)}, f32[128,128]{1,0:T(8,128)}, u32[]{:S(2)}) copy-start(f32[128,128]{1,0:T(8,128)} %constant.18.clone.refs_5_.refs_4_) | copy-start | bytes 196612
  22.0 44.7 %copy-start.9 = (bf16[2,256,256]{2,1,0:T(8,128)(2,1)S(1)}, bf16[2,256,256]{2,1,0:T(8,128)(2,1)}, u32[]{:S(2)}) copy-start(bf16[2,256,256]{2,1,0:T(8,128)(2,1)} %constant.22.clone.refs_2_) | copy-start | bytes 786436
  22.0 44.6 %copy-start.10 = (bf16[256,256]{1,0:T(8,128)(2,1)S(1)}, bf16[256,256]{1,0:T(8,128)(2,1)}, u32[]{:S(2)}) copy-start(bf16[256,256]{1,0:T(8,128)(2,1)} %constant.23.clone.refs_3_) | copy-start | bytes 393220
  29.0 0.8 copy-start.1
  29.8 2.1 %collective-permute-start.1 = (bf16[64,8,128]{2,1,0:T(8,128)(2,1)}, bf16[64,8,128]{2,1,0:T(8,128)(2,1)S(1)}, u32[]{:S(2)}, u32[]{:S(2)}) collective-permute-start(bf16[64,8,128]{2,1,0:T(8,128)(2,1)} %get-tuple-element.21), channel_id=1, source_target_pairs={{0,2},{2,0},{4,6},{6,4},{8,10},{10,8},{12,14},{14,12},{16,18},{18,... | collective-permute-start | bytes 393224 | tf_op jit(solution)/shard_map/ppermute | solution.py:430
  70.0 8.4 %collective-permute-start.2 = (bf16[64,8,128]{2,1,0:T(8,128)(2,1)}, bf16[64,8,128]{2,1,0:T(8,128)(2,1)S(1)}, u32[]{:S(2)}, u32[]{:S(2)}) collective-permute-start(bf16[64,8,128]{2,1,0:T(8,128)(2,1)} %get-tuple-element.24), channel_id=1, source_target_pairs={{0,2},{2,0},{4,6},{6,4},{8,10},{10,8},{12,14},{14,12},{16,18},{18,... | collective-permute-start | bytes 393224 | tf_op jit(solution)/shard_map/ppermute | solution.py:430
  72.0 28.5 %all-to-all-start.2 = ((bf16[128,16,128]{2,1,0:T(8,128)(2,1)}), bf16[128,16,128]{2,1,0:T(8,128)(2,1)S(1)}, u32[]{:S(2)}, u32[]{:S(2)}) async-start(bf16[128,16,128]{2,1,0:T(8,128)(2,1)} %get-tuple-element.32), calls=%async_computation.2 | async-start | bytes 1048576 | tf_op jit(solution)/shard_map/all_to_all | solution.py:443
  81.8 18.6 %copy-start = (bf16[128,3,1024]{2,0,1:T(8,128)(2,1)S(1)}, bf16[128,3,1024]{2,0,1:T(8,128)(2,1)}, u32[]{:S(2)}) copy-start(bf16[128,3,1024]{2,0,1:T(8,128)(2,1)} %param.13) | copy-start | bytes 2359300
  81.8 16.7 %collective-permute-start.3 = (bf16[128,2048]{1,0:T(8,128)(2,1)}, bf16[128,2048]{1,0:T(8,128)(2,1)S(1)}, u32[]{:S(2)}, u32[]{:S(2)}) collective-permute-start(bf16[128,2048]{1,0:T(8,128)(2,1)} %get-tuple-element.31), channel_id=1, source_target_pairs={{0,1},{1,0},{2,3},{3,2},{4,5},{5,4},{6,7},{7,6},{8,9},{9,8},{10,11... | collective-permute-start | bytes 1572872 | tf_op jit(solution)/shard_map/ppermute | solution.py:527

commit v5 on v4

--- a/solution.py
+++ b/solution.py
@@ -32,11 +32,11 @@
     outer = np.concatenate([np.cos(angle), -np.sin(angle)], axis=0)
     outer_high, outer_low = halves(outer)
     outer_both = np.concatenate([outer_high, outer_low], axis=1)
-    back_both = np.concatenate(halves(outer.T), axis=0)
+    back = outer.T.astype(BF16)
     even = np.arange(blocks).reshape(blocks // 2, 2).T.reshape(-1)
     orders = [even, np.roll(even, blocks // 2)]
     outer_order = np.stack([np.concatenate([outer_high[:, o], outer_low[:, o]], 1) for o in orders])
-    back_order = np.stack([np.concatenate(halves(outer.T[o]), axis=0) for o in orders])
+    back_order = np.stack([outer.T[o].astype(BF16) for o in orders])
     turn = 2.0 * np.pi * k1 * np.arange(rows)[None, :] / length
     turn_re = np.cos(turn).astype(np.float32)
     turn_im = -np.sin(turn).astype(np.float32)
@@ -44,7 +44,7 @@
     cos, sin = np.cos(grid), np.sin(grid)
     inner = GAIN * np.block([[cos, -sin], [sin, cos]])
     shared = [turn_re, turn_im, inner.astype(BF16), inner.T.astype(BF16)]
-    return [outer_both, back_order, *shared], [outer_order, back_both, *shared]
+    return [outer_both, back_order, *shared], [outer_order, back, *shared]
 
 
 def dot(a, b):
@@ -82,7 +82,7 @@
 
 
 def inverse(high_ref, low_ref, part_ref, tabs, scale, blocks, rows, count, store):
-    _, back_both, turn_re, turn_im, _, inner = tabs
+    _, back, turn_re, turn_im, _, inner = tabs
     scale /= GAIN**3
     tre, tim = turn_re[...] * scale, turn_im[...] * scale
     part_ref[...] = transform(high_ref, low_ref, inner)
@@ -94,8 +94,7 @@
             cim = part_ref[at : at + blocks, rows:]
             both.append(jnp.concatenate([cre * tre + cim * tim, cim * tre - cre * tim], axis=0))
         high, low = split(jnp.concatenate(both, axis=1))
-        y = dot(back_both[...], high)
-        y = y[:blocks] + y[blocks:] + dot(back_both[:blocks, :], low)
+        y = dot(back[...], high) + dot(back[...], low)
         for j in range(2):
             store(2 * pair + j, y[:, j * rows : (j + 1) * rows])
 
@@ -243,9 +242,9 @@
 def corr_kernel(*refs):
     in_ref, spec_ref = refs[:2]
     tabs = refs[2:8]
-    out_ref, piece = refs[8:10]
-    wide_ref, high_ref, low_ref, part_ref, grad_ref, back_ref, sem = refs[10:]
-    blocks, two, rows = out_ref.shape
+    out_hbm, piece = refs[8:10]
+    wide_ref, high_ref, low_ref, part_ref, grad_ref, back_ref, out_ref, sem, out_sem = refs[10:]
+    blocks, two, rows = out_hbm.shape
     count = two // 2
     middle = blocks // 2
     copy = pltpu.make_async_copy(in_ref.at[:, 3 * count :, :], piece, sem)
@@ -260,6 +259,7 @@
     mine = (tabs[0].at[core()], *tabs[1:])
     forward(load, blocks, rows, count, mine, high_ref, low_ref, grad_ref)
     scale = 1.0 / (blocks * rows)
+    writes = []
     for s, factor in ((1, scale), (0, scale / math.sqrt(blocks * rows))):
 
         def store(c, y):
@@ -267,21 +267,31 @@
 
         product(spec_ref.at[s], grad_ref, True, high_ref, low_ref)
         inverse(high_ref, low_ref, part_ref, tabs, factor, blocks, rows, count, store)
-    for k in range(2):
-        out_ref[:, k * count : (k + 1) * count, :] = (
-            back_ref[k].reshape(blocks, count, rows).astype(BF16)
+        k = 1 - s
+        out_ref[k] = back_ref[k].reshape(blocks, count, rows).astype(BF16)
+        writes.append(
+            pltpu.make_async_copy(
+                out_ref.at[k], out_hbm.at[:, k * count : (k + 1) * count, :], out_sem.at[k]
+            )
         )
+        writes[-1].start()
+    for write in writes:
+        write.wait()
     copy.wait()
 
 
 def weight_copies(w_hbm, chan, buf_ref, sem_ref):
     parts, band, width = buf_ref.shape
     columns = pl.ds(pl.multiple_of(chan * width, width), width)
+    part = band // 2
     return [
         pltpu.make_async_copy(
-            w_hbm.at[i * band : (i + 1) * band, columns], buf_ref.at[i], sem_ref.at[i]
+            w_hbm.at[i * band + j * part : i * band + (j + 1) * part, columns],
+            buf_ref.at[i, j * part : (j + 1) * part],
+            sem_ref.at[i, j],
         )
         for i in range(parts)
+        for j in range(2)
     ]
 
 
@@ -289,8 +299,10 @@
     parts, band, width = buf_ref.shape
     total = 0.0
     for i in range(parts - 1):
-        copies[i].wait()
+        copies[2 * i].wait()
+        copies[2 * i + 1].wait()
         total = total + dot(gated_ref[:, i * band : (i + 1) * band], buf_ref[i])
+    copies[-2].wait()
     copies[-1].wait()
     step = width // 4
     for j in range(4):
@@ -398,8 +410,8 @@
     return pl.pallas_call(
         corr_kernel,
         in_specs=[VMEM] * (2 + len(tabs)),
-        out_specs=[VMEM, HBM],
-        out_shape=[jax.ShapeDtypeStruct((blocks, 2 * each, rows), BF16)]
+        out_specs=[HBM, HBM],
+        out_shape=[pltpu.HBM((blocks, 2 * each, rows), BF16)]
         + [pltpu.HBM((middle, each, rows), BF16)],
         scratch_shapes=[
             pltpu.VMEM((blocks * each, rows), F32),
@@ -408,7 +420,9 @@
             pltpu.VMEM(spec_shape, F32),
             pltpu.VMEM(spec_shape, F32),
             pltpu.VMEM((2, blocks * each, rows), F32),
+            pltpu.VMEM((2, blocks, each, rows), BF16),
             pltpu.SemaphoreType.DMA(()),
+            pltpu.SemaphoreType.DMA((2,)),
         ],
         compiler_params=params(),
         cost_estimate=COSTLY,
@@ -503,7 +517,7 @@
     pieces = 4
     wb = half // pieces
     weights = pltpu.VMEM((pieces, channels // pieces, half), BF16)
-    sems = pltpu.SemaphoreType.DMA((pieces,))
+    sems = pltpu.SemaphoreType.DMA((pieces, 2))
     send, gated, mixing = pl.pallas_call(
         mix_kernel,
         in_specs=[vmem] * 4 + [hbm],
@@ -518,7 +532,7 @@
             weights,
             pltpu.VMEM((pieces, rows, wb), BF16),
             sems,
-            sems,
+            pltpu.SemaphoreType.DMA((pieces,)),
         ],
         compiler_params=params(),
         cost_estimate=COSTLY,

time: 102 us -> 102 us (level)
  no operation moved by 1% of the time
where the time goes in v5:
time: 102 us; the launch traced here: 101 us
  starting transfers between devices  27.1 us (27%)
  waiting for transfers between devices  25.6 us (25%)
  Pallas kernels  22.4 us (22%)
  blocking collectives  22 us (22%)
  local copies, waits for them, and re-layouts  2.32 us (2%)
    all_to_all x2, starting transfers between devices, exchange(): return lax.all_to_all(x, 'seq', 0, 0, tiled=True)  22 us
    all_to_all x1, blocking collectives, local(): back = lax.all_to_all(mid, 'seq', 0, 0, tiled=True, axis_index_groups=chips)  22 us
    ppermute x1, waiting for transfers between devices, local(): received = lax.ppermute(send, 'chan', [(0, 1), (1, 0)])  12.8 us
    all_to_all x2, waiting for transfers between devices, exchange(): return lax.all_to_all(x, 'seq', 0, 0, tiled=True)  11.6 us
    pallas_call x1, Pallas kernels, local(): pl.pallas_call(grad_kernel, grid_spec=pl.GridSpec(grid=(parts,), in_specs...  7 us
    pallas_call x1, Pallas kernels, local(): pl.pallas_call(own_kernel, in_specs=[vmem, vmem, vmem, hbm], out_specs=[v...  3.78 us
    pallas_call x1, Pallas kernels, local(): pl.pallas_call(mix_kernel, in_specs=[vmem] * 4 + [hbm], out_specs=[hbm, v...  3.39 us
    pallas_call x1, Pallas kernels, corr_call(): pl.pallas_call(corr_kernel, in_specs=[VMEM] * (2 + len(tabs)), out_specs=...  2.92 us
  transfers between devices with their start and end apart: 6, of which 4 were waited for; matrix products, arithmetic and copies ran while one was open for 1% of the time, Pallas kernels for 16%

profile of v5, /device:TPU:1, one launch (start us, length us, event | category | flops | bytes accessed | tf_op | source)
XLA Modules:
  0.0 101.3 jit_solution(18354276304544419321)
XLA Ops:
  0.6 2.1 %collective-permute-start = (bf16[128,2048]{1,0:T(8,128)(2,1)}, bf16[128,2048]{1,0:T(8,128)(2,1)S(1)}, u32[]{:S(2)}, u32[]{:S(2)}) collective-permute-start(bf16[128,2048]{1,0:T(8,128)(2,1)} %own_ref.1), channel_id=1, source_target_pairs={{0,1},{1,0},{2,3},{3,2},{4,5},{5,4},{6,7},{7,6},{8,9},{9,8},{10,11... | collective-permute-start | bytes 1572872 | tf_op jit(solution)/shard_map/ppermute | solution.py:454
  2.8 2.1 %prep.1 = bf16[128,16,128]{2,1,0:T(8,128)(2,1)} custom-call(bf16[3,128,1024]{2,1,0:T(8,128)(2,1)} %bitcast.3, f32[128,1024]{1,0:T(8,128)} %filter_hbm.1), custom_call_target="tpu_custom_call" | custom-call | tf_op jit(solution)/shard_map/prep/pallas_call | solution.py:464
  4.9 15.6 %all-to-all-start = ((bf16[128,16,128]{2,1,0:T(8,128)(2,1)}), bf16[128,16,128]{2,1,0:T(8,128)(2,1)S(1)}, u32[]{:S(2)}, u32[]{:S(2)}) async-start(bf16[128,16,128]{2,1,0:T(8,128)(2,1)} %prep.1), calls=%async_computation | async-start | bytes 1048576 | tf_op jit(solution)/shard_map/all_to_all | solution.py:457
  20.5 0.0 collective-permute-done.other_ref
  20.5 0.0 copy-start.11
  20.5 0.8 copy-done.11
  21.3 0.7 copy-done.8
  22.0 0.0 copy-start.6
  22.0 0.0 copy-start.7
  22.0 0.0 copy-start.9
  22.0 0.0 copy-start.10
  22.0 7.0 %grad.1 = (bf16[1024,128]{1,0:T(8,128)(2,1)S(1)}, f32[1024,128]{1,0:T(8,128)S(1)}, f32[1024,128]{1,0:T(8,128)S(1)}, f32[128,1024]{1,0:T(8,128)S(1)}, bf16[64,8,1...) custom-call(bf16[1024,4096]{1,0:T(8,128)(2,1)} %w_hbm.1, bf16[128,2048]{1,0:T(8,128)(2,1)} %own_ref.1, ...), custom_call_target="tpu_custom_call" | custom-call | flops 99999997952 | bytes 1000000000 | tf_op jit(solution)/shard_map/grad/pallas_call | solution.py:482
  29.0 0.0 copy-start.1
  29.0 0.8 copy-done.1
  29.8 0.9 collective-permute-start.1
  30.7 1.2 %collective-permute-done.1.refs_2_ = bf16[64,8,128]{2,1,0:T(8,128)(2,1)S(1)} collective-permute-done((bf16[64,8,128]{2,1,0:T(8,128)(2,1)}, bf16[64,8,128]{2,1,0:T(8,128)(2,1)S(1)}, u32[]{:S(2)}, u32[]{:S(2)}) %collective-permute-start.1) | collective-permute-done | bytes 131104 | tf_op jit(solution)/shard_map/ppermute | solution.py:444
  31.9 10.6 %all-to-all-done.refs_0_ = bf16[128,16,128]{2,1,0:T(8,128)(2,1)S(1)} async-done(((bf16[128,16,128]{2,1,0:T(8,128)(2,1)}), bf16[128,16,128]{2,1,0:T(8,128)(2,1)S(1)}, u32[]{:S(2)}, u32[]{:S(2)}) %all-to-all-start) | async-done | bytes 524320 | tf_op jit(solution)/shard_map/all_to_all | solution.py:457
  42.6 2.0 %conv.1 = (f32[2,1024,256]{2,1,0:T(8,128)S(1)}, bf16[64,32,128]{2,1,0:T(8,128)(2,1)S(1)}) custom-call(bf16[128,16,128]{2,1,0:T(8,128)(2,1)S(1)} %all-to-all-done.refs_0_, bf16[64,8,128]{2,1,0:T(8,128)(2,1)} %get-tuple-element.20.refs_1_, bf16[64,8,128]{2,1,0:T(8,128)(2,1)S(1)} %collective-permute-done.1.refs_2_, bf16[256,256]{1,0:T(8,128)(2,1)S(1)} %copy-done.5, ...), custom_call_target="tpu_custom_call" | custom-call | tf_op jit(solution)/shard_map/conv/pallas_call | solution.py:385
  44.6 22.0 %all_to_all.15.refs_0_.in_ref = bf16[64,32,128]{2,1,0:T(8,128)(2,1)S(1)} all-to-all(bf16[64,32,128]{2,1,0:T(8,128)(2,1)S(1)} %get-tuple-element.22), channel_id=1, replica_groups={{0,4,8,12,16,20,24,28,32,36,40,44,48,52,56,60,64,68,72,76,80,84,88,92,9..., dimensions={0} | all-to-all | bytes 1048576 | tf_op jit(solution)/shard_map/all_to_all | solution.py:512
  66.6 2.9 %corr.1 = (bf16[128,16,128]{2,1,0:T(8,128)(2,1)}, bf16[64,8,128]{2,1,0:T(8,128)(2,1)}) custom-call(bf16[64,32,128]{2,1,0:T(8,128)(2,1)S(1)} %all_to_all.15.refs_0_.in_ref, f32[2,1024,256]{2,1,0:T(8,128)S(1)} %get-tuple-element.23.refs_1_, bf16[2,256,256]{2,1,0:T(8,128)(2,1)S(1)} %copy-done.9, bf16[128,256]{1,0:T(8,128)(2,1)S(1)} %copy-done.10, ...), custom_call_target="tpu_custom_call" | custom-call | flops 99999997952 | bytes 1000000000 | tf_op jit(solution)/shard_map/corr/pallas_call | solution.py:410
  69.5 2.0 %collective-permute-start.2 = (bf16[64,8,128]{2,1,0:T(8,128)(2,1)}, bf16[64,8,128]{2,1,0:T(8,128)(2,1)S(1)}, u32[]{:S(2)}, u32[]{:S(2)}) collective-permute-start(bf16[64,8,128]{2,1,0:T(8,128)(2,1)} %get-tuple-element.24), channel_id=1, source_target_pairs={{0,2},{2,0},{4,6},{6,4},{8,10},{10,8},{12,14},{14,12},{16,18},{18,... | collective-permute-start | bytes 393224 | tf_op jit(solution)/shard_map/ppermute | solution.py:444
  71.5 6.4 %all-to-all-start.2 = ((bf16[128,16,128]{2,1,0:T(8,128)(2,1)}), bf16[128,16,128]{2,1,0:T(8,128)(2,1)S(1)}, u32[]{:S(2)}, u32[]{:S(2)}) async-start(bf16[128,16,128]{2,1,0:T(8,128)(2,1)} %get-tuple-element.32), calls=%async_computation.2 | async-start | bytes 1048576 | tf_op jit(solution)/shard_map/all_to_all | solution.py:457
  78.0 0.0 collective-permute-done.2.refs_0_
  78.0 3.4 %mix.1 = (bf16[128,2048]{1,0:T(8,128)(2,1)}, bf16[128,1024]{1,0:T(8,128)(2,1)S(1)}, f32[1024,128]{1,0:T(8,128)S(1)}) custom-call(bf16[64,32,128]{2,1,0:T(8,128)(2,1)S(1)} %all_to_all.15.refs_0_.in_ref, bf16[64,8,128]{2,1,0:T(8,128)(2,1)S(1)} %collective-permute-done.2.refs_0_, f32[1024,128]{1,0:T(8,128)S(1)} %get-tuple-element.25.refs_1_, ...), custom_call_target="tpu_custom_call" | custom-call | flops 99999997952 | bytes 1000000000 | tf_op jit(solution)/shard_map/mix/pallas_call | solution.py:521
  81.4 0.0 copy-start
  81.4 0.1 collective-permute-start.3
  81.5 3.8 %own.1 = (f32[128,2048]{1,0:T(8,128)S(1)}, bf16[3,128,1024]{2,1,0:T(8,128)(2,1)}) custom-call(f32[1024,128]{1,0:T(8,128)S(1)} %get-tuple-element.27.mixing_ref, f32[1024,128]{1,0:T(8,128)} %copy-done.1, bf16[128,1024]{1,0:T(8,128)(2,1)S(1)} %get-tuple-element.29.gated_ref, bf16[1024,4096]{1,0:T(8,128)(2,1)} %w_hbm.1), custom_call_target="tpu_custom_call" | custom-call | tf_op jit(solution)/shard_map/own/pallas_call | solution.py:542
  85.3 12.8 %collective-permute-done.3 = bf16[128,2048]{1,0:T(8,128)(2,1)S(1)} collective-permute-done((bf16[128,2048]{1,0:T(8,128)(2,1)}, bf16[128,2048]{1,0:T(8,128)(2,1)S(1)}, u32[]{:S(2)}, u32[]{:S(2)}) %collective-permute-start.3) | collective-permute-done | bytes 524320 | tf_op jit(solution)/shard_map/ppermute | solution.py:541
  98.1 0.9 add_convert_fusion
  99.0 1.0 %all-to-all-done.2.in_ref = bf16[128,16,128]{2,1,0:T(8,128)(2,1)S(1)} async-done(((bf16[128,16,128]{2,1,0:T(8,128)(2,1)}), bf16[128,16,128]{2,1,0:T(8,128)(2,1)S(1)}, u32[]{:S(2)}, u32[]{:S(2)}) %all-to-all-start.2) | async-done | bytes 524320 | tf_op jit(solution)/shard_map/all_to_all | solution.py:457
  100.0 0.0 copy-done
  100.0 1.1 %end.1 = (bf16[3,128,1024]{2,1,0:T(8,128)(2,1)}, f32[128,1024]{1,0:T(8,128)}) custom-call(bf16[128,16,128]{2,1,0:T(8,128)(2,1)S(1)} %all-to-all-done.2.in_ref, f32[128,1024]{1,0:T(8,128)S(1)} %get-tuple-element.33.sg_ref, bf16[3,128,1024]{2,1,0:T(8,128)(2,1)S(1)} %bitcast.5, ...), custom_call_target="tpu_custom_call", output_to_operand_aliasing={{0}: (3, {})} | custom-call | tf_op jit(solution)/shard_map/end/pallas_call | solution.py:558
  (13 shorter events, 0.0 us)
Async XLA Ops:
  0.6 19.8 %collective-permute-start = (bf16[128,2048]{1,0:T(8,128)(2,1)}, bf16[128,2048]{1,0:T(8,128)(2,1)S(1)}, u32[]{:S(2)}, u32[]{:S(2)}) collective-permute-start(bf16[128,2048]{1,0:T(8,128)(2,1)} %own_ref.1), channel_id=1, source_target_pairs={{0,1},{1,0},{2,3},{3,2},{4,5},{5,4},{6,7},{7,6},{8,9},{9,8},{10,11... | collective-permute-start | bytes 1572872 | tf_op jit(solution)/shard_map/ppermute | solution.py:454
  4.9 37.6 %all-to-all-start = ((bf16[128,16,128]{2,1,0:T(8,128)(2,1)}), bf16[128,16,128]{2,1,0:T(8,128)(2,1)S(1)}, u32[]{:S(2)}, u32[]{:S(2)}) async-start(bf16[128,16,128]{2,1,0:T(8,128)(2,1)} %prep.1), calls=%async_computation | async-start | bytes 1048576 | tf_op jit(solution)/shard_map/all_to_all | solution.py:457
  20.5 0.8 copy-start.11
  21.3 0.7 copy-start.8
  22.0 20.6 %copy-start.2 = (bf16[256,256]{1,0:T(8,128)(2,1)S(1)}, bf16[256,256]{1,0:T(8,128)(2,1)}, u32[]{:S(2)}) copy-start(bf16[256,256]{1,0:T(8,128)(2,1)} %constant.21.clone.refs_8_.refs_7_) | copy-start | bytes 393220
  22.0 20.6 %copy-start.3 = (bf16[256,256]{1,0:T(8,128)(2,1)S(1)}, bf16[256,256]{1,0:T(8,128)(2,1)}, u32[]{:S(2)}) copy-start(bf16[256,256]{1,0:T(8,128)(2,1)} %constant.20.clone.refs_7_.refs_6_) | copy-start | bytes 393220
  22.0 20.6 %copy-start.4 = (bf16[2,128,256]{2,1,0:T(8,128)(2,1)S(1)}, bf16[2,128,256]{2,1,0:T(8,128)(2,1)}, u32[]{:S(2)}) copy-start(bf16[2,128,256]{2,1,0:T(8,128)(2,1)} %constant.17.clone.refs_4_) | copy-start | bytes 393220
  22.0 20.6 %copy-start.5 = (bf16[256,256]{1,0:T(8,128)(2,1)S(1)}, bf16[256,256]{1,0:T(8,128)(2,1)}, u32[]{:S(2)}) copy-start(bf16[256,256]{1,0:T(8,128)(2,1)} %constant.16.clone.refs_3_) | copy-start | bytes 393220
  22.0 20.6 %copy-start.6 = (f32[128,128]{1,0:T(8,128)S(1)}, f32[128,128]{1,0:T(8,128)}, u32[]{:S(2)}) copy-start(f32[128,128]{1,0:T(8,128)} %constant.19.clone.refs_6_.refs_5_) | copy-start | bytes 196612
  22.0 20.6 %copy-start.7 = (f32[128,128]{1,0:T(8,128)S(1)}, f32[128,128]{1,0:T(8,128)}, u32[]{:S(2)}) copy-start(f32[128,128]{1,0:T(8,128)} %constant.18.clone.refs_5_.refs_4_) | copy-start | bytes 196612
  22.0 44.6 %copy-start.9 = (bf16[2,256,256]{2,1,0:T(8,128)(2,1)S(1)}, bf16[2,256,256]{2,1,0:T(8,128)(2,1)}, u32[]{:S(2)}) copy-start(bf16[2,256,256]{2,1,0:T(8,128)(2,1)} %constant.22.clone.refs_2_) | copy-start | bytes 786436
  22.0 44.6 %copy-start.10 = (bf16[128,256]{1,0:T(8,128)(2,1)S(1)}, bf16[128,256]{1,0:T(8,128)(2,1)}, u32[]{:S(2)}) copy-start(bf16[128,256]{1,0:T(8,128)(2,1)} %constant.23.clone.refs_3_) | copy-start | bytes 196612
  29.0 0.8 copy-start.1
  29.8 2.1 %collective-permute-start.1 = (bf16[64,8,128]{2,1,0:T(8,128)(2,1)}, bf16[64,8,128]{2,1,0:T(8,128)(2,1)S(1)}, u32[]{:S(2)}, u32[]{:S(2)}) collective-permute-start(bf16[64,8,128]{2,1,0:T(8,128)(2,1)} %get-tuple-element.21), channel_id=1, source_target_pairs={{0,2},{2,0},{4,6},{6,4},{8,10},{10,8},{12,14},{14,12},{16,18},{18,... | collective-permute-start | bytes 393224 | tf_op jit(solution)/shard_map/ppermute | solution.py:444
  69.5 8.4 %collective-permute-start.2 = (bf16[64,8,128]{2,1,0:T(8,128)(2,1)}, bf16[64,8,128]{2,1,0:T(8,128)(2,1)S(1)}, u32[]{:S(2)}, u32[]{:S(2)}) collective-permute-start(bf16[64,8,128]{2,1,0:T(8,128)(2,1)} %get-tuple-element.24), channel_id=1, source_target_pairs={{0,2},{2,0},{4,6},{6,4},{8,10},{10,8},{12,14},{14,12},{16,18},{18,... | collective-permute-start | bytes 393224 | tf_op jit(solution)/shard_map/ppermute | solution.py:444
  71.5 28.5 %all-to-all-start.2 = ((bf16[128,16,128]{2,1,0:T(8,128)(2,1)}), bf16[128,16,128]{2,1,0:T(8,128)(2,1)S(1)}, u32[]{:S(2)}, u32[]{:S(2)}) async-start(bf16[128,16,128]{2,1,0:T(8,128)(2,1)} %get-tuple-element.32), calls=%async_computation.2 | async-start | bytes 1048576 | tf_op jit(solution)/shard_map/all_to_all | solution.py:457
  81.4 18.6 %copy-start = (bf16[128,3,1024]{2,0,1:T(8,128)(2,1)S(1)}, bf16[128,3,1024]{2,0,1:T(8,128)(2,1)}, u32[]{:S(2)}) copy-start(bf16[128,3,1024]{2,0,1:T(8,128)(2,1)} %param.13) | copy-start | bytes 2359300
  81.4 16.7 %collective-permute-start.3 = (bf16[128,2048]{1,0:T(8,128)(2,1)}, bf16[128,2048]{1,0:T(8,128)(2,1)S(1)}, u32[]{:S(2)}, u32[]{:S(2)}) collective-permute-start(bf16[128,2048]{1,0:T(8,128)(2,1)} %get-tuple-element.31), channel_id=1, source_target_pairs={{0,1},{1,0},{2,3},{3,2},{4,5},{5,4},{6,7},{7,6},{8,9},{9,8},{10,11... | collective-permute-start | bytes 1572872 | tf_op jit(solution)/shard_map/ppermute | solution.py:541

commit v6 on v5

--- a/solution.py
+++ b/solution.py
@@ -30,12 +30,10 @@
     k1 = np.arange(blocks)[:, None] + 0.5
     angle = 2.0 * np.pi * k1 * np.arange(blocks)[None, :] / (2 * blocks)
     outer = np.concatenate([np.cos(angle), -np.sin(angle)], axis=0)
-    outer_high, outer_low = halves(outer)
-    outer_both = np.concatenate([outer_high, outer_low], axis=1)
     back = outer.T.astype(BF16)
     even = np.arange(blocks).reshape(blocks // 2, 2).T.reshape(-1)
     orders = [even, np.roll(even, blocks // 2)]
-    outer_order = np.stack([np.concatenate([outer_high[:, o], outer_low[:, o]], 1) for o in orders])
+    outer_order = np.stack([outer[:, o].astype(BF16) for o in orders])
     back_order = np.stack([outer.T[o].astype(BF16) for o in orders])
     turn = 2.0 * np.pi * k1 * np.arange(rows)[None, :] / length
     turn_re = np.cos(turn).astype(np.float32)
@@ -44,7 +42,7 @@
     cos, sin = np.cos(grid), np.sin(grid)
     inner = GAIN * np.block([[cos, -sin], [sin, cos]])
     shared = [turn_re, turn_im, inner.astype(BF16), inner.T.astype(BF16)]
-    return [outer_both, back_order, *shared], [outer_order, back, *shared]
+    return [outer.astype(BF16), back_order, *shared], [outer_order, back, *shared]
 
 
 def dot(a, b):
@@ -69,7 +67,7 @@
     tre, tim = turn_re[...], turn_im[...]
     for pair in range(count // 2):
         x = jnp.concatenate([load(2 * pair + j).astype(BF16) for j in range(2)], axis=1)
-        a = dot(outer[...], jnp.concatenate([x, x], axis=0))
+        a = dot(outer[...], x)
         for j in range(2):
             are = a[:blocks, j * rows : (j + 1) * rows]
             aim = a[blocks:, j * rows : (j + 1) * rows]

time: 102 us -> 102 us (level)
  no operation moved by 1% of the time
where the time goes in v6:
time: 102 us; the launch traced here: 101 us
  starting transfers between devices  27.1 us (27%)
  waiting for transfers between devices  25.6 us (25%)
  Pallas kernels  22.3 us (22%)
  blocking collectives  22 us (22%)
  local copies, waits for them, and re-layouts  2.32 us (2%)
    all_to_all x2, starting transfers between devices, exchange(): return lax.all_to_all(x, 'seq', 0, 0, tiled=True)  22 us
    all_to_all x1, blocking collectives, local(): back = lax.all_to_all(mid, 'seq', 0, 0, tiled=True, axis_index_groups=chips)  22 us
    ppermute x1, waiting for transfers between devices, local(): received = lax.ppermute(send, 'chan', [(0, 1), (1, 0)])  12.8 us
    all_to_all x2, waiting for transfers between devices, exchange(): return lax.all_to_all(x, 'seq', 0, 0, tiled=True)  11.6 us
    pallas_call x1, Pallas kernels, local(): pl.pallas_call(grad_kernel, grid_spec=pl.GridSpec(grid=(parts,), in_specs...  7 us
    pallas_call x1, Pallas kernels, local(): pl.pallas_call(own_kernel, in_specs=[vmem, vmem, vmem, hbm], out_specs=[v...  3.78 us
    pallas_call x1, Pallas kernels, local(): pl.pallas_call(mix_kernel, in_specs=[vmem] * 4 + [hbm], out_specs=[hbm, v...  3.39 us
    pallas_call x1, Pallas kernels, corr_call(): pl.pallas_call(corr_kernel, in_specs=[VMEM] * (2 + len(tabs)), out_specs=...  2.9 us
  transfers between devices with their start and end apart: 6, of which 4 were waited for; matrix products, arithmetic and copies ran while one was open for 1% of the time, Pallas kernels for 16%

profile of v6, /device:TPU:1, one launch (start us, length us, event | category | flops | bytes accessed | tf_op | source)
XLA Modules:
  0.0 101.2 jit_solution(17319717508939273224)
XLA Ops:
  0.6 2.1 %collective-permute-start = (bf16[128,2048]{1,0:T(8,128)(2,1)}, bf16[128,2048]{1,0:T(8,128)(2,1)S(1)}, u32[]{:S(2)}, u32[]{:S(2)}) collective-permute-start(bf16[128,2048]{1,0:T(8,128)(2,1)} %own_ref.1), channel_id=1, source_target_pairs={{0,1},{1,0},{2,3},{3,2},{4,5},{5,4},{6,7},{7,6},{8,9},{9,8},{10,11... | collective-permute-start | bytes 1572872 | tf_op jit(solution)/shard_map/ppermute | solution.py:452
  2.8 2.1 %prep.1 = bf16[128,16,128]{2,1,0:T(8,128)(2,1)} custom-call(bf16[3,128,1024]{2,1,0:T(8,128)(2,1)} %bitcast.3, f32[128,1024]{1,0:T(8,128)} %filter_hbm.1), custom_call_target="tpu_custom_call" | custom-call | tf_op jit(solution)/shard_map/prep/pallas_call | solution.py:462
  4.9 15.6 %all-to-all-start = ((bf16[128,16,128]{2,1,0:T(8,128)(2,1)}), bf16[128,16,128]{2,1,0:T(8,128)(2,1)S(1)}, u32[]{:S(2)}, u32[]{:S(2)}) async-start(bf16[128,16,128]{2,1,0:T(8,128)(2,1)} %prep.1), calls=%async_computation | async-start | bytes 1048576 | tf_op jit(solution)/shard_map/all_to_all | solution.py:455
  20.5 0.0 collective-permute-done.other_ref
  20.5 0.0 copy-start.11
  20.5 0.8 copy-done.11
  21.3 0.7 copy-done.8
  22.0 0.0 copy-start.6
  22.0 0.0 copy-start.7
  22.0 0.0 copy-start.9
  22.0 0.0 copy-start.10
  22.0 7.0 %grad.1 = (bf16[1024,128]{1,0:T(8,128)(2,1)S(1)}, f32[1024,128]{1,0:T(8,128)S(1)}, f32[1024,128]{1,0:T(8,128)S(1)}, f32[128,1024]{1,0:T(8,128)S(1)}, bf16[64,8,1...) custom-call(bf16[1024,4096]{1,0:T(8,128)(2,1)} %w_hbm.1, bf16[128,2048]{1,0:T(8,128)(2,1)} %own_ref.1, ...), custom_call_target="tpu_custom_call" | custom-call | flops 99999997952 | bytes 1000000000 | tf_op jit(solution)/shard_map/grad/pallas_call | solution.py:480
  29.0 0.8 copy-done.1
  29.8 0.9 collective-permute-start.1
  30.7 1.2 %collective-permute-done.1.refs_2_ = bf16[64,8,128]{2,1,0:T(8,128)(2,1)S(1)} collective-permute-done((bf16[64,8,128]{2,1,0:T(8,128)(2,1)}, bf16[64,8,128]{2,1,0:T(8,128)(2,1)S(1)}, u32[]{:S(2)}, u32[]{:S(2)}) %collective-permute-start.1) | collective-permute-done | bytes 131104 | tf_op jit(solution)/shard_map/ppermute | solution.py:442
  31.9 10.6 %all-to-all-done.refs_0_ = bf16[128,16,128]{2,1,0:T(8,128)(2,1)S(1)} async-done(((bf16[128,16,128]{2,1,0:T(8,128)(2,1)}), bf16[128,16,128]{2,1,0:T(8,128)(2,1)S(1)}, u32[]{:S(2)}, u32[]{:S(2)}) %all-to-all-start) | async-done | bytes 524320 | tf_op jit(solution)/shard_map/all_to_all | solution.py:455
  42.5 0.0 copy-done.5
  42.5 0.0 copy-done.6
  42.6 2.0 %conv.1 = (f32[2,1024,256]{2,1,0:T(8,128)S(1)}, bf16[64,32,128]{2,1,0:T(8,128)(2,1)S(1)}) custom-call(bf16[128,16,128]{2,1,0:T(8,128)(2,1)S(1)} %all-to-all-done.refs_0_, bf16[64,8,128]{2,1,0:T(8,128)(2,1)} %get-tuple-element.20.refs_1_, bf16[64,8,128]{2,1,0:T(8,128)(2,1)S(1)} %collective-permute-done.1.refs_2_, bf16[256,128]{1,0:T(8,128)(2,1)S(1)} %copy-done.7, ...), custom_call_target="tpu_custom_call" | custom-call | tf_op jit(solution)/shard_map/conv/pallas_call | solution.py:383
  44.6 22.0 %all_to_all.15.refs_0_.in_ref = bf16[64,32,128]{2,1,0:T(8,128)(2,1)S(1)} all-to-all(bf16[64,32,128]{2,1,0:T(8,128)(2,1)S(1)} %get-tuple-element.22), channel_id=1, replica_groups={{0,4,8,12,16,20,24,28,32,36,40,44,48,52,56,60,64,68,72,76,80,84,88,92,9..., dimensions={0} | all-to-all | bytes 1048576 | tf_op jit(solution)/shard_map/all_to_all | solution.py:510
  66.6 2.9 %corr.1 = (bf16[128,16,128]{2,1,0:T(8,128)(2,1)}, bf16[64,8,128]{2,1,0:T(8,128)(2,1)}) custom-call(bf16[64,32,128]{2,1,0:T(8,128)(2,1)S(1)} %all_to_all.15.refs_0_.in_ref, f32[2,1024,256]{2,1,0:T(8,128)S(1)} %get-tuple-element.23.refs_1_, bf16[2,256,128]{2,1,0:T(8,128)(2,1)S(1)} %copy-done.9, bf16[128,256]{1,0:T(8,128)(2,1)S(1)} %copy-done.10, ...), custom_call_target="tpu_custom_call" | custom-call | flops 99999997952 | bytes 1000000000 | tf_op jit(solution)/shard_map/corr/pallas_call | solution.py:408
  69.5 2.0 %collective-permute-start.2 = (bf16[64,8,128]{2,1,0:T(8,128)(2,1)}, bf16[64,8,128]{2,1,0:T(8,128)(2,1)S(1)}, u32[]{:S(2)}, u32[]{:S(2)}) collective-permute-start(bf16[64,8,128]{2,1,0:T(8,128)(2,1)} %get-tuple-element.24), channel_id=1, source_target_pairs={{0,2},{2,0},{4,6},{6,4},{8,10},{10,8},{12,14},{14,12},{16,18},{18,... | collective-permute-start | bytes 393224 | tf_op jit(solution)/shard_map/ppermute | solution.py:442
  71.5 6.4 %all-to-all-start.2 = ((bf16[128,16,128]{2,1,0:T(8,128)(2,1)}), bf16[128,16,128]{2,1,0:T(8,128)(2,1)S(1)}, u32[]{:S(2)}, u32[]{:S(2)}) async-start(bf16[128,16,128]{2,1,0:T(8,128)(2,1)} %get-tuple-element.32), calls=%async_computation.2 | async-start | bytes 1048576 | tf_op jit(solution)/shard_map/all_to_all | solution.py:455
  77.9 0.0 collective-permute-done.2.refs_0_
  77.9 3.4 %mix.1 = (bf16[128,2048]{1,0:T(8,128)(2,1)}, bf16[128,1024]{1,0:T(8,128)(2,1)S(1)}, f32[1024,128]{1,0:T(8,128)S(1)}) custom-call(bf16[64,32,128]{2,1,0:T(8,128)(2,1)S(1)} %all_to_all.15.refs_0_.in_ref, bf16[64,8,128]{2,1,0:T(8,128)(2,1)S(1)} %collective-permute-done.2.refs_0_, f32[1024,128]{1,0:T(8,128)S(1)} %get-tuple-element.25.refs_1_, ...), custom_call_target="tpu_custom_call" | custom-call | flops 99999997952 | bytes 1000000000 | tf_op jit(solution)/shard_map/mix/pallas_call | solution.py:519
  81.3 0.0 copy-start
  81.3 0.1 collective-permute-start.3
  81.4 3.8 %own.1 = (f32[128,2048]{1,0:T(8,128)S(1)}, bf16[3,128,1024]{2,1,0:T(8,128)(2,1)}) custom-call(f32[1024,128]{1,0:T(8,128)S(1)} %get-tuple-element.27.mixing_ref, f32[1024,128]{1,0:T(8,128)} %copy-done.1, bf16[128,1024]{1,0:T(8,128)(2,1)S(1)} %get-tuple-element.29.gated_ref, bf16[1024,4096]{1,0:T(8,128)(2,1)} %w_hbm.1), custom_call_target="tpu_custom_call" | custom-call | tf_op jit(solution)/shard_map/own/pallas_call | solution.py:540
  85.2 12.8 %collective-permute-done.3 = bf16[128,2048]{1,0:T(8,128)(2,1)S(1)} collective-permute-done((bf16[128,2048]{1,0:T(8,128)(2,1)}, bf16[128,2048]{1,0:T(8,128)(2,1)S(1)}, u32[]{:S(2)}, u32[]{:S(2)}) %collective-permute-start.3) | collective-permute-done | bytes 524320 | tf_op jit(solution)/shard_map/ppermute | solution.py:539
  98.1 0.9 add_convert_fusion
  99.0 1.0 all-to-all-done.2.in_ref
  100.0 1.1 %end.1 = (bf16[3,128,1024]{2,1,0:T(8,128)(2,1)}, f32[128,1024]{1,0:T(8,128)}) custom-call(bf16[128,16,128]{2,1,0:T(8,128)(2,1)S(1)} %all-to-all-done.2.in_ref, f32[128,1024]{1,0:T(8,128)S(1)} %get-tuple-element.33.sg_ref, bf16[3,128,1024]{2,1,0:T(8,128)(2,1)S(1)} %bitcast.5, ...), custom_call_target="tpu_custom_call", output_to_operand_aliasing={{0}: (3, {})} | custom-call | tf_op jit(solution)/shard_map/end/pallas_call | solution.py:556
  (13 shorter events, 0.0 us)
Async XLA Ops:
  0.6 19.8 %collective-permute-start = (bf16[128,2048]{1,0:T(8,128)(2,1)}, bf16[128,2048]{1,0:T(8,128)(2,1)S(1)}, u32[]{:S(2)}, u32[]{:S(2)}) collective-permute-start(bf16[128,2048]{1,0:T(8,128)(2,1)} %own_ref.1), channel_id=1, source_target_pairs={{0,1},{1,0},{2,3},{3,2},{4,5},{5,4},{6,7},{7,6},{8,9},{9,8},{10,11... | collective-permute-start | bytes 1572872 | tf_op jit(solution)/shard_map/ppermute | solution.py:452
  4.9 37.6 %all-to-all-start = ((bf16[128,16,128]{2,1,0:T(8,128)(2,1)}), bf16[128,16,128]{2,1,0:T(8,128)(2,1)S(1)}, u32[]{:S(2)}, u32[]{:S(2)}) async-start(bf16[128,16,128]{2,1,0:T(8,128)(2,1)} %prep.1), calls=%async_computation | async-start | bytes 1048576 | tf_op jit(solution)/shard_map/all_to_all | solution.py:455
  20.5 0.8 copy-start.11
  21.3 0.7 copy-start.8
  22.0 20.6 %copy-start.2 = (bf16[256,256]{1,0:T(8,128)(2,1)S(1)}, bf16[256,256]{1,0:T(8,128)(2,1)}, u32[]{:S(2)}) copy-start(bf16[256,256]{1,0:T(8,128)(2,1)} %constant.21.clone.refs_8_.refs_7_) | copy-start | bytes 393220
  22.0 20.6 %copy-start.3 = (bf16[256,256]{1,0:T(8,128)(2,1)S(1)}, bf16[256,256]{1,0:T(8,128)(2,1)}, u32[]{:S(2)}) copy-start(bf16[256,256]{1,0:T(8,128)(2,1)} %constant.20.clone.refs_7_.refs_6_) | copy-start | bytes 393220
  22.0 20.6 %copy-start.4 = (bf16[2,128,256]{2,1,0:T(8,128)(2,1)S(1)}, bf16[2,128,256]{2,1,0:T(8,128)(2,1)}, u32[]{:S(2)}) copy-start(bf16[2,128,256]{2,1,0:T(8,128)(2,1)} %constant.17.clone.refs_4_) | copy-start | bytes 393220
  22.0 20.6 %copy-start.5 = (f32[128,128]{1,0:T(8,128)S(1)}, f32[128,128]{1,0:T(8,128)}, u32[]{:S(2)}) copy-start(f32[128,128]{1,0:T(8,128)} %constant.19.clone.refs_6_.refs_5_) | copy-start | bytes 196612
  22.0 20.6 %copy-start.6 = (f32[128,128]{1,0:T(8,128)S(1)}, f32[128,128]{1,0:T(8,128)}, u32[]{:S(2)}) copy-start(f32[128,128]{1,0:T(8,128)} %constant.18.clone.refs_5_.refs_4_) | copy-start | bytes 196612
  22.0 20.6 %copy-start.7 = (bf16[256,128]{1,0:T(8,128)(2,1)S(1)}, bf16[256,128]{1,0:T(8,128)(2,1)}, u32[]{:S(2)}) copy-start(bf16[256,128]{1,0:T(8,128)(2,1)} %constant.16.clone.refs_3_) | copy-start | bytes 196612
  22.0 44.6 %copy-start.9 = (bf16[2,256,128]{2,1,0:T(8,128)(2,1)S(1)}, bf16[2,256,128]{2,1,0:T(8,128)(2,1)}, u32[]{:S(2)}) copy-start(bf16[2,256,128]{2,1,0:T(8,128)(2,1)} %constant.22.clone.refs_2_) | copy-start | bytes 393220
  22.0 44.6 %copy-start.10 = (bf16[128,256]{1,0:T(8,128)(2,1)S(1)}, bf16[128,256]{1,0:T(8,128)(2,1)}, u32[]{:S(2)}) copy-start(bf16[128,256]{1,0:T(8,128)(2,1)} %constant.23.clone.refs_3_) | copy-start | bytes 196612
  29.0 0.8 copy-start.1
  29.8 2.1 %collective-permute-start.1 = (bf16[64,8,128]{2,1,0:T(8,128)(2,1)}, bf16[64,8,128]{2,1,0:T(8,128)(2,1)S(1)}, u32[]{:S(2)}, u32[]{:S(2)}) collective-permute-start(bf16[64,8,128]{2,1,0:T(8,128)(2,1)} %get-tuple-element.21), channel_id=1, source_target_pairs={{0,2},{2,0},{4,6},{6,4},{8,10},{10,8},{12,14},{14,12},{16,18},{18,... | collective-permute-start | bytes 393224 | tf_op jit(solution)/shard_map/ppermute | solution.py:442
  69.5 8.4 %collective-permute-start.2 = (bf16[64,8,128]{2,1,0:T(8,128)(2,1)}, bf16[64,8,128]{2,1,0:T(8,128)(2,1)S(1)}, u32[]{:S(2)}, u32[]{:S(2)}) collective-permute-start(bf16[64,8,128]{2,1,0:T(8,128)(2,1)} %get-tuple-element.24), channel_id=1, source_target_pairs={{0,2},{2,0},{4,6},{6,4},{8,10},{10,8},{12,14},{14,12},{16,18},{18,... | collective-permute-start | bytes 393224 | tf_op jit(solution)/shard_map/ppermute | solution.py:442
  71.5 28.5 %all-to-all-start.2 = ((bf16[128,16,128]{2,1,0:T(8,128)(2,1)}), bf16[128,16,128]{2,1,0:T(8,128)(2,1)S(1)}, u32[]{:S(2)}, u32[]{:S(2)}) async-start(bf16[128,16,128]{2,1,0:T(8,128)(2,1)} %get-tuple-element.32), calls=%async_computation.2 | async-start | bytes 1048576 | tf_op jit(solution)/shard_map/all_to_all | solution.py:455
  81.3 18.6 %copy-start = (bf16[128,3,1024]{2,0,1:T(8,128)(2,1)S(1)}, bf16[128,3,1024]{2,0,1:T(8,128)(2,1)}, u32[]{:S(2)}) copy-start(bf16[128,3,1024]{2,0,1:T(8,128)(2,1)} %param.13) | copy-start | bytes 2359300
  81.3 16.7 %collective-permute-start.3 = (bf16[128,2048]{1,0:T(8,128)(2,1)}, bf16[128,2048]{1,0:T(8,128)(2,1)S(1)}, u32[]{:S(2)}, u32[]{:S(2)}) collective-permute-start(bf16[128,2048]{1,0:T(8,128)(2,1)} %get-tuple-element.31), channel_id=1, source_target_pairs={{0,1},{1,0},{2,3},{3,2},{4,5},{5,4},{6,7},{7,6},{8,9},{9,8},{10,11... | collective-permute-start | bytes 1572872 | tf_op jit(solution)/shard_map/ppermute | solution.py:539
